TPU v7x, 256 devices: a whole 4x4x8 slice. The times are simulated.
256 devices in a mesh: space: 8 (over x, core), snap: 32 (over y, z).
Axes of the slice: x: 4, y: 4, z: 8, core: 2. Of those that a mesh axis runs over, the one named last changes fastest.
Arguments:
- velocity: bfloat16 [256, 3, 16, 32, 128], P('snap', None, 'space'), may hold values from -40 to 40
- block_id: int32 [16, 32, 128], P('space'), may hold values from 0 to 7
- metric: float32 [8, 3], replicated, may hold values from 0.5 to 2
- leaf_rot: float32 [32, 8, 16], P('snap'), may hold values from -2 to 2
- merge_rot: float32 [31, 32, 16], replicated, may hold values from -1 to 1
- merge_order: int32 [31], replicated, may hold values from 0 to 1
- ref_cell: int32 [16], replicated, may hold values from 0 to 196607
Outputs:
- modes: float32 [16, 3, 16, 4096], P(None, None, 'space', 'snap')
All inputs are finite; a program needn't handle non-finite values.
Results may differ from a plain program's by a relative error of at most 0.0003.
Values may be sent and summed in bfloat16 or wider, within the bound.
No kernel may reach another device: no remote copies, remote signals or barrier semaphores. Data moves between devices by JAX's collectives and lax.ppermute only.
A program may use at most 64 MiB of HBM per device.

v0:
```python
import jax
import jax.numpy as jnp
from jax import lax
from jax.sharding import PartitionSpec as P

HIGHEST = lax.Precision.HIGHEST


def padded(cells, sides, width):
    for axis, dim in sides:
        count = lax.axis_size(axis)
        ends = count - 1
        head = lax.slice_in_dim(cells, 0, width, axis=dim)
        tail = lax.slice_in_dim(cells, cells.shape[dim] - width, cells.shape[dim], axis=dim)
        cells = jnp.concatenate(
            [
                lax.ppermute(tail, axis, [(i, (i + 1) % count) for i in range(ends)]),
                cells,
                lax.ppermute(head, axis, [((i + 1) % count, i) for i in range(ends)]),
            ],
            axis=dim,
        )
    return cells


def from_partner(value, axis, apart):
    mask = 2**apart
    pairs = [(source, source ^ mask) for source in range(lax.axis_size(axis))]
    return lax.ppermute(value, axis, pairs)


def matmul(left, right):
    return jnp.dot(left, right, precision=HIGHEST, preferred_element_type=jnp.float32)


def along_x(field, spacing):
    return spacing[0] * (jnp.roll(field, -1, axis=2) - jnp.roll(field, 1, axis=2)) * 0.5


def along_z(field, spacing):
    return spacing[2] * (jnp.roll(field, -1, axis=3) - jnp.roll(field, 1, axis=3)) * 0.5


def ortho_factor(gram_total, rank):
    scale = (jnp.trace(gram_total) + 1e-06) / rank
    return 1.5 * jnp.eye(rank, dtype=jnp.float32) - 0.5 * gram_total / scale


def local(velocity, block_id, metric, leaf_rot, merge_rot, merge_order, ref_cell):
    snaps_here, _, rows_y, cells_x, cells_z = velocity.shape
    rank = leaf_rot.shape[2]
    blocks_count = metric.shape[0]
    onehot = (
        block_id[None] == jnp.arange(blocks_count, dtype=jnp.int32)[:, None, None, None]
    ).astype(jnp.float32)
    spacing = jnp.einsum("bxyz,bk->kxyz", onehot, metric, precision=HIGHEST)
    vel_uw = velocity[:, 0::2]
    extended = padded(vel_uw, (("space", 2),), 1).astype(jnp.float32)
    wall_diff = spacing[1] * (extended[:, :, 2:] - extended[:, :, :-2]) * 0.5
    vel_full = velocity.astype(jnp.float32)
    vel_u = vel_full[:, 0]
    vel_v = vel_full[:, 1]
    vel_w = vel_full[:, 2]
    omega_x = wall_diff[:, 1] - along_z(vel_v, spacing)
    omega_y = along_z(vel_u, spacing) - along_x(vel_w, spacing)
    omega_z = along_x(vel_v, spacing) - wall_diff[:, 0]
    omega = jnp.stack([omega_x, omega_y, omega_z], axis=1).reshape(snaps_here, -1)
    own_block = matmul(leaf_rot[0].T, omega)
    snap_count = lax.axis_size("snap")
    depth = snap_count.bit_length() - 1
    snap_index = lax.axis_index("snap")
    space_index = lax.axis_index("space")
    plane = cells_x * cells_z
    rows_total = rows_y * lax.axis_size("space")
    cells_all = 3 * rows_total * plane
    comp_of = ref_cell // (rows_total * plane)
    rest = ref_cell % (rows_total * plane)
    row_of = rest // plane - space_index * rows_y
    width = plane // snap_count
    inside = ((row_of >= 0) & (row_of < rows_y)).astype(jnp.float32)
    local_ref = jnp.clip(
        comp_of * rows_y * plane + row_of * plane + rest % plane, 0, 3 * rows_y * plane - 1
    )
    sign_value = None
    norm_sq = None
    for tree_level in range(depth):
        final_level = tree_level == depth - 1
        node_id = snap_count - (snap_count >> tree_level) + (snap_index >> tree_level + 1)
        rotation = lax.dynamic_index_in_dim(merge_rot, node_id, 0, keepdims=False)
        order_bit = lax.dynamic_index_in_dim(merge_order, node_id, 0, keepdims=False)
        position = snap_index >> tree_level & 1
        own_first = position == order_bit
        rot_top = rotation[:rank]
        rot_bottom = rotation[rank:]
        rot_own = jnp.where(own_first, rot_top, rot_bottom)
        rot_partner = jnp.where(own_first, rot_bottom, rot_top)
        partner = from_partner(own_block, "snap", tree_level)
        merged = matmul(rot_own.T, own_block) + matmul(rot_partner.T, partner)
        gram_total = lax.psum(matmul(merged, merged.T), "space")
        factor = ortho_factor(gram_total, rank)
        own_block = matmul(factor.T, merged)
        if final_level:
            picked = jnp.take_along_axis(own_block, local_ref[:, None], axis=1)[:, 0] * inside
            sign_value = lax.psum(picked, "space")
            norm_sq = jnp.sum(factor * matmul(gram_total, factor), axis=0)
    floor_value = 0.5 * jnp.sqrt(norm_sq / cells_all + 1e-06)
    sign = sign_value / jnp.maximum(jnp.abs(sign_value), floor_value)
    modes_full = (own_block * sign[:, None]).reshape(rank, 3, rows_y, plane)
    return lax.dynamic_slice_in_dim(modes_full, snap_index * width, width, 3)


def solution(mesh):
    placed = (
        P("snap", None, "space", None, None),
        P("space", None, None),
        P(),
        P("snap", None, None),
        P(),
        P(),
        P(),
    )
    return jax.shard_map(
        local, mesh=mesh, in_specs=placed, out_specs=P(None, None, "space", "snap"), check_vma=False
    )
```

profile of v0, /device:TPU:1, one launch (start us, length us, event | category | flops | bytes accessed | tf_op | source)
XLA Modules:
  0.0 422.1 jit_solution(16041817159791190780)
XLA Ops:
  0.0 1.0 slice.148
  1.0 0.7 fusion.143
  1.7 4.5 %collective-permute-start = (bf16[8,2,1,32,128]{4,3,2,1,0:T(8,128)(2,1)}, bf16[8,2,1,32,128]{4,3,2,1,0:T(8,128)(2,1)}, u32[]{:S(2)}, u32[]{:S(2)}) collective-permute-start(bf16[8,2,1,32,128]{4,3,2,1,0:T(8,128)(2,1)} %get-tuple-element.28), channel_id=1, source_target_pairs={{0,32},{32,64},{64,96},{96,128},{128,160},{160,192},{192,224},{1,3... | collective-permute-start | bytes 393224 | tf_op jit(solution)/shard_map/ppermute | solution.py:17
  6.2 2.5 collective-permute-start.1
  8.8 1.8 copy.43
  11.0 2.1 slice_bitcast_fusion.7
  13.1 2.6 fusion.141
  15.7 1.7 slice_bitcast_fusion
  17.7 0.9 copy.50
  18.6 0.9 copy.49
  19.5 0.9 copy.45
  20.4 0.9 copy.46
  21.3 2.3 copy.51
  23.5 2.3 copy.48
  25.8 2.3 copy.44
  28.0 2.3 copy.47
  30.3 1.6 copy.55
  31.9 1.6 copy.52
  33.5 1.6 copy.58
  35.0 1.6 copy.61
  36.6 2.3 copy.63
  38.9 1.1 copy.59
  41.0 1.3 fusion.10
  42.4 1.2 maximum_convert_fusion
  44.2 1.7 fusion.1
  45.9 1.6 collective-permute-start.2
  48.8 1.5 fusion.25
  50.3 32.4 %collective-permute-done.2 = f32[16,24576]{1,0:T(8,128)} collective-permute-done((f32[16,24576]{1,0:T(8,128)S(1)}, f32[16,24576]{1,0:T(8,128)}, u32[]{:S(2)}, u32[]{:S(2)}) %collective-permute-start.2) | collective-permute-done | bytes 1572896 | tf_op jit(solution)/shard_map/ppermute | solution.py:29
  82.7 2.9 convolution_add_fusion.4
  85.6 2.2 fusion.146
  87.9 12.3 %psum.42 = f32[16,16]{1,0:T(8,128)S(1)} all-reduce(f32[16,16]{1,0:T(8,128)S(1)} %fusion.146), channel_id=1, replica_groups=mesh['space'=8,'snap'=32] {'space'}, use_global_device_ids=true, to_apply=%region_0.1 | all-reduce | flops 256 | bytes 2048 | tf_op jit(solution)/shard_map/psum | solution.py:99
  100.1 0.7 select_reduce_fusion.4
  101.5 1.5 fusion.16
  103.0 2.5 collective-permute-start.3
  106.2 1.5 fusion.27
  107.7 65.3 %collective-permute-done.3 = f32[16,24576]{1,0:T(8,128)} collective-permute-done((f32[16,24576]{1,0:T(8,128)S(1)}, f32[16,24576]{1,0:T(8,128)}, u32[]{:S(2)}, u32[]{:S(2)}) %collective-permute-start.3) | collective-permute-done | bytes 1572896 | tf_op jit(solution)/shard_map/ppermute | solution.py:29
  173.1 2.9 convolution_add_fusion.3
  176.0 2.1 fusion.147
  178.1 13.8 %psum.43 = f32[16,16]{1,0:T(8,128)S(1)} all-reduce(f32[16,16]{1,0:T(8,128)S(1)} %fusion.147), channel_id=1, replica_groups=mesh['space'=8,'snap'=32] {'space'}, use_global_device_ids=true, to_apply=%region_2.3 | all-reduce | flops 256 | bytes 2048 | tf_op jit(solution)/shard_map/psum | solution.py:99
  193.3 1.5 fusion.17
  194.8 6.2 %collective-permute-start.4 = (f32[16,24576]{1,0:T(8,128)S(1)}, f32[16,24576]{1,0:T(8,128)}, u32[]{:S(2)}, u32[]{:S(2)}) collective-permute-start(f32[16,24576]{1,0:T(8,128)S(1)} %fusion.17), channel_id=1, source_target_pairs={{0,4},{1,5},{2,6},{3,7},{4,0},{5,1},{6,2},{7,3},{8,12},{9,13},{10,... | collective-permute-start | bytes 4718600 | tf_op jit(solution)/shard_map/ppermute | solution.py:29
  201.6 1.5 fusion.29
  203.1 65.8 %collective-permute-done.4 = f32[16,24576]{1,0:T(8,128)} collective-permute-done((f32[16,24576]{1,0:T(8,128)S(1)}, f32[16,24576]{1,0:T(8,128)}, u32[]{:S(2)}, u32[]{:S(2)}) %collective-permute-start.4) | collective-permute-done | bytes 1572896 | tf_op jit(solution)/shard_map/ppermute | solution.py:29
  268.9 2.9 convolution_add_fusion.2
  271.8 2.1 fusion.148
  273.9 13.5 %psum.44 = f32[16,16]{1,0:T(8,128)S(1)} all-reduce(f32[16,16]{1,0:T(8,128)S(1)} %fusion.148), channel_id=1, replica_groups=mesh['space'=8,'snap'=32] {'space'}, use_global_device_ids=true, to_apply=%region_4.5 | all-reduce | flops 256 | bytes 2048 | tf_op jit(solution)/shard_map/psum | solution.py:99
  288.9 1.5 fusion.18
  290.4 1.7 collective-permute-start.5
  292.7 1.5 fusion.31
  294.2 31.8 %collective-permute-done.5 = f32[16,24576]{1,0:T(8,128)} collective-permute-done((f32[16,24576]{1,0:T(8,128)S(1)}, f32[16,24576]{1,0:T(8,128)}, u32[]{:S(2)}, u32[]{:S(2)}) %collective-permute-start.5) | collective-permute-done | bytes 1572896 | tf_op jit(solution)/shard_map/ppermute | solution.py:29
  326.0 2.9 convolution_add_fusion.1
  329.0 2.2 fusion.149
  331.2 13.5 %psum.45 = f32[16,16]{1,0:T(8,128)S(1)} all-reduce(f32[16,16]{1,0:T(8,128)S(1)} %fusion.149), channel_id=1, replica_groups=mesh['space'=8,'snap'=32] {'space'}, use_global_device_ids=true, to_apply=%region_6.7 | all-reduce | flops 256 | bytes 2048 | tf_op jit(solution)/shard_map/psum | solution.py:99
  346.1 1.5 fusion.19
  347.6 3.0 collective-permute-start.6
  351.4 1.5 fusion.33
  352.9 31.7 %collective-permute-done.6 = f32[16,24576]{1,0:T(8,128)} collective-permute-done((f32[16,24576]{1,0:T(8,128)S(1)}, f32[16,24576]{1,0:T(8,128)}, u32[]{:S(2)}, u32[]{:S(2)}) %collective-permute-start.6) | collective-permute-done | bytes 1572896 | tf_op jit(solution)/shard_map/ppermute | solution.py:29
  384.6 2.9 convolution_add_fusion
  387.5 2.2 fusion.150
  389.7 13.8 %psum.46 = f32[16,16]{1,0:T(8,128)S(1)} all-reduce(f32[16,16]{1,0:T(8,128)S(1)} %fusion.150), channel_id=1, replica_groups=mesh['space'=8,'snap'=32] {'space'}, use_global_device_ids=true, to_apply=%region_8.9 | all-reduce | flops 256 | bytes 2048 | tf_op jit(solution)/shard_map/psum | solution.py:99
  404.8 1.5 fusion.73
  406.4 0.7 gather_fusion
  407.1 12.5 %psum.47 = f32[16]{0:T(128)S(1)} all-reduce(f32[16]{0:T(128)S(1)} %and_select_fusion.3), channel_id=1, replica_groups=mesh['space'=8,'snap'=32] {'space'}, use_global_device_ids=true, to_apply=%region_10.11 | all-reduce | flops 16 | bytes 128 | tf_op jit(solution)/shard_map/psum | solution.py:104
  419.8 1.3 reshape.310
  (58 shorter events, 6.8 us)
Async XLA Ops:
  0.0 44.2 %copy-start = (f32[1,8,16]{2,1,0:T(8,128)S(1)}, f32[1,8,16]{2,1,0:T(8,128)}, u32[]{:S(2)}) copy-start(f32[1,8,16]{2,1,0:T(8,128)} %param.10) | copy-start | bytes 1540
  1.7 40.6 %collective-permute-start = (bf16[8,2,1,32,128]{4,3,2,1,0:T(8,128)(2,1)}, bf16[8,2,1,32,128]{4,3,2,1,0:T(8,128)(2,1)}, u32[]{:S(2)}, u32[]{:S(2)}) collective-permute-start(bf16[8,2,1,32,128]{4,3,2,1,0:T(8,128)(2,1)} %get-tuple-element.28), channel_id=1, source_target_pairs={{0,32},{32,64},{64,96},{96,128},{128,160},{160,192},{192,224},{1,3... | collective-permute-start | bytes 393224 | tf_op jit(solution)/shard_map/ppermute | solution.py:17
  6.2 36.2 %collective-permute-start.1 = (bf16[8,2,1,32,128]{4,3,2,1,0:T(8,128)(2,1)}, bf16[8,2,1,32,128]{4,3,2,1,0:T(8,128)(2,1)}, u32[]{:S(2)}, u32[]{:S(2)}) collective-permute-start(bf16[8,2,1,32,128]{4,3,2,1,0:T(8,128)(2,1)} %get-tuple-element.29), channel_id=1, source_target_pairs={{32,0},{64,32},{96,64},{128,96},{160,128},{192,160},{224,192},{33,... | collective-permute-start | bytes 393224 | tf_op jit(solution)/shard_map/ppermute | solution.py:19
  15.7 1.7 copy-start.10
  15.7 1.7 copy-start.12
  40.0 0.9 copy-start.5
  40.0 1.0 copy-start.6
  42.3 1.4 copy-start.1
  42.3 1.4 copy-start.2
  42.3 1.4 copy-start.3
  42.3 1.4 copy-start.4
  42.4 1.4 copy-start.7
  42.4 1.4 copy-start.8
  44.1 3.4 copy-start.11
  44.1 4.7 %copy-start.9 = (f32[31,32,16]{1,2,0:T(8,128)S(1)}, f32[31,32,16]{1,2,0:T(8,128)}, u32[]{:S(2)}) copy-start(f32[31,32,16]{1,2,0:T(8,128)} %param.11) | copy-start | bytes 190468
  45.9 36.8 %collective-permute-start.2 = (f32[16,24576]{1,0:T(8,128)S(1)}, f32[16,24576]{1,0:T(8,128)}, u32[]{:S(2)}, u32[]{:S(2)}) collective-permute-start(f32[16,24576]{1,0:T(8,128)S(1)} %bitcast.119), channel_id=1, source_target_pairs={{0,1},{1,0},{2,3},{3,2},{4,5},{5,4},{6,7},{7,6},{8,9},{9,8},{10,11... | collective-permute-start | bytes 4718600 | tf_op jit(solution)/shard_map/ppermute | solution.py:29
  103.0 70.0 %collective-permute-start.3 = (f32[16,24576]{1,0:T(8,128)S(1)}, f32[16,24576]{1,0:T(8,128)}, u32[]{:S(2)}, u32[]{:S(2)}) collective-permute-start(f32[16,24576]{1,0:T(8,128)S(1)} %fusion.16), channel_id=1, source_target_pairs={{0,2},{1,3},{2,0},{3,1},{4,6},{5,7},{6,4},{7,5},{8,10},{9,11},{10,... | collective-permute-start | bytes 4718600 | tf_op jit(solution)/shard_map/ppermute | solution.py:29
  194.8 74.1 %collective-permute-start.4 = (f32[16,24576]{1,0:T(8,128)S(1)}, f32[16,24576]{1,0:T(8,128)}, u32[]{:S(2)}, u32[]{:S(2)}) collective-permute-start(f32[16,24576]{1,0:T(8,128)S(1)} %fusion.17), channel_id=1, source_target_pairs={{0,4},{1,5},{2,6},{3,7},{4,0},{5,1},{6,2},{7,3},{8,12},{9,13},{10,... | collective-permute-start | bytes 4718600 | tf_op jit(solution)/shard_map/ppermute | solution.py:29
  290.4 35.7 %collective-permute-start.5 = (f32[16,24576]{1,0:T(8,128)S(1)}, f32[16,24576]{1,0:T(8,128)}, u32[]{:S(2)}, u32[]{:S(2)}) collective-permute-start(f32[16,24576]{1,0:T(8,128)S(1)} %fusion.18), channel_id=1, source_target_pairs={{0,8},{1,9},{2,10},{3,11},{4,12},{5,13},{6,14},{7,15},{8,0},{9,1},... | collective-permute-start | bytes 4718600 | tf_op jit(solution)/shard_map/ppermute | solution.py:29
  346.1 5.2 %copy-start.13 = (s32[16]{0:T(128)S(1)}, s32[16]{0:T(128)}, u32[]{:S(2)}) copy-start(s32[16]{0:T(128)} %param.13) | copy-start | bytes 196
  347.6 37.0 %collective-permute-start.6 = (f32[16,24576]{1,0:T(8,128)S(1)}, f32[16,24576]{1,0:T(8,128)}, u32[]{:S(2)}, u32[]{:S(2)}) collective-permute-start(f32[16,24576]{1,0:T(8,128)S(1)} %fusion.19), channel_id=1, source_target_pairs={{0,16},{1,17},{2,18},{3,19},{4,20},{5,21},{6,22},{7,23},{8,24},{9,... | collective-permute-start | bytes 4718600 | tf_op jit(solution)/shard_map/ppermute | solution.py:29
where the time goes:
time: 430 us; the launch traced here: 422 us
  waiting for transfers between devices  227 us (53%)
  blocking collectives  79.4 us (18%)
  matrix products  42.5 us (10%)
  local copies, waits for them, and re-layouts  36.9 us (9%)
  starting transfers between devices  22.1 us (5%)
  between operations  7.42 us (2%)
  other arithmetic  6.66 us (2%)
    ppermute x5, waiting for transfers between devices, from_partner(): return lax.ppermute(value, axis, pairs)  227 us
    psum x5, blocking collectives, local(): gram_total = lax.psum(matmul(merged, merged.T), 'space')  66.9 us
    dot_general x22, matrix products, matmul(): jnp.dot(left, right, precision=HIGHEST, preferred_element_type=jnp.float32)  42.3 us
    ppermute x5, starting transfers between devices, from_partner(): return lax.ppermute(value, axis, pairs)  15.1 us
    psum x1, blocking collectives, local(): sign_value = lax.psum(picked, 'space')  12.5 us
  transfers between devices with their start and end apart: 7, of which 5 were waited for; matrix products, arithmetic and copies ran while one was open for 10% of the time, Pallas kernels for 0%

commit v1 on v0

v1 whole, which is shorter than its diff:
```python
import functools

import jax
import jax.numpy as jnp
from jax import lax
from jax.experimental import pallas as pl
from jax.experimental.pallas import tpu as pltpu
from jax.sharding import PartitionSpec as P

HIGHEST = lax.Precision.HIGHEST
VMEM = pl.BlockSpec(memory_space=pltpu.VMEM)
SMEM = pl.BlockSpec(memory_space=pltpu.SMEM)


def neighbours(cells, axis):
    count = lax.axis_size(axis)
    head, tail = cells[:, :, 0], cells[:, :, -1]
    below = lax.ppermute(tail, axis, [(i, i + 1) for i in range(count - 1)])
    above = lax.ppermute(head, axis, [(i + 1, i) for i in range(count - 1)])
    return below, above


def mm(left, right):
    return lax.dot_general(
        left, right, (((1,), (0,)), ((), ())), precision=HIGHEST, preferred_element_type=jnp.float32
    )


def mm_t(left, right):
    return lax.dot_general(
        left, right, (((1,), (1,)), ((), ())), precision=HIGHEST, preferred_element_type=jnp.float32
    )


def curl_kernel(metric_ref, block_ref, vel_ref, below_ref, above_ref, out_ref):
    snaps, _, rows_y, cells_x, _ = vel_ref.shape
    per_x = 3 * rows_y * snaps
    blocks = metric_ref.shape[0]
    half = []
    for y in range(rows_y):
        ids = block_ref[y]
        trio = []
        for k in range(3):
            value = jnp.full(ids.shape, metric_ref[0, k], jnp.float32)
            for b in range(1, blocks):
                value = jnp.where(ids == b, metric_ref[b, k], value)
            trio.append(0.5 * value)
        half.append(trio)

    def diff_x(field):
        return pltpu.roll(field, cells_x - 1, 0) - pltpu.roll(field, 1, 0)

    def diff_z(field):
        return pltpu.roll(field, field.shape[1] - 1, 1) - pltpu.roll(field, 1, 1)

    for s in range(snaps):
        u = [vel_ref[s, 0, y].astype(jnp.float32) for y in range(rows_y)]
        v = [vel_ref[s, 1, y].astype(jnp.float32) for y in range(rows_y)]
        w = [vel_ref[s, 2, y].astype(jnp.float32) for y in range(rows_y)]
        u_all = [below_ref[s, 0].astype(jnp.float32)] + u + [above_ref[s, 0].astype(jnp.float32)]
        w_all = [below_ref[s, 1].astype(jnp.float32)] + w + [above_ref[s, 1].astype(jnp.float32)]
        for y in range(rows_y):
            hx, hy, hz = half[y]
            trio = (
                hy * (w_all[y + 2] - w_all[y]) - hz * diff_z(v[y]),
                hz * diff_z(u[y]) - hx * diff_x(w[y]),
                hx * diff_x(v[y]) - hy * (u_all[y + 2] - u_all[y]),
            )
            for c in range(3):
                out_ref[pl.ds((c * rows_y + y) * snaps + s, cells_x, stride=per_x), :] = trio[c]


def gram_kernel(ref_pos_ref, field_ref, out_ref):
    groups, fields, snaps, lanes = field_ref.shape
    total = groups * snaps
    columns = [field_ref[:, f].reshape(total, lanes) for f in range(fields)]
    field = jnp.concatenate(columns, axis=1)
    gram = mm_t(field, field)
    positions = ref_pos_ref[...]
    hot = (lax.broadcasted_iota(jnp.int32, (lanes, fields * lanes), 1) == positions).astype(jnp.float32)
    picked = mm_t(field, hot)
    row = lax.broadcasted_iota(jnp.int32, gram.shape, 0)
    col = lax.broadcasted_iota(jnp.int32, gram.shape, 1)
    diagonal = jnp.sum(jnp.where(row == col, gram, 0.0), axis=1, keepdims=True)
    lane = lax.broadcasted_iota(jnp.int32, picked.shape, 1)
    extra = jnp.where(lane == 16, diagonal, picked)
    h = total // 2
    row_h = lax.broadcasted_iota(jnp.int32, (h, h), 0)
    col_h = lax.broadcasted_iota(jnp.int32, (h, h), 1)
    mixed = jnp.where(row_h <= col_h, gram[:h, :h], gram[h:, h:])
    out_ref[: groups // 2, :8] = mixed.reshape(groups // 2, snaps, h)
    out_ref[groups // 2 :, :8] = gram[:h, h:].reshape(groups // 2, snaps, h)
    out_ref[:, 8:] = extra.reshape(groups, snaps, h)


def sum_spread_kernel(parts_ref, out_ref):
    total = jnp.sum(parts_ref[...], axis=0)
    for i in range(out_ref.shape[0]):
        out_ref[i] = total


def sum_leaf_spread_kernel(parts_ref, leaf_ref, out_ref):
    total = jnp.sum(parts_ref[...], axis=0)
    snaps = leaf_ref.shape[1]
    bottom = total[snaps:]
    leaf = jnp.concatenate(
        [jnp.zeros((snaps, 32), jnp.float32), leaf_ref[0], jnp.zeros((snaps, 80), jnp.float32)], axis=1
    )
    for i in range(out_ref.shape[0]):
        out_ref[i, :snaps] = total[:snaps]
        out_ref[i, snaps:] = bottom + leaf


def tile_rows(block, count):
    return jnp.concatenate([block] * count, axis=0) if count > 1 else block


def spread(weights, count, span, offset=0):
    wide = tile_rows(weights, count)
    row = lax.broadcasted_iota(jnp.int32, wide.shape, 0)
    col = lax.broadcasted_iota(jnp.int32, wide.shape, 1)
    rank = weights.shape[0]
    return jnp.where(row // rank == col // span + offset, wide, 0.0)


def tree_kernel(cells_all, levels, table_ref, rot_ref, field_ref, out_ref):
    groups, fields, snaps, lanes = field_ref.shape
    total = groups * snaps
    h = total // 2
    packed = table_ref[:, :8].reshape(total, lanes)
    extra = table_ref[:, 8:].reshape(total, lanes)
    extra_t = extra.T
    picked = extra_t[:16]
    weights = extra_t[32:48]
    mixed = packed[:h]
    cross = packed[h:]
    mixed_t = mixed.T
    row = lax.broadcasted_iota(jnp.int32, (h, h), 0)
    col = lax.broadcasted_iota(jnp.int32, (h, h), 1)
    first = jnp.where(row <= col, mixed, mixed_t)
    last_diag = extra[h:, 16:17]
    last = jnp.where(row > col, mixed, jnp.where(row == col, last_diag, mixed_t))
    gram = jnp.concatenate(
        [jnp.concatenate([first, cross], axis=1), jnp.concatenate([cross.T, last], axis=1)], axis=0
    )
    row = lax.broadcasted_iota(jnp.int32, (total, total), 0)
    col = lax.broadcasted_iota(jnp.int32, (total, total), 1)
    rank = weights.shape[0]
    start = 0
    for level in range(levels):
        children = groups >> level
        width = children * rank
        base = start // lanes * lanes
        offset = (start - base) // rank
        cover = max(width, lanes)
        rot = rot_ref[:, base : base + cover]
        weights = mm(rot, spread(weights, cover // rank, total // children, offset))
        start += width
        nodes = children // 2
        span = total // nodes
        if nodes > 1:
            same = (row // span == col // span).astype(jnp.float32)
            local_gram = gram * same
        else:
            same = jnp.ones((total, total), jnp.float32)
            local_gram = gram
        moved = mm(weights, local_gram)
        own = jnp.sum(weights * moved, axis=0, keepdims=True)
        trace = mm(jnp.broadcast_to(own, (8, total)), same)[:1]
        wide = spread(weights, nodes, span)
        small = mm_t(moved, wide)
        turned = mm(small, wide)
        scale = (trace + 1e-06) / rank
        weights = 1.5 * weights - 0.5 * turned / scale
    norm_sq = jnp.sum(weights * mm(weights, gram), axis=1, keepdims=True)
    norm_sq = jnp.maximum(norm_sq, 0.0)
    value = jnp.sum(weights * picked, axis=1, keepdims=True)
    floor_value = 0.5 * jnp.sqrt(norm_sq / cells_all + 1e-06)
    weights = weights * (value / jnp.maximum(jnp.abs(value), floor_value))
    rows_y = out_ref.shape[2]
    for f in range(fields):
        modes = mm(weights, field_ref[:, f].reshape(total, lanes))
        out_ref[:, f // rows_y, f % rows_y, :] = modes


def call(kernel, shape, specs, *args, name):
    return pl.pallas_call(
        kernel,
        out_shape=jax.ShapeDtypeStruct(shape, jnp.float32),
        in_specs=specs,
        out_specs=VMEM,
        name=name,
        compiler_params=pltpu.CompilerParams(vmem_limit_bytes=48 * 2**20),
    )(*args)


def exchange(value, axis):
    return lax.all_to_all(value, axis, 0, 0, tiled=True)


def local(velocity, block_id, metric, leaf_rot, merge_rot, merge_order, ref_cell):
    snaps, _, rows_y, cells_x, cells_z = velocity.shape
    rank = leaf_rot.shape[2]
    groups = lax.axis_size("snap")
    slabs = lax.axis_size("space")
    snap_index = lax.axis_index("snap")
    space_index = lax.axis_index("space")
    fields = 3 * rows_y

    below, above = neighbours(velocity[:, 0::2], "space")
    swapped = jnp.where(merge_order[:, None, None] == 0, merge_rot, jnp.roll(merge_rot, rank, axis=1))
    rot = jnp.pad(jnp.transpose(swapped, (2, 0, 1)).reshape(rank, -1), ((0, 0), (0, 2 * rank)))
    plane = cells_x * cells_z
    rows_total = rows_y * slabs
    comp_of = ref_cell // (rows_total * plane)
    row_of = ref_cell // plane % rows_total - space_index * rows_y
    x_of = ref_cell % plane // cells_z
    here = (row_of >= 0) & (row_of < rows_y) & (x_of == snap_index)
    position = jnp.where(here, (comp_of * rows_y + row_of) * cells_z + ref_cell % cells_z, -1)
    position = jnp.pad(position, (0, cells_z - rank), constant_values=-1)[:, None]

    field = call(
        curl_kernel,
        (cells_x * fields * snaps, cells_z),
        [SMEM, VMEM, VMEM, VMEM, VMEM],
        metric,
        block_id,
        velocity,
        below,
        above,
        name="curl",
    )
    field = exchange(field.reshape(groups, fields * snaps, cells_z), "snap")
    field = field.reshape(groups, fields, snaps, cells_z)
    table = call(gram_kernel, (groups, 2 * snaps, cells_z), [VMEM, VMEM], position, field, name="gram")
    table = exchange(table, "snap")
    table = call(sum_spread_kernel, (slabs, 2 * snaps, cells_z), [VMEM], table, name="sum_snap")
    table = exchange(table, "space")
    table = call(
        sum_leaf_spread_kernel, (groups, 2 * snaps, cells_z), [VMEM, VMEM], table, leaf_rot, name="sum_space"
    )
    table = exchange(table, "snap")
    return call(
        functools.partial(tree_kernel, fields // 3 * plane * 3 * slabs, groups.bit_length() - 1),
        (rank, 3, rows_y, cells_z),
        [VMEM, VMEM, VMEM],
        table,
        rot,
        field,
        name="tree",
    )


def solution(mesh):
    placed = (
        P("snap", None, "space", None, None),
        P("space", None, None),
        P(),
        P("snap", None, None),
        P(),
        P(),
        P(),
    )
    return jax.shard_map(
        local, mesh=mesh, in_specs=placed, out_specs=P(None, None, "space", "snap"), check_vma=False
    )
```

time: 430 us -> 97.8 us (0.23)
  the two profiles are of different devices: /device:TPU:1 before, /device:TPU:32 now
where the time goes in v1:
time: 97.8 us; the launch traced here: 97.4 us
  waiting for transfers between devices  34.6 us (35%)
  blocking collectives  28.3 us (29%)
  starting transfers between devices  20.5 us (21%)
  Pallas kernels  11.4 us (12%)
  local copies, waits for them, and re-layouts  2.23 us (2%)
    all_to_all x2, waiting for transfers between devices, exchange(): return lax.all_to_all(value, axis, 0, 0, tiled=True)  33.8 us
    all_to_all x2, blocking collectives, exchange(): return lax.all_to_all(value, axis, 0, 0, tiled=True)  28.3 us
    all_to_all x2, starting transfers between devices, exchange(): return lax.all_to_all(value, axis, 0, 0, tiled=True)  16.1 us
    pallas_call x5, Pallas kernels, call(): pl.pallas_call(kernel, out_shape=jax.ShapeDtypeStruct(shape, jnp.float32)...  11.4 us
    ppermute x1, starting transfers between devices, neighbours(): below = lax.ppermute(tail, axis, [(i, i + 1) for i in range(count - 1)])  3.04 us
  transfers between devices with their start and end apart: 4, of which 3 were waited for; matrix products, arithmetic and copies ran while one was open for 1% of the time, Pallas kernels for 0%

profile of v1, /device:TPU:32, one launch (start us, length us, event | category | flops | bytes accessed | tf_op | source)
XLA Modules:
  0.0 97.4 jit_solution(3866830789593995684)
XLA Ops:
  0.0 1.0 slice.17
  1.0 0.0 copy-start
  1.0 0.0 copy-start.1
  1.0 0.0 copy-start.4
  1.0 1.4 %collective-permute-start.1 = (bf16[8,2,32,128]{3,2,1,0:T(8,128)(2,1)S(1)}, bf16[8,2,32,128]{3,2,1,0:T(8,128)(2,1)S(1)}, u32[]{:S(2)}, u32[]{:S(2)}) collective-permute-start(bf16[8,2,32,128]{3,2,1,0:T(8,128)(2,1)S(1)} %get-tuple-element.5), channel_id=1, source_target_pairs={{32,0},{64,32},{96,64},{128,96},{160,128},{192,160},{224,192},{33,... | collective-permute-start | bytes 393224 | tf_op jit(solution)/shard_map/ppermute | solution.py:19
  2.5 3.0 %collective-permute-start = (bf16[8,2,32,128]{3,2,1,0:T(8,128)(2,1)S(1)}, bf16[8,2,32,128]{3,2,1,0:T(8,128)(2,1)S(1)}, u32[]{:S(2)}, u32[]{:S(2)}) collective-permute-start(bf16[8,2,32,128]{3,2,1,0:T(8,128)(2,1)S(1)} %get-tuple-element.6), channel_id=1, source_target_pairs={{0,32},{32,64},{64,96},{96,128},{128,160},{160,192},{192,224},{1,3... | collective-permute-start | bytes 393224 | tf_op jit(solution)/shard_map/ppermute | solution.py:18
  5.5 0.0 copy-done.4
  5.5 0.1 copy.13.metric_ref
  5.6 0.0 collective-permute-done.1.above_ref
  5.6 0.9 collective-permute-done.below_ref
  6.5 0.0 copy-done
  6.5 0.0 copy-done.1
  6.5 2.1 %curl.1 = f32[1536,128]{1,0:T(8,128)} custom-call(f32[8,3]{1,0:T(8,128)S(1)} %copy.13.metric_ref, s32[2,32,128]{2,1,0:T(8,128)S(1)} %copy-done.1, bf16[8,3,2,32,128]{4,3,2,1,0:T(8,128)(2,1)S(1)} %copy-done, bf16[8,2,32,128]{3,2,1,0:T(8,128)(2,1)S(1)} %collective-permute-done.below_ref, bf16[8,2,32,128]{3,2,1,0:T(8,128)(2,1)S(1)} %collective-permute-done.1.above_ref), custom_call_target="tpu_custom_call" | custom-call | tf_op jit(solution)/shard_map/curl/pallas_call | solution.py:187
  8.5 11.4 %all-to-all-start = ((f32[32,48,128]{2,1,0:T(8,128)}), f32[32,48,128]{2,1,0:T(8,128)S(1)}, u32[]{:S(2)}, u32[]{:S(2)}) async-start(f32[32,48,128]{2,1,0:T(8,128)} %bitcast.3), calls=%async_computation | async-start | bytes 1572864 | tf_op jit(solution)/shard_map/all_to_all | solution.py:198
  19.9 0.0 copy-start.5
  19.9 0.6 copy-done.5
  20.6 0.1 copy.14.ref_pos_ref
  20.7 22.2 %all-to-all-done = f32[32,48,128]{2,1,0:T(8,128)S(1)} async-done(((f32[32,48,128]{2,1,0:T(8,128)}), f32[32,48,128]{2,1,0:T(8,128)S(1)}, u32[]{:S(2)}, u32[]{:S(2)}) %all-to-all-start) | async-done | bytes 786464 | tf_op jit(solution)/shard_map/all_to_all | solution.py:198
  42.9 1.5 %gram.1 = f32[32,16,128]{2,1,0:T(8,128)S(1)} custom-call(s32[128,1]{1,0:T(8,128)S(1)} %copy.14.ref_pos_ref, f32[32,6,8,128]{3,2,1,0:T(8,128)S(1)} %bitcast.14), custom_call_target="tpu_custom_call" | custom-call | tf_op jit(solution)/shard_map/gram/pallas_call | solution.py:187
  44.5 18.6 %all_to_all.20.parts_ref = f32[32,16,128]{2,1,0:T(8,128)S(1)} all-to-all(f32[32,16,128]{2,1,0:T(8,128)S(1)} %gram.1), channel_id=1, replica_groups=mesh['space'=8,'snap'=32] {'snap'}, dimensions={0} | all-to-all | bytes 524288 | tf_op jit(solution)/shard_map/all_to_all | solution.py:198
  63.0 0.0 copy-start.2
  63.1 9.7 %all_to_all.21.parts_ref = f32[8,16,128]{2,1,0:T(8,128)S(1)} all-to-all(f32[8,16,128]{2,1,0:T(8,128)S(1)} %sum_snap.1), channel_id=1, replica_groups=mesh['space'=8,'snap'=32] {'space'}, dimensions={0} | all-to-all | bytes 131072 | tf_op jit(solution)/shard_map/all_to_all | solution.py:198
  72.8 0.0 copy-done.2
  72.8 0.8 sum_space.1
  73.6 0.0 copy-start.6
  73.6 0.0 copy-start.3
  73.6 4.7 %all-to-all-start.3 = ((f32[32,16,128]{2,1,0:T(8,128)}), f32[32,16,128]{2,1,0:T(8,128)S(1)}, u32[]{:S(2)}, u32[]{:S(2)}) async-start(f32[32,16,128]{2,1,0:T(8,128)} %sum_space.1), calls=%async_computation.3 | async-start | bytes 524288 | tf_op jit(solution)/shard_map/all_to_all | solution.py:198
  78.3 0.0 copy-done.6
  78.3 0.0 copy-done.3
  78.3 0.1 fusion.4
  78.4 0.2 fusion
  78.6 0.1 copy.15
  78.7 0.1 reshape.13
  78.9 11.6 %all-to-all-done.3.table_ref = f32[32,16,128]{2,1,0:T(8,128)S(1)} async-done(((f32[32,16,128]{2,1,0:T(8,128)}), f32[32,16,128]{2,1,0:T(8,128)S(1)}, u32[]{:S(2)}, u32[]{:S(2)}) %all-to-all-start.3) | async-done | bytes 262176 | tf_op jit(solution)/shard_map/all_to_all | solution.py:198
  90.4 7.0 %tree.1 = f32[16,3,2,128]{3,2,1,0:T(2,128)} custom-call(f32[32,16,128]{2,1,0:T(8,128)S(1)} %all-to-all-done.3.table_ref, f32[16,1024]{1,0:T(8,128)S(1)} %pad.9.rot_ref, f32[32,6,8,128]{3,2,1,0:T(8,128)S(1)} %bitcast.15), custom_call_target="tpu_custom_call" | custom-call | tf_op jit(solution)/shard_map/tree/pallas_call | solution.py:187
  (6 shorter events, 0.1 us)
Async XLA Ops:
  1.0 5.5 %copy-start = (bf16[8,3,2,32,128]{4,3,2,1,0:T(8,128)(2,1)S(1)}, bf16[8,3,2,32,128]{4,3,2,1,0:T(8,128)(2,1)}, u32[]{:S(2)}) copy-start(bf16[8,3,2,32,128]{4,3,2,1,0:T(8,128)(2,1)} %vel_ref.1) | copy-start | bytes 1179652
  1.0 5.5 %copy-start.1 = (s32[2,32,128]{2,1,0:T(8,128)S(1)}, s32[2,32,128]{2,1,0:T(8,128)}, u32[]{:S(2)}) copy-start(s32[2,32,128]{2,1,0:T(8,128)} %block_ref.1) | copy-start | bytes 98308
  1.0 4.5 %copy-start.4 = (f32[8,3]{0,1:T(4,128)S(1)}, f32[8,3]{0,1:T(4,128)}, u32[]{:S(2)}) copy-start(f32[8,3]{0,1:T(4,128)} %param.9) | copy-start | bytes 292
  1.0 4.6 %collective-permute-start.1 = (bf16[8,2,32,128]{3,2,1,0:T(8,128)(2,1)S(1)}, bf16[8,2,32,128]{3,2,1,0:T(8,128)(2,1)S(1)}, u32[]{:S(2)}, u32[]{:S(2)}) collective-permute-start(bf16[8,2,32,128]{3,2,1,0:T(8,128)(2,1)S(1)} %get-tuple-element.5), channel_id=1, source_target_pairs={{32,0},{64,32},{96,64},{128,96},{160,128},{192,160},{224,192},{33,... | collective-permute-start | bytes 393224 | tf_op jit(solution)/shard_map/ppermute | solution.py:19
  2.5 4.0 %collective-permute-start = (bf16[8,2,32,128]{3,2,1,0:T(8,128)(2,1)S(1)}, bf16[8,2,32,128]{3,2,1,0:T(8,128)(2,1)S(1)}, u32[]{:S(2)}, u32[]{:S(2)}) collective-permute-start(bf16[8,2,32,128]{3,2,1,0:T(8,128)(2,1)S(1)} %get-tuple-element.6), channel_id=1, source_target_pairs={{0,32},{32,64},{64,96},{96,128},{128,160},{160,192},{192,224},{1,3... | collective-permute-start | bytes 393224 | tf_op jit(solution)/shard_map/ppermute | solution.py:18
  8.5 34.4 %all-to-all-start = ((f32[32,48,128]{2,1,0:T(8,128)}), f32[32,48,128]{2,1,0:T(8,128)S(1)}, u32[]{:S(2)}, u32[]{:S(2)}) async-start(f32[32,48,128]{2,1,0:T(8,128)} %bitcast.3), calls=%async_computation | async-start | bytes 1572864 | tf_op jit(solution)/shard_map/all_to_all | solution.py:198
  19.9 0.7 copy-start.5
  63.0 9.7 %copy-start.2 = (f32[1,8,16]{2,1,0:T(8,128)S(1)}, f32[1,8,16]{2,1,0:T(8,128)}, u32[]{:S(2)}) copy-start(f32[1,8,16]{2,1,0:T(8,128)} %leaf_ref.1) | copy-start | bytes 1540
  73.6 4.7 %copy-start.6 = (s32[31]{0:T(128)S(1)}, s32[31]{0:T(128)}, u32[]{:S(2)}) copy-start(s32[31]{0:T(128)} %param.12) | copy-start | bytes 376
  73.6 4.7 %copy-start.3 = (f32[31,32,16]{1,2,0:T(8,128)S(1)}, f32[31,32,16]{1,2,0:T(8,128)}, u32[]{:S(2)}) copy-start(f32[31,32,16]{1,2,0:T(8,128)} %param.11) | copy-start | bytes 190468
  73.6 16.9 %all-to-all-start.3 = ((f32[32,16,128]{2,1,0:T(8,128)}), f32[32,16,128]{2,1,0:T(8,128)S(1)}, u32[]{:S(2)}, u32[]{:S(2)}) async-start(f32[32,16,128]{2,1,0:T(8,128)} %sum_space.1), calls=%async_computation.3 | async-start | bytes 524288 | tf_op jit(solution)/shard_map/all_to_all | solution.py:198

commit v2 on v1

--- a/solution.py
+++ b/solution.py
@@ -12,14 +12,6 @@
 SMEM = pl.BlockSpec(memory_space=pltpu.SMEM)
 
 
-def neighbours(cells, axis):
-    count = lax.axis_size(axis)
-    head, tail = cells[:, :, 0], cells[:, :, -1]
-    below = lax.ppermute(tail, axis, [(i, i + 1) for i in range(count - 1)])
-    above = lax.ppermute(head, axis, [(i + 1, i) for i in range(count - 1)])
-    return below, above
-
-
 def mm(left, right):
     return lax.dot_general(
         left, right, (((1,), (0,)), ((), ())), precision=HIGHEST, preferred_element_type=jnp.float32
@@ -32,49 +24,54 @@
     )
 
 
-def curl_kernel(metric_ref, block_ref, vel_ref, below_ref, above_ref, out_ref):
-    snaps, _, rows_y, cells_x, _ = vel_ref.shape
-    per_x = 3 * rows_y * snaps
-    blocks = metric_ref.shape[0]
-    half = []
+SLOTS = {(0, 0): 0, (2, 0): 1, (1, 0): 2, (1, 1): 3, (2, 1): 4, (0, 1): 5}
+
+
+def pack_kernel(vel_ref, out_ref, rows_ref):
+    snaps, comps, rows_y, cells_x, lanes = vel_ref.shape
+    per_x = comps * rows_y * snaps
+    for (c, y), slot in SLOTS.items():
+        for s in range(snaps):
+            rows_ref[pl.ds(slot * snaps + s, cells_x, stride=per_x), :] = vel_ref[s, c, y].astype(jnp.float32)
+    out_ref[...] = rows_ref[...].reshape(cells_x, per_x, lanes).astype(out_ref.dtype)
+
+
+def gram_kernel(metric_ref, block_ref, ref_pos_ref, own_ref, left_ref, right_ref, below_ref, above_ref, field_ref, out_ref):
+    groups, per_x, lanes = own_ref.shape
+    rows_y = block_ref.shape[0]
+    fields = 3 * rows_y
+    snaps = per_x // fields
+    total = groups * snaps
+
+    def rows(ref, slot):
+        return ref[:, slot * snaps : (slot + 1) * snaps, :].astype(jnp.float32).reshape(total, lanes)
+
+    def diff_z(field):
+        return pltpu.roll(field, lanes - 1, 1) - pltpu.roll(field, 1, 1)
+
+    def diff_x(c, y):
+        slot = SLOTS[c, y] - 1
+        return rows(right_ref, slot) - rows(left_ref, slot)
+
+    u, v, w = ([rows(own_ref, SLOTS[c, y]) for y in range(rows_y)] for c in range(3))
+    u_all = [rows(below_ref, 1)] + u + [rows(above_ref, 0)]
+    w_all = [rows(below_ref, 0)] + w + [rows(above_ref, 1)]
     for y in range(rows_y):
         ids = block_ref[y]
-        trio = []
+        half = []
         for k in range(3):
             value = jnp.full(ids.shape, metric_ref[0, k], jnp.float32)
-            for b in range(1, blocks):
+            for b in range(1, metric_ref.shape[0]):
                 value = jnp.where(ids == b, metric_ref[b, k], value)
-            trio.append(0.5 * value)
-        half.append(trio)
-
-    def diff_x(field):
-        return pltpu.roll(field, cells_x - 1, 0) - pltpu.roll(field, 1, 0)
-
-    def diff_z(field):
-        return pltpu.roll(field, field.shape[1] - 1, 1) - pltpu.roll(field, 1, 1)
-
-    for s in range(snaps):
-        u = [vel_ref[s, 0, y].astype(jnp.float32) for y in range(rows_y)]
-        v = [vel_ref[s, 1, y].astype(jnp.float32) for y in range(rows_y)]
-        w = [vel_ref[s, 2, y].astype(jnp.float32) for y in range(rows_y)]
-        u_all = [below_ref[s, 0].astype(jnp.float32)] + u + [above_ref[s, 0].astype(jnp.float32)]
-        w_all = [below_ref[s, 1].astype(jnp.float32)] + w + [above_ref[s, 1].astype(jnp.float32)]
-        for y in range(rows_y):
-            hx, hy, hz = half[y]
-            trio = (
-                hy * (w_all[y + 2] - w_all[y]) - hz * diff_z(v[y]),
-                hz * diff_z(u[y]) - hx * diff_x(w[y]),
-                hx * diff_x(v[y]) - hy * (u_all[y + 2] - u_all[y]),
-            )
-            for c in range(3):
-                out_ref[pl.ds((c * rows_y + y) * snaps + s, cells_x, stride=per_x), :] = trio[c]
-
-
-def gram_kernel(ref_pos_ref, field_ref, out_ref):
-    groups, fields, snaps, lanes = field_ref.shape
-    total = groups * snaps
-    columns = [field_ref[:, f].reshape(total, lanes) for f in range(fields)]
-    field = jnp.concatenate(columns, axis=1)
+            half.append(0.5 * value)
+        hx, hy, hz = half
+        field_ref[:, y * lanes : (y + 1) * lanes] = hy * (w_all[y + 2] - w_all[y]) - hz * diff_z(v[y])
+        at = rows_y + y
+        field_ref[:, at * lanes : (at + 1) * lanes] = hz * diff_z(u[y]) - hx * diff_x(2, y)
+        at = 2 * rows_y + y
+        field_ref[:, at * lanes : (at + 1) * lanes] = hx * diff_x(1, y) - hy * (u_all[y + 2] - u_all[y])
+
+    field = field_ref[...]
     gram = mm_t(field, field)
     positions = ref_pos_ref[...]
     hot = (lax.broadcasted_iota(jnp.int32, (lanes, fields * lanes), 1) == positions).astype(jnp.float32)
@@ -124,7 +121,8 @@
 
 
 def tree_kernel(cells_all, levels, table_ref, rot_ref, field_ref, out_ref):
-    groups, fields, snaps, lanes = field_ref.shape
+    groups, rows_all, lanes = table_ref.shape
+    snaps = rows_all // 2
     total = groups * snaps
     h = total // 2
     packed = table_ref[:, :8].reshape(total, lanes)
@@ -178,20 +176,26 @@
     floor_value = 0.5 * jnp.sqrt(norm_sq / cells_all + 1e-06)
     weights = weights * (value / jnp.maximum(jnp.abs(value), floor_value))
     rows_y = out_ref.shape[2]
-    for f in range(fields):
-        modes = mm(weights, field_ref[:, f].reshape(total, lanes))
-        out_ref[:, f // rows_y, f % rows_y, :] = modes
-
-
-def call(kernel, shape, specs, *args, name):
+    modes = mm(weights, field_ref[...])
+    for f in range(3 * rows_y):
+        out_ref[:, f // rows_y, f % rows_y, :] = modes[:, f * lanes : (f + 1) * lanes]
+
+
+def call(kernel, shapes, specs, *args, name, scratch=()):
+    outs = jax.tree.map(lambda _: VMEM, shapes)
     return pl.pallas_call(
         kernel,
-        out_shape=jax.ShapeDtypeStruct(shape, jnp.float32),
+        out_shape=shapes,
         in_specs=specs,
-        out_specs=VMEM,
+        out_specs=outs,
+        scratch_shapes=scratch,
         name=name,
         compiler_params=pltpu.CompilerParams(vmem_limit_bytes=48 * 2**20),
     )(*args)
+
+
+def f32(*shape):
+    return jax.ShapeDtypeStruct(shape, jnp.float32)
 
 
 def exchange(value, axis):
@@ -207,7 +211,6 @@
     space_index = lax.axis_index("space")
     fields = 3 * rows_y
 
-    below, above = neighbours(velocity[:, 0::2], "space")
     swapped = jnp.where(merge_order[:, None, None] == 0, merge_rot, jnp.roll(merge_rot, rank, axis=1))
     rot = jnp.pad(jnp.transpose(swapped, (2, 0, 1)).reshape(rank, -1), ((0, 0), (0, 2 * rank)))
     plane = cells_x * cells_z
@@ -219,30 +222,47 @@
     position = jnp.where(here, (comp_of * rows_y + row_of) * cells_z + ref_cell % cells_z, -1)
     position = jnp.pad(position, (0, cells_z - rank), constant_values=-1)[:, None]
 
-    field = call(
-        curl_kernel,
-        (cells_x * fields * snaps, cells_z),
-        [SMEM, VMEM, VMEM, VMEM, VMEM],
+    ids = lax.dynamic_slice_in_dim(block_id, snap_index, 1, 1)
+
+    per_x = fields * snaps
+    packed = call(
+        pack_kernel,
+        jax.ShapeDtypeStruct((cells_x, per_x, cells_z), velocity.dtype),
+        [VMEM],
+        velocity,
+        name="pack",
+        scratch=[pltpu.VMEM((cells_x * per_x, cells_z), jnp.float32)],
+    )
+    own = exchange(packed, "snap")
+    inner = own[:, snaps : 5 * snaps]
+    left = lax.ppermute(inner, "snap", [(i, (i + 1) % groups) for i in range(groups)])
+    right = lax.ppermute(inner, "snap", [((i + 1) % groups, i) for i in range(groups)])
+    below = lax.ppermute(own[:, 4 * snaps :], "space", [(i, i + 1) for i in range(slabs - 1)])
+    above = lax.ppermute(own[:, : 2 * snaps], "space", [(i + 1, i) for i in range(slabs - 1)])
+    field, table = call(
+        gram_kernel,
+        (f32(groups * snaps, fields * cells_z), f32(groups, 2 * snaps, cells_z)),
+        [SMEM] + [VMEM] * 7,
         metric,
-        block_id,
-        velocity,
+        ids,
+        position,
+        own,
+        left,
+        right,
         below,
         above,
-        name="curl",
-    )
-    field = exchange(field.reshape(groups, fields * snaps, cells_z), "snap")
-    field = field.reshape(groups, fields, snaps, cells_z)
-    table = call(gram_kernel, (groups, 2 * snaps, cells_z), [VMEM, VMEM], position, field, name="gram")
+        name="gram",
+    )
     table = exchange(table, "snap")
-    table = call(sum_spread_kernel, (slabs, 2 * snaps, cells_z), [VMEM], table, name="sum_snap")
+    table = call(sum_spread_kernel, f32(slabs, 2 * snaps, cells_z), [VMEM], table, name="sum_snap")
     table = exchange(table, "space")
     table = call(
-        sum_leaf_spread_kernel, (groups, 2 * snaps, cells_z), [VMEM, VMEM], table, leaf_rot, name="sum_space"
+        sum_leaf_spread_kernel, f32(groups, 2 * snaps, cells_z), [VMEM, VMEM], table, leaf_rot, name="sum_space"
     )
     table = exchange(table, "snap")
     return call(
-        functools.partial(tree_kernel, fields // 3 * plane * 3 * slabs, groups.bit_length() - 1),
-        (rank, 3, rows_y, cells_z),
+        functools.partial(tree_kernel, fields * plane * slabs, groups.bit_length() - 1),
+        f32(rank, 3, rows_y, cells_z),
         [VMEM, VMEM, VMEM],
         table,
         rot,

time: 97.8 us -> 95.2 us (0.973)
  waiting for transfers between devices: 34.6 us -> 28.6 us
  blocking collectives: 28.3 us -> 30.8 us
    all_to_all x2, waiting for transfers between devices: 33.8 us -> 25.8 us  [exchange(): return lax.all_to_all(value, axis, 0, 0, tiled=True)]
    all_to_all x2, blocking collectives: 28.3 us -> 30.8 us  [exchange(): return lax.all_to_all(value, axis, 0, 0, tiled=True)]
    ppermute x2 -> x4, waiting for transfers between devices: 0.87 us -> 2.87 us  [the longest x1 2.86 us: local(): lax.ppermute(own[:, :2 * snaps], 'space', [(i + 1, i) for i in range(slab...]
    unnamed x15, local copies, waits for them, and re-layouts: 0.76 us -> 2.31 us
    ppermute x2 -> x4, starting transfers between devices: 4.46 us -> 4.69 us  [the longest x1 1.3 us: local(): lax.ppermute(own[:, 4 * snaps:], 'space', [(i, i + 1) for i in range(slab...]
  transfers between devices with their start and end apart: 4 -> 6, of which waited for: 3 -> 3; matrix products, arithmetic and copies ran while one was open for 1% -> 1% of each run, Pallas kernels for 0% -> 0%
where the time goes in v2:
time: 95.2 us; the launch traced here: 94.8 us
  blocking collectives  30.8 us (32%)
  waiting for transfers between devices  28.6 us (30%)
  starting transfers between devices  21 us (22%)
  Pallas kernels  11.2 us (12%)
  local copies, waits for them, and re-layouts  2.83 us (3%)
    all_to_all x2, blocking collectives, exchange(): return lax.all_to_all(value, axis, 0, 0, tiled=True)  30.8 us
    all_to_all x2, waiting for transfers between devices, exchange(): return lax.all_to_all(value, axis, 0, 0, tiled=True)  25.8 us
    all_to_all x2, starting transfers between devices, exchange(): return lax.all_to_all(value, axis, 0, 0, tiled=True)  16.3 us
    pallas_call x5, Pallas kernels, call(): pl.pallas_call(kernel, out_shape=shapes, in_specs=specs, out_specs=outs,...  11.2 us
    ppermute x1, waiting for transfers between devices, local(): lax.ppermute(own[:, :2 * snaps], 'space', [(i + 1, i) for i in range(slab...  2.86 us
    unnamed x15, local copies, waits for them, and re-layouts  2.31 us
  transfers between devices with their start and end apart: 6, of which 3 were waited for; matrix products, arithmetic and copies ran while one was open for 1% of the time, Pallas kernels for 0%

profile of v2, /device:TPU:32, one launch (start us, length us, event | category | flops | bytes accessed | tf_op | source)
XLA Modules:
  0.0 94.8 jit_solution(16310985809387016812)
XLA Ops:
  0.0 0.0 copy-start
  0.0 0.0 copy-start.1
  0.0 1.0 %copy-done.1 = bf16[8,3,2,32,128]{4,3,2,1,0:T(8,128)(2,1)S(1)} copy-done((bf16[8,3,2,32,128]{4,3,2,1,0:T(8,128)(2,1)S(1)}, bf16[8,3,2,32,128]{4,3,2,1,0:T(8,128)(2,1)}, u32[]{:S(2)}) %copy-start.1) | copy-done | bytes 393240
  1.0 1.1 %pack.1 = bf16[32,48,128]{2,1,0:T(8,128)(2,1)} custom-call(bf16[8,3,2,32,128]{4,3,2,1,0:T(8,128)(2,1)S(1)} %copy-done.1), custom_call_target="tpu_custom_call" | custom-call | tf_op jit(solution)/shard_map/pack/pallas_call | solution.py:186
  2.1 11.4 %all-to-all-start = ((bf16[32,48,128]{2,1,0:T(8,128)(2,1)}), bf16[32,48,128]{2,1,0:T(8,128)(2,1)S(1)}, u32[]{:S(2)}, u32[]{:S(2)}) async-start(bf16[32,48,128]{2,1,0:T(8,128)(2,1)} %pack.1), calls=%async_computation | async-start | bytes 786432 | tf_op jit(solution)/shard_map/all_to_all | solution.py:202
  13.5 0.0 copy-start.5
  13.5 0.6 copy-done.5
  14.2 14.2 %all-to-all-done.own_ref = bf16[32,48,128]{2,1,0:T(8,128)(2,1)S(1)} async-done(((bf16[32,48,128]{2,1,0:T(8,128)(2,1)}), bf16[32,48,128]{2,1,0:T(8,128)(2,1)S(1)}, u32[]{:S(2)}, u32[]{:S(2)}) %all-to-all-start) | async-done | bytes 393248 | tf_op jit(solution)/shard_map/all_to_all | solution.py:202
  28.4 0.9 collective-permute-start
  29.3 1.2 %collective-permute-start.1 = (bf16[32,32,128]{2,1,0:T(8,128)(2,1)S(1)}, bf16[32,32,128]{2,1,0:T(8,128)(2,1)S(1)}, u32[]{:S(2)}, u32[]{:S(2)}) collective-permute-start(bf16[32,32,128]{2,1,0:T(8,128)(2,1)S(1)} %slice.22), channel_id=1, source_target_pairs={{1,0},{2,1},{3,2},{4,3},{5,4},{6,5},{7,6},{8,7},{9,8},{10,9},{11,1... | collective-permute-start | bytes 786440 | tf_op jit(solution)/shard_map/ppermute | solution.py:239
  30.5 1.3 %collective-permute-start.2 = (bf16[32,16,128]{2,1,0:T(8,128)(2,1)S(1)}, bf16[32,16,128]{2,1,0:T(8,128)(2,1)S(1)}, u32[]{:S(2)}, u32[]{:S(2)}) collective-permute-start(bf16[32,16,128]{2,1,0:T(8,128)(2,1)S(1)} %get-tuple-element.10), channel_id=1, source_target_pairs={{0,32},{32,64},{64,96},{96,128},{128,160},{160,192},{192,224},{1,3... | collective-permute-start | bytes 393224 | tf_op jit(solution)/shard_map/ppermute | solution.py:240
  31.8 1.3 %collective-permute-start.3 = (bf16[32,16,128]{2,1,0:T(8,128)(2,1)S(1)}, bf16[32,16,128]{2,1,0:T(8,128)(2,1)S(1)}, u32[]{:S(2)}, u32[]{:S(2)}) collective-permute-start(bf16[32,16,128]{2,1,0:T(8,128)(2,1)S(1)} %get-tuple-element.9), channel_id=1, source_target_pairs={{32,0},{64,32},{96,64},{128,96},{160,128},{192,160},{224,192},{33,... | collective-permute-start | bytes 393224 | tf_op jit(solution)/shard_map/ppermute | solution.py:241
  33.1 0.0 copy-start.4
  33.1 0.1 copy.12.ref_pos_ref
  33.3 0.6 copy-done.4
  33.8 0.1 copy.11.metric_ref
  33.9 0.0 copy-done
  33.9 0.0 collective-permute-done.2.below_ref
  33.9 2.9 %collective-permute-done.3.above_ref = bf16[32,16,128]{2,1,0:T(8,128)(2,1)S(1)} collective-permute-done((bf16[32,16,128]{2,1,0:T(8,128)(2,1)S(1)}, bf16[32,16,128]{2,1,0:T(8,128)(2,1)S(1)}, u32[]{:S(2)}, u32[]{:S(2)}) %collective-permute-start.3) | collective-permute-done | bytes 131104 | tf_op jit(solution)/shard_map/ppermute | solution.py:241
  36.8 0.0 collective-permute-done.left_ref
  36.8 0.0 collective-permute-done.1.right_ref
  36.8 2.2 %gram.1 = (f32[256,768]{1,0:T(8,128)S(1)}, f32[32,16,128]{2,1,0:T(8,128)S(1)}) custom-call(f32[8,3]{1,0:T(8,128)S(1)} %copy.11.metric_ref, s32[2,1,128]{2,1,0:T(1,128)S(1)} %constant_dynamic-slice_fusion.block_ref, s32[128,1]{1,0:T(8,128)S(1)} %copy.12.ref_pos_ref, bf16[32,48,128]{2,1,0:T(8,128)(2,1)S(1)} %all-to-all-done.own_ref, ...), custom_call_target="tpu_custom_call" | custom-call | tf_op jit(solution)/shard_map/gram/pallas_call | solution.py:186
  39.0 20.6 %all_to_all.20.parts_ref = f32[32,16,128]{2,1,0:T(8,128)S(1)} all-to-all(f32[32,16,128]{2,1,0:T(8,128)S(1)} %get-tuple-element.7), channel_id=1, replica_groups=mesh['space'=8,'snap'=32] {'snap'}, dimensions={0} | all-to-all | bytes 524288 | tf_op jit(solution)/shard_map/all_to_all | solution.py:202
  59.6 0.0 copy-start.2
  59.6 10.2 %all_to_all.21.parts_ref = f32[8,16,128]{2,1,0:T(8,128)S(1)} all-to-all(f32[8,16,128]{2,1,0:T(8,128)S(1)} %sum_snap.1), channel_id=1, replica_groups=mesh['space'=8,'snap'=32] {'space'}, dimensions={0} | all-to-all | bytes 131072 | tf_op jit(solution)/shard_map/all_to_all | solution.py:202
  69.8 0.0 copy-done.2
  69.8 0.8 sum_space.1
  70.6 0.0 copy-start.6
  70.6 0.0 copy-start.3
  70.6 4.9 %all-to-all-start.3 = ((f32[32,16,128]{2,1,0:T(8,128)}), f32[32,16,128]{2,1,0:T(8,128)S(1)}, u32[]{:S(2)}, u32[]{:S(2)}) async-start(f32[32,16,128]{2,1,0:T(8,128)} %sum_space.1), calls=%async_computation.3 | async-start | bytes 524288 | tf_op jit(solution)/shard_map/all_to_all | solution.py:202
  75.5 0.0 copy-done.6
  75.5 0.0 copy-done.3
  75.5 0.1 fusion.5
  75.7 0.2 fusion
  75.8 0.1 copy.13
  75.9 0.1 reshape.5
  76.1 11.6 %all-to-all-done.3.table_ref = f32[32,16,128]{2,1,0:T(8,128)S(1)} async-done(((f32[32,16,128]{2,1,0:T(8,128)}), f32[32,16,128]{2,1,0:T(8,128)S(1)}, u32[]{:S(2)}, u32[]{:S(2)}) %all-to-all-start.3) | async-done | bytes 262176 | tf_op jit(solution)/shard_map/all_to_all | solution.py:202
  87.7 7.1 %tree.1 = f32[16,3,2,128]{3,2,1,0:T(2,128)} custom-call(f32[32,16,128]{2,1,0:T(8,128)S(1)} %all-to-all-done.3.table_ref, f32[16,1024]{1,0:T(8,128)S(1)} %pad.9.rot_ref, f32[256,768]{1,0:T(8,128)S(1)} %get-tuple-element.8.field_ref), custom_call_target="tpu_custom_call" | custom-call | tf_op jit(solution)/shard_map/tree/pallas_call | solution.py:186
  (8 shorter events, 0.1 us)
Async XLA Ops:
  0.0 33.9 %copy-start = (s32[2,32,128]{2,1,0:T(8,128)S(1)}, s32[2,32,128]{2,1,0:T(8,128)}, u32[]{:S(2)}) copy-start(s32[2,32,128]{2,1,0:T(8,128)} %param.8) | copy-start | bytes 98308
  0.0 1.0 %copy-start.1 = (bf16[8,3,2,32,128]{4,3,2,1,0:T(8,128)(2,1)S(1)}, bf16[8,3,2,32,128]{4,3,2,1,0:T(8,128)(2,1)}, u32[]{:S(2)}) copy-start(bf16[8,3,2,32,128]{4,3,2,1,0:T(8,128)(2,1)} %vel_ref.1) | copy-start | bytes 1179652
  2.1 26.2 %all-to-all-start = ((bf16[32,48,128]{2,1,0:T(8,128)(2,1)}), bf16[32,48,128]{2,1,0:T(8,128)(2,1)S(1)}, u32[]{:S(2)}, u32[]{:S(2)}) async-start(bf16[32,48,128]{2,1,0:T(8,128)(2,1)} %pack.1), calls=%async_computation | async-start | bytes 786432 | tf_op jit(solution)/shard_map/all_to_all | solution.py:202
  13.5 0.7 copy-start.5
  28.4 8.4 %collective-permute-start = (bf16[32,32,128]{2,1,0:T(8,128)(2,1)S(1)}, bf16[32,32,128]{2,1,0:T(8,128)(2,1)S(1)}, u32[]{:S(2)}, u32[]{:S(2)}) collective-permute-start(bf16[32,32,128]{2,1,0:T(8,128)(2,1)S(1)} %slice.22), channel_id=1, source_target_pairs={{0,1},{1,2},{2,3},{3,4},{4,5},{5,6},{6,7},{7,8},{8,9},{9,10},{10,1... | collective-permute-start | bytes 786440 | tf_op jit(solution)/shard_map/ppermute | solution.py:238
  29.3 7.5 %collective-permute-start.1 = (bf16[32,32,128]{2,1,0:T(8,128)(2,1)S(1)}, bf16[32,32,128]{2,1,0:T(8,128)(2,1)S(1)}, u32[]{:S(2)}, u32[]{:S(2)}) collective-permute-start(bf16[32,32,128]{2,1,0:T(8,128)(2,1)S(1)} %slice.22), channel_id=1, source_target_pairs={{1,0},{2,1},{3,2},{4,3},{5,4},{6,5},{7,6},{8,7},{9,8},{10,9},{11,1... | collective-permute-start | bytes 786440 | tf_op jit(solution)/shard_map/ppermute | solution.py:239
  30.5 3.4 %collective-permute-start.2 = (bf16[32,16,128]{2,1,0:T(8,128)(2,1)S(1)}, bf16[32,16,128]{2,1,0:T(8,128)(2,1)S(1)}, u32[]{:S(2)}, u32[]{:S(2)}) collective-permute-start(bf16[32,16,128]{2,1,0:T(8,128)(2,1)S(1)} %get-tuple-element.10), channel_id=1, source_target_pairs={{0,32},{32,64},{64,96},{96,128},{128,160},{160,192},{192,224},{1,3... | collective-permute-start | bytes 393224 | tf_op jit(solution)/shard_map/ppermute | solution.py:240
  31.8 5.0 %collective-permute-start.3 = (bf16[32,16,128]{2,1,0:T(8,128)(2,1)S(1)}, bf16[32,16,128]{2,1,0:T(8,128)(2,1)S(1)}, u32[]{:S(2)}, u32[]{:S(2)}) collective-permute-start(bf16[32,16,128]{2,1,0:T(8,128)(2,1)S(1)} %get-tuple-element.9), channel_id=1, source_target_pairs={{32,0},{64,32},{96,64},{128,96},{160,128},{192,160},{224,192},{33,... | collective-permute-start | bytes 393224 | tf_op jit(solution)/shard_map/ppermute | solution.py:241
  33.1 0.7 copy-start.4
  59.6 10.2 %copy-start.2 = (f32[1,8,16]{2,1,0:T(8,128)S(1)}, f32[1,8,16]{2,1,0:T(8,128)}, u32[]{:S(2)}) copy-start(f32[1,8,16]{2,1,0:T(8,128)} %leaf_ref.1) | copy-start | bytes 1540
  70.6 4.9 %copy-start.6 = (s32[31]{0:T(128)S(1)}, s32[31]{0:T(128)}, u32[]{:S(2)}) copy-start(s32[31]{0:T(128)} %param.12) | copy-start | bytes 376
  70.6 4.9 %copy-start.3 = (f32[31,32,16]{1,2,0:T(8,128)S(1)}, f32[31,32,16]{1,2,0:T(8,128)}, u32[]{:S(2)}) copy-start(f32[31,32,16]{1,2,0:T(8,128)} %param.11) | copy-start | bytes 190468
  70.6 17.1 %all-to-all-start.3 = ((f32[32,16,128]{2,1,0:T(8,128)}), f32[32,16,128]{2,1,0:T(8,128)S(1)}, u32[]{:S(2)}, u32[]{:S(2)}) async-start(f32[32,16,128]{2,1,0:T(8,128)} %sum_space.1), calls=%async_computation.3 | async-start | bytes 524288 | tf_op jit(solution)/shard_map/all_to_all | solution.py:202

commit v3 on v2

v3 whole, which is shorter than its diff:
```python
import functools

import jax
import jax.numpy as jnp
from jax import lax
from jax.experimental import pallas as pl
from jax.experimental.pallas import tpu as pltpu
from jax.sharding import PartitionSpec as P

HIGHEST = lax.Precision.HIGHEST
VMEM = pl.BlockSpec(memory_space=pltpu.VMEM)
SNAP = ("y", "z")
WIDE = ("space", "y")


BF16 = jnp.bfloat16


def split3(value):
    high = value.astype(BF16)
    rest = value - high.astype(jnp.float32)
    middle = rest.astype(BF16)
    low = (rest - middle.astype(jnp.float32)).astype(BF16)
    return high, middle, low


def dot(left, right, transposed=False):
    dims = (((1,), (1 if transposed else 0,)), ((), ()))
    return lax.dot_general(left, right, dims, preferred_element_type=jnp.float32)


def mm3(left, right, transposed=False):
    rows = left[0].shape[0]
    high = dot(jnp.concatenate(left, axis=0), right[0], transposed)
    middle = dot(jnp.concatenate(left[:2], axis=0), right[1], transposed)
    low = dot(left[0], right[2], transposed)
    small = low + middle[rows:] + high[2 * rows :]
    return small + (middle[:rows] + high[rows : 2 * rows]) + high[:rows]


SLOTS = {(0, 0): 0, (2, 0): 1, (1, 0): 2, (1, 1): 3, (2, 1): 4, (0, 1): 5}


def pack_kernel(vel_hbm, out_hbm, vel_ref, rows_ref, out_ref, in_sems, out_sems):
    snaps, comps, rows_y, cells_x, lanes = vel_hbm.shape
    arrivals, leaving = {}, []
    for (c, y), slot in SLOTS.items():
        arrivals[slot] = pltpu.make_async_copy(vel_hbm.at[:, c, y], vel_ref.at[slot], in_sems.at[slot])
        arrivals[slot].start()
    for slot, copy in arrivals.items():
        copy.wait()
        for s in range(snaps):
            rows_ref[slot, pl.ds(s, cells_x, stride=snaps), :] = vel_ref[slot, s].astype(jnp.float32)
        out_ref[slot] = rows_ref[slot].reshape(cells_x, snaps, lanes).astype(out_ref.dtype)
        target = out_hbm.at[:, pl.ds(slot * snaps, snaps)]
        leaving.append(pltpu.make_async_copy(out_ref.at[slot], target, out_sems.at[slot]))
        leaving[-1].start()
    for copy in leaving:
        copy.wait()


def gram_kernel(
    half_ref, ref_pos_ref, own_ref, left_ref, right_ref, below_ref, above_ref, leaf_ref,
    parts_ref, out_ref
):
    groups, per_x, lanes = own_ref.shape
    rows_y = half_ref.shape[0]
    fields = 3 * rows_y
    snaps = per_x // fields
    total = groups * snaps

    def rows(ref, slot):
        return ref[:, slot * snaps : (slot + 1) * snaps, :].astype(jnp.float32).reshape(total, lanes)

    def diff_z(field):
        return pltpu.roll(field, lanes - 1, 1) - pltpu.roll(field, 1, 1)

    def diff_x(c, y):
        slot = SLOTS[c, y] - 1
        return rows(right_ref, slot) - rows(left_ref, slot)

    u, v, w = ([rows(own_ref, SLOTS[c, y]) for y in range(rows_y)] for c in range(3))
    u_all = [rows(below_ref, 1)] + u + [rows(above_ref, 0)]
    w_all = [rows(below_ref, 0)] + w + [rows(above_ref, 1)]
    pieces = [None] * fields
    for y in range(rows_y):
        half = (half_ref[y, k : k + 1] for k in range(3))
        hx, hy, hz = half
        pieces[y] = hy * (w_all[y + 2] - w_all[y]) - hz * diff_z(v[y])
        pieces[rows_y + y] = hz * diff_z(u[y]) - hx * diff_x(2, y)
        pieces[2 * rows_y + y] = hx * diff_x(1, y) - hy * (u_all[y + 2] - u_all[y])
    for f, piece in enumerate(pieces):
        for i, part in enumerate(split3(piece)):
            parts_ref[i * total : (i + 1) * total, f * lanes : (f + 1) * lanes] = part

    high = dot(parts_ref[...], parts_ref[:total], True)
    middle = dot(parts_ref[: 2 * total], parts_ref[total : 2 * total], True)
    low = dot(parts_ref[:total], parts_ref[2 * total :], True)
    gram = low + middle[total:] + high[2 * total :]
    gram = gram + (middle[:total] + high[total : 2 * total]) + high[:total]
    positions = ref_pos_ref[...]
    hot = (lax.broadcasted_iota(jnp.int32, (lanes, fields * lanes), 1) == positions).astype(jnp.float32).astype(BF16)
    picked = dot(parts_ref[...], hot, True)
    picked = picked[:total] + picked[total : 2 * total] + picked[2 * total :]
    row = lax.broadcasted_iota(jnp.int32, gram.shape, 0)
    col = lax.broadcasted_iota(jnp.int32, gram.shape, 1)
    diagonal = jnp.sum(jnp.where(row == col, gram, 0.0), axis=1, keepdims=True)
    lane = lax.broadcasted_iota(jnp.int32, picked.shape, 1)
    extra = jnp.where(lane == 16, diagonal, picked)
    h = total // 2
    row_h = lax.broadcasted_iota(jnp.int32, (h, h), 0)
    col_h = lax.broadcasted_iota(jnp.int32, (h, h), 1)
    mixed = jnp.where(row_h <= col_h, gram[:h, :h], gram[h:, h:])
    out_ref[: groups // 2, :8] = mixed.reshape(groups // 2, snaps, h)
    out_ref[groups // 2 :, :8] = gram[:h, h:].reshape(groups // 2, snaps, h)
    out_ref[:, 8:] = extra.reshape(groups, snaps, h) + leaf_ref[...][None]


def sum_spread_kernel(parts_ref, out_ref):
    total = jnp.sum(parts_ref[...], axis=0)
    for i in range(out_ref.shape[0]):
        out_ref[i] = total


def start_kernel(parts_ref, children_ref, weights_ref, rotate_ref):
    snaps = parts_ref.shape[1] // 2
    rank, total = weights_ref.shape
    levels = rotate_ref.shape[1] // total + 1
    misc = parts_ref[:, snaps:].reshape(-1, parts_ref.shape[2]).T
    count = total // misc.shape[1]
    leaves = jnp.concatenate([misc[(2 + i) * rank : (3 + i) * rank] for i in range(count)], axis=1)
    tables = jnp.concatenate(split3(children_ref[...].T), axis=0)
    width = tables.shape[1]
    child = lax.broadcasted_iota(jnp.int32, (width, total), 0)
    snap = lax.broadcasted_iota(jnp.int32, (width, total), 1)
    first, span = 0, snaps
    for level in range(levels):
        chosen = (child == first + snap // span).astype(jnp.float32).astype(BF16)
        first, span = first + total // span, span * 2
        spread = dot(tables, chosen)
        size = spread.shape[0] // 3
        spread = spread[:size] + spread[size : 2 * size] + spread[2 * size :]
        if level:
            rotate_ref[:, (level - 1) * total : level * total] = spread
        else:
            weights_ref[...] = rotated(leaves, spread)


def rotated(weights, rotate_ref):
    rank = weights.shape[0]
    total = rotate_ref[:rank] * weights[:1]
    for a in range(1, rank):
        total = total + rotate_ref[a * rank : (a + 1) * rank] * weights[a : a + 1]
    return total


def tree_kernel(cells_all, table_ref, weights_ref, rotate_ref, parts_ref, out_ref):
    groups, rows_all, lanes = table_ref.shape
    snaps = rows_all // 2
    rank = weights_ref.shape[0]
    total = groups * snaps
    h = total // 2
    packed = table_ref[:, :snaps].reshape(total, lanes)
    extra = table_ref[:, snaps:].reshape(total, lanes)
    picked = extra.T[:rank]
    mixed = packed[:h]
    cross = packed[h:]
    mixed_t = mixed.T
    row = lax.broadcasted_iota(jnp.int32, (h, h), 0)
    col = lax.broadcasted_iota(jnp.int32, (h, h), 1)
    first = jnp.where(row <= col, mixed, mixed_t)
    last = jnp.where(row > col, mixed, jnp.where(row == col, extra[h:, rank : rank + 1], mixed_t))
    first = split3(first)
    last = split3(last)
    cross = split3(cross)

    def moved_by(left):
        lower = tuple(part[:, :h] for part in left)
        upper = tuple(part[:, h:] for part in left)
        begin = mm3(lower, first) + mm3(upper, cross, True)
        return jnp.concatenate([begin, mm3(lower, cross) + mm3(upper, last)], axis=1)

    row_all = lax.broadcasted_iota(jnp.int32, (total, total), 0)
    col_all = lax.broadcasted_iota(jnp.int32, (total, total), 1)
    weights = weights_ref[...]
    levels = groups.bit_length() - 1
    for level in range(levels):
        span = 2 * snaps << level
        if level:
            weights = rotated(weights, rotate_ref.at[:, (level - 1) * total : level * total])
        left = split3(weights)
        same = (row_all // span == col_all // span).astype(jnp.float32).astype(BF16)
        if span < total:
            inside = same[:h, :h]
            begin = mm3(tuple(part[:, :h] for part in left), tuple(part * inside for part in first))
            end = mm3(tuple(part[:, h:] for part in left), tuple(part * inside for part in last))
            moved = jnp.concatenate([begin, end], axis=1)
        else:
            moved = moved_by(left)
        own = jnp.sum(weights * moved, axis=0, keepdims=True)
        products = [weights[j : j + 1] * moved for j in range(rank)]
        products = jnp.concatenate(products + [jnp.broadcast_to(own, (rank, total))], axis=0)
        upper = products.astype(BF16)
        lower = (products - upper.astype(jnp.float32)).astype(BF16)
        count = products.shape[0]
        sums = dot(jnp.concatenate([upper, lower], axis=0), same)
        sums = sums[count:] + sums[:count]
        scale = (sums[rank * rank :] + 1e-06) / rank
        turned = sums[:rank] * weights[:1]
        for j in range(1, rank):
            turned = turned + sums[j * rank : (j + 1) * rank] * weights[j : j + 1]
        weights = 1.5 * weights - 0.5 * turned / scale
    norm_sq = jnp.sum(weights * moved_by(split3(weights)), axis=1, keepdims=True)
    norm_sq = jnp.maximum(norm_sq, 0.0)
    value = jnp.sum(weights * picked, axis=1, keepdims=True)
    floor_value = 0.5 * jnp.sqrt(norm_sq / cells_all + 1e-06)
    weights = weights * (value / jnp.maximum(jnp.abs(value), floor_value))
    rows_y = out_ref.shape[2]
    modes = mm3(split3(weights), tuple(parts_ref[i * total : (i + 1) * total] for i in range(3)))
    for f in range(3 * rows_y):
        out_ref[:, f // rows_y, f % rows_y, :] = modes[:, f * lanes : (f + 1) * lanes]


def call(kernel, shapes, specs, *args, name, scratch=()):
    outs = jax.tree.map(lambda _: VMEM, shapes)
    return pl.pallas_call(
        kernel,
        out_shape=shapes,
        in_specs=specs,
        out_specs=outs,
        scratch_shapes=scratch,
        name=name,
        compiler_params=pltpu.CompilerParams(vmem_limit_bytes=20 * 2**20),
    )(*args)


def f32(*shape):
    return jax.ShapeDtypeStruct(shape, jnp.float32)


def exchange(value, axis):
    return lax.all_to_all(value, axis, 0, 0, tiled=True)


def child_maps(merge_rot, merge_order):
    rank = merge_rot.shape[2]
    swapped = jnp.where(merge_order[:, None, None] == 0, merge_rot, jnp.roll(merge_rot, rank, axis=1))
    children = swapped.reshape(-1, rank * rank)
    return jnp.pad(children, ((0, -children.shape[0] % 128), (0, 0)))


def local(velocity, block_id, metric, leaf_rot, merge_rot, merge_order, ref_cell):
    snaps, _, rows_y, cells_x, cells_z = velocity.shape
    rank = leaf_rot.shape[2]
    groups = lax.axis_size(SNAP)
    slabs = lax.axis_size("space")
    snap_index = lax.axis_index(SNAP)
    space_index = lax.axis_index("space")
    fields = 3 * rows_y
    total = groups * snaps
    plane = cells_x * cells_z

    per_x = fields * snaps
    packed = pl.pallas_call(
        pack_kernel,
        out_shape=jax.ShapeDtypeStruct((cells_x, per_x, cells_z), velocity.dtype),
        in_specs=[pl.BlockSpec(memory_space=pl.ANY)],
        out_specs=pl.BlockSpec(memory_space=pl.ANY),
        scratch_shapes=[
            pltpu.VMEM((fields, snaps, cells_x, cells_z), velocity.dtype),
            pltpu.VMEM((fields, cells_x * snaps, cells_z), jnp.float32),
            pltpu.VMEM((fields, cells_x, snaps, cells_z), velocity.dtype),
            pltpu.SemaphoreType.DMA((fields,)),
            pltpu.SemaphoreType.DMA((fields,)),
        ],
        name="pack",
    )(velocity)
    own = exchange(packed, SNAP)

    children = child_maps(merge_rot, merge_order)
    rows_total = rows_y * slabs
    comp_of = ref_cell // (rows_total * plane)
    row_of = ref_cell // plane % rows_total - space_index * rows_y
    x_of = ref_cell % plane // cells_z
    here = (row_of >= 0) & (row_of < rows_y) & (x_of == snap_index)
    position = jnp.where(here, (comp_of * rows_y + row_of) * cells_z + ref_cell % cells_z, -1)
    position = jnp.pad(position, (0, cells_z - rank), constant_values=-1)[:, None]
    ids = lax.dynamic_index_in_dim(block_id, snap_index, 1, keepdims=False)
    half = 0.5 * sum(
        jnp.where(ids[:, None] == b, metric[b][None, :, None], 0.0) for b in range(metric.shape[0])
    )
    slot = jnp.arange(cells_z, dtype=jnp.int32) // rank - 2
    leaf_here = (slot == lax.axis_index("y")) & (space_index == 0)
    leaf_tile = jnp.where(leaf_here, jnp.tile(leaf_rot[0], (1, cells_z // rank)), 0.0)

    own, children, position, half, leaf_tile = lax.optimization_barrier((own, children, position, half, leaf_tile))
    inner = own[:, snaps : 5 * snaps]
    below = lax.ppermute(own[:, 4 * snaps :], "space", [(i, i + 1) for i in range(slabs - 1)])
    above = lax.ppermute(own[:, : 2 * snaps], "space", [(i + 1, i) for i in range(slabs - 1)])
    left = lax.ppermute(inner, SNAP, [(i, (i + 1) % groups) for i in range(groups)])
    right = lax.ppermute(inner, SNAP, [((i + 1) % groups, i) for i in range(groups)])
    field_parts, table = call(
        gram_kernel,
        (jax.ShapeDtypeStruct((3 * total, fields * cells_z), BF16), f32(groups, 2 * snaps, cells_z)),
        [VMEM] * 8,
        half,
        position,
        own,
        left,
        right,
        below,
        above,
        leaf_tile,
        name="gram",
    )
    table = exchange(table, WIDE)
    table = call(sum_spread_kernel, f32(lax.axis_size("z"), 2 * snaps, cells_z), [VMEM], table, name="sum_wide")
    parts, children = lax.optimization_barrier((exchange(table, "z"), children))
    table = call(sum_spread_kernel, f32(groups, 2 * snaps, cells_z), [VMEM], parts, name="sum_z")
    table = exchange(table, WIDE)
    levels = groups.bit_length() - 1
    weights, rotate = call(
        start_kernel,
        (f32(rank, total), f32(rank * rank, (levels - 1) * total)),
        [VMEM, VMEM],
        parts,
        children,
        name="start",
    )
    return call(
        functools.partial(tree_kernel, fields * plane * slabs),
        f32(rank, 3, rows_y, cells_z),
        [VMEM] * 4,
        table,
        weights,
        rotate,
        field_parts,
        name="tree",
    )


def solution(mesh):
    torus = jax.sharding.Mesh(mesh.devices.reshape(mesh.shape["space"], 4, -1), ("space", "y", "z"))
    placed = (
        P(SNAP, None, "space", None, None),
        P("space", None, None),
        P(),
        P(SNAP, None, None),
        P(),
        P(),
        P(),
    )
    return jax.shard_map(
        local, mesh=torus, in_specs=placed, out_specs=P(None, None, "space", SNAP), check_vma=False
    )
```

time: 95.2 us -> 87.7 us (0.921)
  the two profiles are of different devices: /device:TPU:32 before, /device:TPU:1 now
where the time goes in v3:
time: 87.7 us; the launch traced here: 87.2 us
  starting transfers between devices  28.7 us (33%)
  blocking collectives  27.8 us (32%)
  waiting for transfers between devices  19.5 us (22%)
  Pallas kernels  8.79 us (10%)
  local copies, waits for them, and re-layouts  1.17 us (1%)
  other arithmetic  1.02 us (1%)
    all_to_all x2, blocking collectives, exchange(): return lax.all_to_all(value, axis, 0, 0, tiled=True)  27.8 us
    all_to_all x2, waiting for transfers between devices, exchange(): return lax.all_to_all(value, axis, 0, 0, tiled=True)  17.7 us
    all_to_all x2, starting transfers between devices, exchange(): return lax.all_to_all(value, axis, 0, 0, tiled=True)  17.5 us
    pallas_call x5, Pallas kernels, call(): pl.pallas_call(kernel, out_shape=shapes, in_specs=specs, out_specs=outs,...  6.94 us
    ppermute x1, starting transfers between devices, local(): lax.ppermute(own[:, :2 * snaps], 'space', [(i + 1, i) for i in range(slab...  4.45 us
    ppermute x1, starting transfers between devices, local(): lax.ppermute(inner, SNAP, [((i + 1) % groups, i) for i in range(groups)])  3.7 us
    ppermute x1, starting transfers between devices, local(): lax.ppermute(own[:, 4 * snaps:], 'space', [(i, i + 1) for i in range(slab...  3.02 us
    pallas_call x1, Pallas kernels, local(): pl.pallas_call(pack_kernel, out_shape=jax.ShapeDtypeStruct((cells_x, per_...  1.85 us
  transfers between devices with their start and end apart: 6, of which 4 were waited for; matrix products, arithmetic and copies ran while one was open for 2% of the time, Pallas kernels for 1%

profile of v3, /device:TPU:1, one launch (start us, length us, event | category | flops | bytes accessed | tf_op | source)
XLA Modules:
  0.0 87.2 jit_solution(5516934465459809837)
XLA Ops:
  0.0 0.0 copy-start.4
  0.0 0.0 copy-start.1
  0.0 0.0 copy-start.2
  0.0 0.0 copy-start
  0.0 1.8 %pack.1 = bf16[32,48,128]{2,1,0:T(8,128)(2,1)} custom-call(bf16[8,3,2,32,128]{4,3,2,1,0:T(8,128)(2,1)} %vel_hbm.1), custom_call_target="tpu_custom_call" | custom-call | tf_op jit(solution)/shard_map/pack/pallas_call | solution.py:264
  1.9 12.0 %all-to-all-start = ((bf16[32,48,128]{2,1,0:T(8,128)(2,1)}), bf16[32,48,128]{2,1,0:T(8,128)(2,1)S(1)}, u32[]{:S(2)}, u32[]{:S(2)}) async-start(bf16[32,48,128]{2,1,0:T(8,128)(2,1)} %pack.1), calls=%async_computation | async-start | bytes 786432 | tf_op jit(solution)/shard_map/all_to_all | solution.py:242
  13.9 0.0 copy-done.4
  14.0 0.0 copy-done.1
  14.0 0.3 slice_reduce_fusion.7
  14.3 0.7 broadcast_compare_fusion.7
  15.0 0.0 copy-done.2
  15.0 0.1 tile.12
  15.1 0.0 copy-done
  15.1 0.1 fusion.5
  15.2 0.0 copy-start.3
  15.2 0.2 maximum_select_fusion
  15.4 0.2 copy.10
  15.6 0.2 reshape.17
  15.9 0.0 copy-done.3
  16.0 0.1 add_multiply_fusion.half_ref
  16.1 9.5 %all-to-all-done.own_ref = bf16[32,48,128]{2,1,0:T(8,128)(2,1)S(1)} async-done(((bf16[32,48,128]{2,1,0:T(8,128)(2,1)}), bf16[32,48,128]{2,1,0:T(8,128)(2,1)S(1)}, u32[]{:S(2)}, u32[]{:S(2)}) %all-to-all-start) | async-done | bytes 393248 | tf_op jit(solution)/shard_map/all_to_all | solution.py:242
  25.7 3.7 %collective-permute-start.1 = (bf16[32,32,128]{2,1,0:T(8,128)(2,1)S(1)}, bf16[32,32,128]{2,1,0:T(8,128)(2,1)S(1)}, u32[]{:S(2)}, u32[]{:S(2)}) collective-permute-start(bf16[32,32,128]{2,1,0:T(8,128)(2,1)S(1)} %slice.51), channel_id=1, source_target_pairs={{1,0},{2,1},{3,2},{4,3},{5,4},{6,5},{7,6},{8,7},{9,8},{10,9},{11,1... | collective-permute-start | bytes 786440 | tf_op jit(solution)/shard_map/ppermute | solution.py:301
  29.4 0.0 collective-permute-start
  29.4 4.5 %collective-permute-start.3 = (bf16[32,16,128]{2,1,0:T(8,128)(2,1)S(1)}, bf16[32,16,128]{2,1,0:T(8,128)(2,1)S(1)}, u32[]{:S(2)}, u32[]{:S(2)}) collective-permute-start(bf16[32,16,128]{2,1,0:T(8,128)(2,1)S(1)} %get-tuple-element.37), channel_id=1, source_target_pairs={{32,0},{64,32},{96,64},{128,96},{160,128},{192,160},{224,192},{33,... | collective-permute-start | bytes 393224 | tf_op jit(solution)/shard_map/ppermute | solution.py:299
  33.8 3.0 %collective-permute-start.2 = (bf16[32,16,128]{2,1,0:T(8,128)(2,1)S(1)}, bf16[32,16,128]{2,1,0:T(8,128)(2,1)S(1)}, u32[]{:S(2)}, u32[]{:S(2)}) collective-permute-start(bf16[32,16,128]{2,1,0:T(8,128)(2,1)S(1)} %get-tuple-element.38), channel_id=1, source_target_pairs={{0,32},{32,64},{64,96},{96,128},{128,160},{160,192},{192,224},{1,3... | collective-permute-start | bytes 393224 | tf_op jit(solution)/shard_map/ppermute | solution.py:298
  36.9 0.1 copy.11.ref_pos_ref
  37.0 0.6 collective-permute-done.3.above_ref
  37.6 1.2 %collective-permute-done.2.below_ref = bf16[32,16,128]{2,1,0:T(8,128)(2,1)S(1)} collective-permute-done((bf16[32,16,128]{2,1,0:T(8,128)(2,1)S(1)}, bf16[32,16,128]{2,1,0:T(8,128)(2,1)S(1)}, u32[]{:S(2)}, u32[]{:S(2)}) %collective-permute-start.2) | collective-permute-done | bytes 131104 | tf_op jit(solution)/shard_map/ppermute | solution.py:298
  38.8 0.0 collective-permute-done.1.right_ref
  38.8 0.0 collective-permute-done.left_ref
  38.8 1.6 %gram.1 = (bf16[768,768]{1,0:T(8,128)(2,1)S(1)}, f32[32,16,128]{2,1,0:T(8,128)S(1)}) custom-call(f32[2,3,128]{2,1,0:T(4,128)S(1)} %add_multiply_fusion.half_ref, s32[128,1]{1,0:T(8,128)S(1)} %copy.11.ref_pos_ref, bf16[32,48,128]{2,1,0:T(8,128)(2,1)S(1)} %all-to-all-done.own_ref, bf16[32,32,128]{2,1,0:T(8,128)(2,1)S(1)} %collective-permute-done.left_ref, ...), custom_call_target="tpu_custom_call" | custom-call | tf_op jit(solution)/shard_map/gram/pallas_call | solution.py:226
  40.4 15.8 %all_to_all.20.parts_ref = f32[32,16,128]{2,1,0:T(8,128)S(1)} all-to-all(f32[32,16,128]{2,1,0:T(8,128)S(1)} %get-tuple-element.20), channel_id=1, replica_groups=mesh['space'=8,'y'=4,'z'=8] {'space','y'}, dimensions={0} | all-to-all | bytes 524288 | tf_op jit(solution)/shard_map/all_to_all | solution.py:242
  56.3 12.0 %all_to_all.21.parts_ref = f32[8,16,128]{2,1,0:T(8,128)S(1)} all-to-all(f32[8,16,128]{2,1,0:T(8,128)S(1)} %sum_wide.1), channel_id=1, replica_groups=mesh['space'=8,'y'=4,'z'=8] {'z'}, dimensions={0} | all-to-all | bytes 131072 | tf_op jit(solution)/shard_map/all_to_all | solution.py:242
  68.3 0.7 sum_z.1
  69.0 5.5 %all-to-all-start.3 = ((f32[32,16,128]{2,1,0:T(8,128)}), f32[32,16,128]{2,1,0:T(8,128)S(1)}, u32[]{:S(2)}, u32[]{:S(2)}) async-start(f32[32,16,128]{2,1,0:T(8,128)} %sum_z.1), calls=%async_computation.3 | async-start | bytes 524288 | tf_op jit(solution)/shard_map/all_to_all | solution.py:242
  74.5 0.7 start.1
  75.2 8.2 %all-to-all-done.3.table_ref = f32[32,16,128]{2,1,0:T(8,128)S(1)} async-done(((f32[32,16,128]{2,1,0:T(8,128)}), f32[32,16,128]{2,1,0:T(8,128)S(1)}, u32[]{:S(2)}, u32[]{:S(2)}) %all-to-all-start.3) | async-done | bytes 262176 | tf_op jit(solution)/shard_map/all_to_all | solution.py:242
  83.3 3.9 %tree.1 = f32[16,3,2,128]{3,2,1,0:T(2,128)} custom-call(f32[32,16,128]{2,1,0:T(8,128)S(1)} %all-to-all-done.3.table_ref, f32[16,256]{1,0:T(8,128)S(1)} %get-tuple-element.24.weights_ref, f32[256,1024]{1,0:T(8,128)S(1)} %get-tuple-element.25.rotate_ref, bf16[768,768]{1,0:T(8,128)(2,1)S(1)} %get-tuple-element.26.parts_ref), custom_call_target="tpu_custom_call" | custom-call | tf_op jit(solution)/shard_map/tree/pallas_call | solution.py:226
  (15 shorter events, 0.2 us)
Async XLA Ops:
  0.0 13.9 %copy-start.4 = (s32[31]{0:T(128)S(1)}, s32[31]{0:T(128)}, u32[]{:S(2)}) copy-start(s32[31]{0:T(128)} %param.12) | copy-start | bytes 376
  0.0 14.0 %copy-start.1 = (f32[8,3]{0,1:T(4,128)S(1)}, f32[8,3]{0,1:T(4,128)}, u32[]{:S(2)}) copy-start(f32[8,3]{0,1:T(4,128)} %param.9) | copy-start | bytes 292
  0.0 15.0 %copy-start.2 = (f32[1,8,16]{2,1,0:T(8,128)S(1)}, f32[1,8,16]{2,1,0:T(8,128)}, u32[]{:S(2)}) copy-start(f32[1,8,16]{2,1,0:T(8,128)} %param.10) | copy-start | bytes 1540
  0.0 15.1 %copy-start = (f32[31,32,16]{1,2,0:T(8,128)S(1)}, f32[31,32,16]{1,2,0:T(8,128)}, u32[]{:S(2)}) copy-start(f32[31,32,16]{1,2,0:T(8,128)} %param.11) | copy-start | bytes 190468
  1.9 23.8 %all-to-all-start = ((bf16[32,48,128]{2,1,0:T(8,128)(2,1)}), bf16[32,48,128]{2,1,0:T(8,128)(2,1)S(1)}, u32[]{:S(2)}, u32[]{:S(2)}) async-start(bf16[32,48,128]{2,1,0:T(8,128)(2,1)} %pack.1), calls=%async_computation | async-start | bytes 786432 | tf_op jit(solution)/shard_map/all_to_all | solution.py:242
  15.2 0.7 copy-start.3
  25.7 13.1 %collective-permute-start.1 = (bf16[32,32,128]{2,1,0:T(8,128)(2,1)S(1)}, bf16[32,32,128]{2,1,0:T(8,128)(2,1)S(1)}, u32[]{:S(2)}, u32[]{:S(2)}) collective-permute-start(bf16[32,32,128]{2,1,0:T(8,128)(2,1)S(1)} %slice.51), channel_id=1, source_target_pairs={{1,0},{2,1},{3,2},{4,3},{5,4},{6,5},{7,6},{8,7},{9,8},{10,9},{11,1... | collective-permute-start | bytes 786440 | tf_op jit(solution)/shard_map/ppermute | solution.py:301
  29.4 9.4 %collective-permute-start = (bf16[32,32,128]{2,1,0:T(8,128)(2,1)S(1)}, bf16[32,32,128]{2,1,0:T(8,128)(2,1)S(1)}, u32[]{:S(2)}, u32[]{:S(2)}) collective-permute-start(bf16[32,32,128]{2,1,0:T(8,128)(2,1)S(1)} %slice.51), channel_id=1, source_target_pairs={{0,1},{1,2},{2,3},{3,4},{4,5},{5,6},{6,7},{7,8},{8,9},{9,10},{10,1... | collective-permute-start | bytes 786440 | tf_op jit(solution)/shard_map/ppermute | solution.py:300
  29.4 8.2 %collective-permute-start.3 = (bf16[32,16,128]{2,1,0:T(8,128)(2,1)S(1)}, bf16[32,16,128]{2,1,0:T(8,128)(2,1)S(1)}, u32[]{:S(2)}, u32[]{:S(2)}) collective-permute-start(bf16[32,16,128]{2,1,0:T(8,128)(2,1)S(1)} %get-tuple-element.37), channel_id=1, source_target_pairs={{32,0},{64,32},{96,64},{128,96},{160,128},{192,160},{224,192},{33,... | collective-permute-start | bytes 393224 | tf_op jit(solution)/shard_map/ppermute | solution.py:299
  33.8 5.0 %collective-permute-start.2 = (bf16[32,16,128]{2,1,0:T(8,128)(2,1)S(1)}, bf16[32,16,128]{2,1,0:T(8,128)(2,1)S(1)}, u32[]{:S(2)}, u32[]{:S(2)}) collective-permute-start(bf16[32,16,128]{2,1,0:T(8,128)(2,1)S(1)} %get-tuple-element.38), channel_id=1, source_target_pairs={{0,32},{32,64},{64,96},{96,128},{128,160},{160,192},{192,224},{1,3... | collective-permute-start | bytes 393224 | tf_op jit(solution)/shard_map/ppermute | solution.py:298
  69.0 14.4 %all-to-all-start.3 = ((f32[32,16,128]{2,1,0:T(8,128)}), f32[32,16,128]{2,1,0:T(8,128)S(1)}, u32[]{:S(2)}, u32[]{:S(2)}) async-start(f32[32,16,128]{2,1,0:T(8,128)} %sum_z.1), calls=%async_computation.3 | async-start | bytes 524288 | tf_op jit(solution)/shard_map/all_to_all | solution.py:242

commit v4 on v3

--- a/solution.py
+++ b/solution.py
@@ -60,7 +60,7 @@
 
 
 def gram_kernel(
-    half_ref, ref_pos_ref, own_ref, left_ref, right_ref, below_ref, above_ref, leaf_ref,
+    half_ref, ref_pos_ref, own_ref, left_ref, right_ref, chip_ref, next_ref, even_ref, leaf_ref,
     parts_ref, out_ref
 ):
     groups, per_x, lanes = own_ref.shape
@@ -80,8 +80,11 @@
         return rows(right_ref, slot) - rows(left_ref, slot)
 
     u, v, w = ([rows(own_ref, SLOTS[c, y]) for y in range(rows_y)] for c in range(3))
-    u_all = [rows(below_ref, 1)] + u + [rows(above_ref, 0)]
-    w_all = [rows(below_ref, 0)] + w + [rows(above_ref, 1)]
+    even = even_ref[:1] > 0
+    chip = [rows(chip_ref, i) for i in range(2)]
+    beyond = [rows(next_ref, i) for i in range(2)]
+    u_all = [jnp.where(even, beyond[1], chip[1])] + u + [jnp.where(even, chip[0], beyond[0])]
+    w_all = [jnp.where(even, beyond[0], chip[0])] + w + [jnp.where(even, chip[1], beyond[1])]
     pieces = [None] * fields
     for y in range(rows_y):
         half = (half_ref[y, k : k + 1] for k in range(3))
@@ -93,20 +96,26 @@
         for i, part in enumerate(split3(piece)):
             parts_ref[i * total : (i + 1) * total, f * lanes : (f + 1) * lanes] = part
 
-    high = dot(parts_ref[...], parts_ref[:total], True)
-    middle = dot(parts_ref[: 2 * total], parts_ref[total : 2 * total], True)
-    low = dot(parts_ref[:total], parts_ref[2 * total :], True)
+    count = ref_pos_ref.shape[0]
+    hot = lax.broadcasted_iota(jnp.int32, (count, fields * lanes), 1) == ref_pos_ref[...]
+    hot = hot.astype(jnp.float32).astype(BF16)
+
+    def against(rows, part):
+        streamed = jnp.concatenate([hot, parts_ref[:rows]], axis=0)
+        result = dot(streamed, parts_ref[part * total : (part + 1) * total], True)
+        return result[:count], result[count:]
+
+    picked_high, high = against(3 * total, 0)
+    picked_middle, middle = against(2 * total, 1)
+    picked_low, low = against(total, 2)
+    picked = picked_low + picked_middle + picked_high
     gram = low + middle[total:] + high[2 * total :]
     gram = gram + (middle[:total] + high[total : 2 * total]) + high[:total]
-    positions = ref_pos_ref[...]
-    hot = (lax.broadcasted_iota(jnp.int32, (lanes, fields * lanes), 1) == positions).astype(jnp.float32).astype(BF16)
-    picked = dot(parts_ref[...], hot, True)
-    picked = picked[:total] + picked[total : 2 * total] + picked[2 * total :]
     row = lax.broadcasted_iota(jnp.int32, gram.shape, 0)
     col = lax.broadcasted_iota(jnp.int32, gram.shape, 1)
-    diagonal = jnp.sum(jnp.where(row == col, gram, 0.0), axis=1, keepdims=True)
-    lane = lax.broadcasted_iota(jnp.int32, picked.shape, 1)
-    extra = jnp.where(lane == 16, diagonal, picked)
+    diagonal = jnp.sum(jnp.where(row == col, gram, 0.0), axis=0, keepdims=True)
+    blank = jnp.zeros((lanes - count - 8, total), jnp.float32)
+    extra = jnp.concatenate([picked, jnp.broadcast_to(diagonal, (8, total)), blank], axis=0).T
     h = total // 2
     row_h = lax.broadcasted_iota(jnp.int32, (h, h), 0)
     col_h = lax.broadcasted_iota(jnp.int32, (h, h), 1)
@@ -184,19 +193,16 @@
     col_all = lax.broadcasted_iota(jnp.int32, (total, total), 1)
     weights = weights_ref[...]
     levels = groups.bit_length() - 1
-    for level in range(levels):
+    for level in range(levels - 1):
         span = 2 * snaps << level
         if level:
             weights = rotated(weights, rotate_ref.at[:, (level - 1) * total : level * total])
         left = split3(weights)
         same = (row_all // span == col_all // span).astype(jnp.float32).astype(BF16)
-        if span < total:
-            inside = same[:h, :h]
-            begin = mm3(tuple(part[:, :h] for part in left), tuple(part * inside for part in first))
-            end = mm3(tuple(part[:, h:] for part in left), tuple(part * inside for part in last))
-            moved = jnp.concatenate([begin, end], axis=1)
-        else:
-            moved = moved_by(left)
+        inside = same[:h, :h]
+        begin = mm3(tuple(part[:, :h] for part in left), tuple(part * inside for part in first))
+        end = mm3(tuple(part[:, h:] for part in left), tuple(part * inside for part in last))
+        moved = jnp.concatenate([begin, end], axis=1)
         own = jnp.sum(weights * moved, axis=0, keepdims=True)
         products = [weights[j : j + 1] * moved for j in range(rank)]
         products = jnp.concatenate(products + [jnp.broadcast_to(own, (rank, total))], axis=0)
@@ -210,15 +216,25 @@
         for j in range(1, rank):
             turned = turned + sums[j * rank : (j + 1) * rank] * weights[j : j + 1]
         weights = 1.5 * weights - 0.5 * turned / scale
-    norm_sq = jnp.sum(weights * moved_by(split3(weights)), axis=1, keepdims=True)
+
+    weights = rotated(weights, rotate_ref.at[:, (levels - 2) * total :])
+    left = split3(weights)
+    small = mm3(split3(moved_by(left)), left, True)
+    identity = lax.broadcasted_iota(jnp.int32, small.shape, 0) == lax.broadcasted_iota(jnp.int32, small.shape, 1)
+    scale = (jnp.sum(jnp.where(identity, small, 0.0), keepdims=True) + 1e-06) / rank
+    factor = jnp.where(identity, 1.5, 0.0) - 0.5 * small / scale
+    turned = factor.T
+    parts = split3(turned)
+    weights = mm3(parts, left)
+    norm_sq = jnp.sum(turned * mm3(parts, split3(small)), axis=1, keepdims=True)
     norm_sq = jnp.maximum(norm_sq, 0.0)
     value = jnp.sum(weights * picked, axis=1, keepdims=True)
     floor_value = 0.5 * jnp.sqrt(norm_sq / cells_all + 1e-06)
-    weights = weights * (value / jnp.maximum(jnp.abs(value), floor_value))
-    rows_y = out_ref.shape[2]
+    sign = value / jnp.maximum(jnp.abs(value), floor_value)
+    fields = out_ref.shape[0] // rank
     modes = mm3(split3(weights), tuple(parts_ref[i * total : (i + 1) * total] for i in range(3)))
-    for f in range(3 * rows_y):
-        out_ref[:, f // rows_y, f % rows_y, :] = modes[:, f * lanes : (f + 1) * lanes]
+    for f in range(fields):
+        out_ref[pl.ds(f, rank, stride=fields), :] = modes[:, f * lanes : (f + 1) * lanes] * sign
 
 
 def call(kernel, shapes, specs, *args, name, scratch=()):
@@ -284,7 +300,7 @@
     x_of = ref_cell % plane // cells_z
     here = (row_of >= 0) & (row_of < rows_y) & (x_of == snap_index)
     position = jnp.where(here, (comp_of * rows_y + row_of) * cells_z + ref_cell % cells_z, -1)
-    position = jnp.pad(position, (0, cells_z - rank), constant_values=-1)[:, None]
+    position = position[:, None]
     ids = lax.dynamic_index_in_dim(block_id, snap_index, 1, keepdims=False)
     half = 0.5 * sum(
         jnp.where(ids[:, None] == b, metric[b][None, :, None], 0.0) for b in range(metric.shape[0])
@@ -295,21 +311,27 @@
 
     own, children, position, half, leaf_tile = lax.optimization_barrier((own, children, position, half, leaf_tile))
     inner = own[:, snaps : 5 * snaps]
-    below = lax.ppermute(own[:, 4 * snaps :], "space", [(i, i + 1) for i in range(slabs - 1)])
-    above = lax.ppermute(own[:, : 2 * snaps], "space", [(i + 1, i) for i in range(slabs - 1)])
+    is_even = space_index % 2 == 0
+    first, last = own[:, : 2 * snaps], own[:, 4 * snaps :]
+    swaps = [(i, i ^ 1) for i in range(slabs)]
+    chip = lax.ppermute(jnp.where(is_even, last, first), "space", swaps)
+    swaps = [(i, i - 1 if i % 2 == 0 else i + 1) for i in range(1, slabs - 1)]
+    beyond = lax.ppermute(jnp.where(is_even, first, last), "space", swaps)
+    even = jnp.full((8, cells_z), is_even, jnp.float32)
     left = lax.ppermute(inner, SNAP, [(i, (i + 1) % groups) for i in range(groups)])
     right = lax.ppermute(inner, SNAP, [((i + 1) % groups, i) for i in range(groups)])
     field_parts, table = call(
         gram_kernel,
         (jax.ShapeDtypeStruct((3 * total, fields * cells_z), BF16), f32(groups, 2 * snaps, cells_z)),
-        [VMEM] * 8,
+        [VMEM] * 9,
         half,
         position,
         own,
         left,
         right,
-        below,
-        above,
+        chip,
+        beyond,
+        even,
         leaf_tile,
         name="gram",
     )
@@ -327,9 +349,9 @@
         children,
         name="start",
     )
-    return call(
+    modes = call(
         functools.partial(tree_kernel, fields * plane * slabs),
-        f32(rank, 3, rows_y, cells_z),
+        f32(rank * fields, cells_z),
         [VMEM] * 4,
         table,
         weights,
@@ -337,6 +359,7 @@
         field_parts,
         name="tree",
     )
+    return modes.reshape(rank, 3, rows_y, cells_z)
 
 
 def solution(mesh):

time: 87.7 us -> 85.3 us (0.973)
  starting transfers between devices: 28.7 us -> 26.9 us
  blocking collectives: 27.8 us -> 26.8 us
  waiting for transfers between devices: 19.5 us -> 20.4 us
    ppermute x2, starting transfers between devices: 7.47 us -> 5.64 us  [the longest x1 5.55 us: local(): beyond = lax.ppermute(jnp.where(is_even, first, last), 'space', swaps)]
    all_to_all x2, blocking collectives: 27.8 us -> 26.8 us  [exchange(): return lax.all_to_all(value, axis, 0, 0, tiled=True)]
where the time goes in v4:
time: 85.3 us; the launch traced here: 84.9 us
  starting transfers between devices  26.9 us (32%)
  blocking collectives  26.8 us (31%)
  waiting for transfers between devices  20.4 us (24%)
  Pallas kernels  8.34 us (10%)
  local copies, waits for them, and re-layouts  1.12 us (1%)
  other arithmetic  1.05 us (1%)
    all_to_all x2, blocking collectives, exchange(): return lax.all_to_all(value, axis, 0, 0, tiled=True)  26.8 us
    all_to_all x2, waiting for transfers between devices, exchange(): return lax.all_to_all(value, axis, 0, 0, tiled=True)  17.7 us
    all_to_all x2, starting transfers between devices, exchange(): return lax.all_to_all(value, axis, 0, 0, tiled=True)  17.5 us
    pallas_call x5, Pallas kernels, call(): pl.pallas_call(kernel, out_shape=shapes, in_specs=specs, out_specs=outs,...  6.5 us
    ppermute x1, starting transfers between devices, local(): beyond = lax.ppermute(jnp.where(is_even, first, last), 'space', swaps)  5.55 us
    ppermute x1, starting transfers between devices, local(): lax.ppermute(inner, SNAP, [((i + 1) % groups, i) for i in range(groups)])  3.7 us
    ppermute x1, waiting for transfers between devices, local(): beyond = lax.ppermute(jnp.where(is_even, first, last), 'space', swaps)  2.45 us
    pallas_call x1, Pallas kernels, local(): pl.pallas_call(pack_kernel, out_shape=jax.ShapeDtypeStruct((cells_x, per_...  1.85 us
  transfers between devices with their start and end apart: 6, of which 4 were waited for; matrix products, arithmetic and copies ran while one was open for 2% of the time, Pallas kernels for 1%

profile of v4, /device:TPU:1, one launch (start us, length us, event | category | flops | bytes accessed | tf_op | source)
XLA Modules:
  0.0 84.9 jit_solution(3126977344447413251)
XLA Ops:
  0.0 0.0 copy-start.4
  0.0 0.0 copy-start.1
  0.0 0.0 copy-start.2
  0.0 0.0 copy-start
  0.0 1.8 %pack.1 = bf16[32,48,128]{2,1,0:T(8,128)(2,1)} custom-call(bf16[8,3,2,32,128]{4,3,2,1,0:T(8,128)(2,1)} %vel_hbm.1), custom_call_target="tpu_custom_call" | custom-call | tf_op jit(solution)/shard_map/pack/pallas_call | solution.py:280
  1.9 12.0 %all-to-all-start = ((bf16[32,48,128]{2,1,0:T(8,128)(2,1)}), bf16[32,48,128]{2,1,0:T(8,128)(2,1)S(1)}, u32[]{:S(2)}, u32[]{:S(2)}) async-start(bf16[32,48,128]{2,1,0:T(8,128)(2,1)} %pack.1), calls=%async_computation | async-start | bytes 786432 | tf_op jit(solution)/shard_map/all_to_all | solution.py:258
  13.9 0.0 copy-done.4
  14.0 0.0 copy-done.1
  14.0 0.3 slice_reduce_fusion.7
  14.3 0.7 broadcast_compare_fusion.7
  15.0 0.0 copy-done.2
  15.0 0.1 tile.12
  15.1 0.0 copy-done
  15.1 0.1 fusion.5
  15.2 0.0 copy-start.3
  15.2 0.2 maximum_select_fusion
  15.4 0.2 copy.10
  15.6 0.2 reshape.20
  15.9 0.0 copy-done.3
  16.0 0.1 add_multiply_fusion.half_ref
  16.1 9.5 %all-to-all-done.own_ref = bf16[32,48,128]{2,1,0:T(8,128)(2,1)S(1)} async-done(((bf16[32,48,128]{2,1,0:T(8,128)(2,1)}), bf16[32,48,128]{2,1,0:T(8,128)(2,1)S(1)}, u32[]{:S(2)}, u32[]{:S(2)}) %all-to-all-start) | async-done | bytes 393248 | tf_op jit(solution)/shard_map/all_to_all | solution.py:258
  25.7 3.7 %collective-permute-start.1 = (bf16[32,32,128]{2,1,0:T(8,128)(2,1)S(1)}, bf16[32,32,128]{2,1,0:T(8,128)(2,1)S(1)}, u32[]{:S(2)}, u32[]{:S(2)}) collective-permute-start(bf16[32,32,128]{2,1,0:T(8,128)(2,1)S(1)} %slice.51), channel_id=1, source_target_pairs={{1,0},{2,1},{3,2},{4,3},{5,4},{6,5},{7,6},{8,7},{9,8},{10,9},{11,1... | collective-permute-start | bytes 786440 | tf_op jit(solution)/shard_map/ppermute | solution.py:322
  29.4 0.0 collective-permute-start
  29.4 5.5 %collective-permute-start.3 = (bf16[32,16,128]{2,1,0:T(8,128)(2,1)S(1)}, bf16[32,16,128]{2,1,0:T(8,128)(2,1)S(1)}, u32[]{:S(2)}, u32[]{:S(2)}) collective-permute-start(bf16[32,16,128]{2,1,0:T(8,128)(2,1)S(1)} %get-tuple-element.37), channel_id=1, source_target_pairs={{32,64},{64,32},{96,128},{128,96},{160,192},{192,160},{33,65},{65,... | collective-permute-start | bytes 393224 | tf_op jit(solution)/shard_map/ppermute | solution.py:319
  34.9 0.1 collective-permute-start.2
  35.1 0.1 copy.11.ref_pos_ref
  35.1 2.4 %collective-permute-done.3.next_ref = bf16[32,16,128]{2,1,0:T(8,128)(2,1)S(1)} collective-permute-done((bf16[32,16,128]{2,1,0:T(8,128)(2,1)S(1)}, bf16[32,16,128]{2,1,0:T(8,128)(2,1)S(1)}, u32[]{:S(2)}, u32[]{:S(2)}) %collective-permute-start.3) | collective-permute-done | bytes 131104 | tf_op jit(solution)/shard_map/ppermute | solution.py:319
  37.6 0.0 collective-permute-done.2.chip_ref
  37.6 0.0 collective-permute-done.1.right_ref
  37.6 0.3 collective-permute-done.left_ref
  37.9 1.3 %gram.1 = (bf16[768,768]{1,0:T(8,128)(2,1)S(1)}, f32[32,16,128]{2,1,0:T(8,128)S(1)}) custom-call(f32[2,3,128]{2,1,0:T(4,128)S(1)} %add_multiply_fusion.half_ref, s32[16,1]{1,0:T(8,128)S(1)} %copy.11.ref_pos_ref, bf16[32,48,128]{2,1,0:T(8,128)(2,1)S(1)} %all-to-all-done.own_ref, bf16[32,32,128]{2,1,0:T(8,128)(2,1)S(1)} %collective-permute-done.left_ref, ...), custom_call_target="tpu_custom_call" | custom-call | tf_op jit(solution)/shard_map/gram/pallas_call | solution.py:242
  39.2 16.7 %all_to_all.20.parts_ref = f32[32,16,128]{2,1,0:T(8,128)S(1)} all-to-all(f32[32,16,128]{2,1,0:T(8,128)S(1)} %get-tuple-element.20), channel_id=1, replica_groups=mesh['space'=8,'y'=4,'z'=8] {'space','y'}, dimensions={0} | all-to-all | bytes 524288 | tf_op jit(solution)/shard_map/all_to_all | solution.py:258
  56.0 10.1 %all_to_all.21.parts_ref = f32[8,16,128]{2,1,0:T(8,128)S(1)} all-to-all(f32[8,16,128]{2,1,0:T(8,128)S(1)} %sum_wide.1), channel_id=1, replica_groups=mesh['space'=8,'y'=4,'z'=8] {'z'}, dimensions={0} | all-to-all | bytes 131072 | tf_op jit(solution)/shard_map/all_to_all | solution.py:258
  66.1 0.7 sum_z.1
  66.8 5.5 %all-to-all-start.3 = ((f32[32,16,128]{2,1,0:T(8,128)}), f32[32,16,128]{2,1,0:T(8,128)S(1)}, u32[]{:S(2)}, u32[]{:S(2)}) async-start(f32[32,16,128]{2,1,0:T(8,128)} %sum_z.1), calls=%async_computation.3 | async-start | bytes 524288 | tf_op jit(solution)/shard_map/all_to_all | solution.py:258
  72.3 0.7 start.1
  73.0 8.2 %all-to-all-done.3.table_ref = f32[32,16,128]{2,1,0:T(8,128)S(1)} async-done(((f32[32,16,128]{2,1,0:T(8,128)}), f32[32,16,128]{2,1,0:T(8,128)S(1)}, u32[]{:S(2)}, u32[]{:S(2)}) %all-to-all-start.3) | async-done | bytes 262176 | tf_op jit(solution)/shard_map/all_to_all | solution.py:258
  81.2 3.7 %tree.1 = f32[96,128]{1,0:T(8,128)} custom-call(f32[32,16,128]{2,1,0:T(8,128)S(1)} %all-to-all-done.3.table_ref, f32[16,256]{1,0:T(8,128)S(1)} %get-tuple-element.24.weights_ref, f32[256,1024]{1,0:T(8,128)S(1)} %get-tuple-element.25.rotate_ref, bf16[768,768]{1,0:T(8,128)(2,1)S(1)} %get-tuple-element.26.parts_ref), custom_call_target="tpu_custom_call" | custom-call | tf_op jit(solution)/shard_map/tree/pallas_call | solution.py:242
  (15 shorter events, 0.2 us)
Async XLA Ops:
  0.0 13.9 %copy-start.4 = (s32[31]{0:T(128)S(1)}, s32[31]{0:T(128)}, u32[]{:S(2)}) copy-start(s32[31]{0:T(128)} %param.12) | copy-start | bytes 376
  0.0 14.0 %copy-start.1 = (f32[8,3]{0,1:T(4,128)S(1)}, f32[8,3]{0,1:T(4,128)}, u32[]{:S(2)}) copy-start(f32[8,3]{0,1:T(4,128)} %param.9) | copy-start | bytes 292
  0.0 15.0 %copy-start.2 = (f32[1,8,16]{2,1,0:T(8,128)S(1)}, f32[1,8,16]{2,1,0:T(8,128)}, u32[]{:S(2)}) copy-start(f32[1,8,16]{2,1,0:T(8,128)} %param.10) | copy-start | bytes 1540
  0.0 15.1 %copy-start = (f32[31,32,16]{1,2,0:T(8,128)S(1)}, f32[31,32,16]{1,2,0:T(8,128)}, u32[]{:S(2)}) copy-start(f32[31,32,16]{1,2,0:T(8,128)} %param.11) | copy-start | bytes 190468
  1.9 23.8 %all-to-all-start = ((bf16[32,48,128]{2,1,0:T(8,128)(2,1)}), bf16[32,48,128]{2,1,0:T(8,128)(2,1)S(1)}, u32[]{:S(2)}, u32[]{:S(2)}) async-start(bf16[32,48,128]{2,1,0:T(8,128)(2,1)} %pack.1), calls=%async_computation | async-start | bytes 786432 | tf_op jit(solution)/shard_map/all_to_all | solution.py:258
  15.2 0.7 copy-start.3
  25.7 11.9 %collective-permute-start.1 = (bf16[32,32,128]{2,1,0:T(8,128)(2,1)S(1)}, bf16[32,32,128]{2,1,0:T(8,128)(2,1)S(1)}, u32[]{:S(2)}, u32[]{:S(2)}) collective-permute-start(bf16[32,32,128]{2,1,0:T(8,128)(2,1)S(1)} %slice.51), channel_id=1, source_target_pairs={{1,0},{2,1},{3,2},{4,3},{5,4},{6,5},{7,6},{8,7},{9,8},{10,9},{11,1... | collective-permute-start | bytes 786440 | tf_op jit(solution)/shard_map/ppermute | solution.py:322
  29.4 8.5 %collective-permute-start = (bf16[32,32,128]{2,1,0:T(8,128)(2,1)S(1)}, bf16[32,32,128]{2,1,0:T(8,128)(2,1)S(1)}, u32[]{:S(2)}, u32[]{:S(2)}) collective-permute-start(bf16[32,32,128]{2,1,0:T(8,128)(2,1)S(1)} %slice.51), channel_id=1, source_target_pairs={{0,1},{1,2},{2,3},{3,4},{4,5},{5,6},{6,7},{7,8},{8,9},{9,10},{10,1... | collective-permute-start | bytes 786440 | tf_op jit(solution)/shard_map/ppermute | solution.py:321
  29.4 8.2 %collective-permute-start.3 = (bf16[32,16,128]{2,1,0:T(8,128)(2,1)S(1)}, bf16[32,16,128]{2,1,0:T(8,128)(2,1)S(1)}, u32[]{:S(2)}, u32[]{:S(2)}) collective-permute-start(bf16[32,16,128]{2,1,0:T(8,128)(2,1)S(1)} %get-tuple-element.37), channel_id=1, source_target_pairs={{32,64},{64,32},{96,128},{128,96},{160,192},{192,160},{33,65},{65,... | collective-permute-start | bytes 393224 | tf_op jit(solution)/shard_map/ppermute | solution.py:319
  34.9 2.6 %collective-permute-start.2 = (bf16[32,16,128]{2,1,0:T(8,128)(2,1)S(1)}, bf16[32,16,128]{2,1,0:T(8,128)(2,1)S(1)}, u32[]{:S(2)}, u32[]{:S(2)}) collective-permute-start(bf16[32,16,128]{2,1,0:T(8,128)(2,1)S(1)} %get-tuple-element.38), channel_id=1, source_target_pairs={{0,32},{32,0},{64,96},{96,64},{128,160},{160,128},{192,224},{224,1... | collective-permute-start | bytes 393224 | tf_op jit(solution)/shard_map/ppermute | solution.py:317
  66.8 14.4 %all-to-all-start.3 = ((f32[32,16,128]{2,1,0:T(8,128)}), f32[32,16,128]{2,1,0:T(8,128)S(1)}, u32[]{:S(2)}, u32[]{:S(2)}) async-start(f32[32,16,128]{2,1,0:T(8,128)} %sum_z.1), calls=%async_computation.3 | async-start | bytes 524288 | tf_op jit(solution)/shard_map/all_to_all | solution.py:258

commit v5 on v4

--- a/solution.py
+++ b/solution.py
@@ -60,8 +60,8 @@
 
 
 def gram_kernel(
-    half_ref, ref_pos_ref, own_ref, left_ref, right_ref, chip_ref, next_ref, even_ref, leaf_ref,
-    parts_ref, out_ref
+    half_ref, ref_pos_ref, own_ref, left_ref, right_ref, chip_ref, next_ref, even_ref, side_ref,
+    parts_ref, out_ref, table_ref
 ):
     groups, per_x, lanes = own_ref.shape
     rows_y = half_ref.shape[0]
@@ -111,33 +111,72 @@
     picked = picked_low + picked_middle + picked_high
     gram = low + middle[total:] + high[2 * total :]
     gram = gram + (middle[:total] + high[total : 2 * total]) + high[:total]
-    row = lax.broadcasted_iota(jnp.int32, gram.shape, 0)
-    col = lax.broadcasted_iota(jnp.int32, gram.shape, 1)
-    diagonal = jnp.sum(jnp.where(row == col, gram, 0.0), axis=0, keepdims=True)
-    blank = jnp.zeros((lanes - count - 8, total), jnp.float32)
-    extra = jnp.concatenate([picked, jnp.broadcast_to(diagonal, (8, total)), blank], axis=0).T
     h = total // 2
-    row_h = lax.broadcasted_iota(jnp.int32, (h, h), 0)
-    col_h = lax.broadcasted_iota(jnp.int32, (h, h), 1)
-    mixed = jnp.where(row_h <= col_h, gram[:h, :h], gram[h:, h:])
-    out_ref[: groups // 2, :8] = mixed.reshape(groups // 2, snaps, h)
-    out_ref[groups // 2 :, :8] = gram[:h, h:].reshape(groups // 2, snaps, h)
-    out_ref[:, 8:] = extra.reshape(groups, snaps, h) + leaf_ref[...][None]
-
-
-def sum_spread_kernel(parts_ref, out_ref):
-    total = jnp.sum(parts_ref[...], axis=0)
-    for i in range(out_ref.shape[0]):
-        out_ref[i] = total
+    row = lax.broadcasted_iota(jnp.int32, (h, h), 0)
+    col = lax.broadcasted_iota(jnp.int32, (h, h), 1)
+    last = gram[h:, h:]
+    diagonal = jnp.sum(jnp.where(row == col, last, 0.0), axis=0, keepdims=True)
+    table_ref[:h] = jnp.where(row <= col, gram[:h, :h], last)
+    table_ref[h:] = gram[:h, h:]
+    chunk = snaps + 2
+    for r in range(snaps):
+        out_ref[pl.ds(r, groups, stride=chunk), :] = table_ref[pl.ds(r, groups, stride=snaps), :]
+    out_ref[pl.ds(snaps, groups, stride=chunk), :] = jnp.concatenate([picked[:, :h], picked[:, h:]], axis=0)
+    side = side_ref[:groups] + jnp.where(side_ref[groups:] > 0, diagonal, 0.0)
+    out_ref[pl.ds(snaps + 1, groups, stride=chunk), :] = side
+
+
+def sum_wide_kernel(parts_ref, origin_ref, out_ref, fold_ref):
+    copies, rows, lanes = out_ref.shape
+    sources = 32
+    chunk = parts_ref.shape[0] // sources
+    block = 4 * chunk
+    total = parts_ref[:block]
+    for i in range(1, sources // 4):
+        total = total + parts_ref[i * block : (i + 1) * block]
+    fold_ref[...] = total
+    total = sum(fold_ref[i * chunk : (i + 1) * chunk] for i in range(4))
+    side = parts_ref[pl.ds(chunk - 1, sources, stride=chunk), :]
+    origin = origin_ref[:1] > 0
+    leaves = jnp.where(origin, side[4:8], side[:4])
+    row = lax.broadcasted_iota(jnp.int32, side.shape, 0)
+    second = (row >= 4) & (row < 8)
+    diagonal = jnp.where(second, 0.0, side), jnp.where(second, side, 0.0)
+    diagonal = [jnp.sum(value, axis=0, keepdims=True) for value in diagonal]
+    out_ref[0, : chunk - 1] = total[: chunk - 1]
+    out_ref[0, chunk - 1 : chunk] = jnp.where(origin, diagonal[0], diagonal[1])
+    out_ref[0, chunk : chunk + 4] = leaves
+    out_ref[0, chunk + 4 :] = jnp.zeros((rows - chunk - 4, lanes), jnp.float32)
+    whole = out_ref[0]
+    for i in range(1, copies):
+        out_ref[i] = whole
+
+
+def sum_z_kernel(parts_ref, out_ref, fold_ref):
+    block = fold_ref.shape[0]
+    chunk = block // 4
+    total = jnp.sum(parts_ref[...], axis=0)[:chunk]
+    for i in range(4):
+        fold_ref[i * chunk : (i + 1) * chunk] = total
+    whole = fold_ref[...]
+    for i in range(out_ref.shape[0] // block):
+        out_ref[i * block : (i + 1) * block] = whole
 
 
 def start_kernel(parts_ref, children_ref, weights_ref, rotate_ref):
-    snaps = parts_ref.shape[1] // 2
     rank, total = weights_ref.shape
+    lanes = parts_ref.shape[2]
+    snaps = lanes // rank
     levels = rotate_ref.shape[1] // total + 1
-    misc = parts_ref[:, snaps:].reshape(-1, parts_ref.shape[2]).T
-    count = total // misc.shape[1]
-    leaves = jnp.concatenate([misc[(2 + i) * rank : (3 + i) * rank] for i in range(count)], axis=1)
+    leaves = jnp.concatenate([parts_ref[:, snaps + 2 + i] for i in range(4)], axis=0)
+    groups = leaves.shape[0]
+    own_group = lax.broadcasted_iota(jnp.int32, (groups, total), 0)
+    own_group = own_group == lax.broadcasted_iota(jnp.int32, (groups, total), 1) // snaps
+    wide = dot(jnp.concatenate(split3(leaves.T), axis=0), own_group.astype(jnp.float32).astype(BF16))
+    wide = wide[:lanes] + wide[lanes : 2 * lanes] + wide[2 * lanes :]
+    row = lax.broadcasted_iota(jnp.int32, wide.shape, 0)
+    col = lax.broadcasted_iota(jnp.int32, wide.shape, 1)
+    leaves = jnp.sum(jnp.where(row % snaps == col % snaps, wide, 0.0).reshape(rank, snaps, total), axis=1)
     tables = jnp.concatenate(split3(children_ref[...].T), axis=0)
     width = tables.shape[1]
     child = lax.broadcasted_iota(jnp.int32, (width, total), 0)
@@ -163,22 +202,25 @@
     return total
 
 
-def tree_kernel(cells_all, table_ref, weights_ref, rotate_ref, parts_ref, out_ref):
-    groups, rows_all, lanes = table_ref.shape
-    snaps = rows_all // 2
-    rank = weights_ref.shape[0]
-    total = groups * snaps
+def tree_kernel(cells_all, table_ref, weights_ref, rotate_ref, parts_ref, out_ref, packed_ref):
+    rank, total = weights_ref.shape
+    lanes = table_ref.shape[1]
     h = total // 2
-    packed = table_ref[:, :snaps].reshape(total, lanes)
-    extra = table_ref[:, snaps:].reshape(total, lanes)
-    picked = extra.T[:rank]
-    mixed = packed[:h]
-    cross = packed[h:]
+    snaps = lanes // rank
+    groups = total // snaps
+    chunk = snaps + 2
+    for r in range(snaps):
+        packed_ref[pl.ds(r, groups, stride=snaps), :] = table_ref[pl.ds(r, groups, stride=chunk), :]
+    picked = table_ref[pl.ds(snaps, groups, stride=chunk), :]
+    picked = jnp.concatenate([picked[:rank], picked[rank:]], axis=1)
+    last_diag = table_ref[chunk - 1 : chunk] + table_ref[2 * chunk - 1 : 2 * chunk]
+    mixed = packed_ref[:h]
+    cross = packed_ref[h:]
     mixed_t = mixed.T
     row = lax.broadcasted_iota(jnp.int32, (h, h), 0)
     col = lax.broadcasted_iota(jnp.int32, (h, h), 1)
     first = jnp.where(row <= col, mixed, mixed_t)
-    last = jnp.where(row > col, mixed, jnp.where(row == col, extra[h:, rank : rank + 1], mixed_t))
+    last = jnp.where(row > col, mixed, jnp.where(row == col, last_diag, mixed_t))
     first = split3(first)
     last = split3(last)
     cross = split3(cross)
@@ -219,14 +261,14 @@
 
     weights = rotated(weights, rotate_ref.at[:, (levels - 2) * total :])
     left = split3(weights)
-    small = mm3(split3(moved_by(left)), left, True)
+    small = mm3(left, split3(moved_by(left)), True)
+    small_parts = split3(small)
+    turned = mm3(small_parts, left)
     identity = lax.broadcasted_iota(jnp.int32, small.shape, 0) == lax.broadcasted_iota(jnp.int32, small.shape, 1)
     scale = (jnp.sum(jnp.where(identity, small, 0.0), keepdims=True) + 1e-06) / rank
+    weights = 1.5 * weights - 0.5 * turned / scale
     factor = jnp.where(identity, 1.5, 0.0) - 0.5 * small / scale
-    turned = factor.T
-    parts = split3(turned)
-    weights = mm3(parts, left)
-    norm_sq = jnp.sum(turned * mm3(parts, split3(small)), axis=1, keepdims=True)
+    norm_sq = jnp.sum(factor * mm3(split3(factor), small_parts), axis=1, keepdims=True)
     norm_sq = jnp.maximum(norm_sq, 0.0)
     value = jnp.sum(weights * picked, axis=1, keepdims=True)
     floor_value = 0.5 * jnp.sqrt(norm_sq / cells_all + 1e-06)
@@ -305,11 +347,17 @@
     half = 0.5 * sum(
         jnp.where(ids[:, None] == b, metric[b][None, :, None], 0.0) for b in range(metric.shape[0])
     )
-    slot = jnp.arange(cells_z, dtype=jnp.int32) // rank - 2
-    leaf_here = (slot == lax.axis_index("y")) & (space_index == 0)
-    leaf_tile = jnp.where(leaf_here, jnp.tile(leaf_rot[0], (1, cells_z // rank)), 0.0)
-
-    own, children, position, half, leaf_tile = lax.optimization_barrier((own, children, position, half, leaf_tile))
+    at = jnp.arange(groups, dtype=jnp.int32)[:, None]
+    origin = (space_index == 0) & (lax.axis_index("y") == 0)
+    leaf_here = ((space_index == 0) & (at != 0)) | ((space_index == 1) & (at == 0))
+    diagonal_here = ((space_index != 1) & (at == 0)) | ((space_index == 1) & (at == 1))
+    leaf = leaf_rot[0].T.reshape(1, cells_z)
+    marks = jnp.broadcast_to(diagonal_here.astype(jnp.float32), (groups, cells_z))
+    side = jnp.concatenate([jnp.where(leaf_here, leaf, 0.0), marks], axis=0)
+    origin = jnp.full((8, cells_z), origin, jnp.float32)
+    own, children, position, half, side, origin = lax.optimization_barrier(
+        (own, children, position, half, side, origin)
+    )
     inner = own[:, snaps : 5 * snaps]
     is_even = space_index % 2 == 0
     first, last = own[:, : 2 * snaps], own[:, 4 * snaps :]
@@ -320,9 +368,10 @@
     even = jnp.full((8, cells_z), is_even, jnp.float32)
     left = lax.ppermute(inner, SNAP, [(i, (i + 1) % groups) for i in range(groups)])
     right = lax.ppermute(inner, SNAP, [((i + 1) % groups, i) for i in range(groups)])
+    chunk = snaps + 2
     field_parts, table = call(
         gram_kernel,
-        (jax.ShapeDtypeStruct((3 * total, fields * cells_z), BF16), f32(groups, 2 * snaps, cells_z)),
+        (jax.ShapeDtypeStruct((3 * total, fields * cells_z), BF16), f32(groups * chunk, cells_z)),
         [VMEM] * 9,
         half,
         position,
@@ -332,14 +381,20 @@
         chip,
         beyond,
         even,
-        leaf_tile,
+        side,
         name="gram",
-    )
-    table = exchange(table, WIDE)
-    table = call(sum_spread_kernel, f32(lax.axis_size("z"), 2 * snaps, cells_z), [VMEM], table, name="sum_wide")
+        scratch=[pltpu.VMEM((total, cells_z), jnp.float32)],
+    )
+    fold = [pltpu.VMEM((4 * chunk, cells_z), jnp.float32)]
+    pieces = (groups, chunk // 2, 2, cells_z)
+    table = exchange(table.reshape(pieces), WIDE).reshape(-1, cells_z)
+    depth = lax.axis_size("z")
+    table = call(
+        sum_wide_kernel, f32(depth, 2 * snaps, cells_z), [VMEM] * 2, table, origin, name="sum_wide", scratch=fold
+    )
     parts, children = lax.optimization_barrier((exchange(table, "z"), children))
-    table = call(sum_spread_kernel, f32(groups, 2 * snaps, cells_z), [VMEM], parts, name="sum_z")
-    table = exchange(table, WIDE)
+    table = call(sum_z_kernel, f32(groups * chunk, cells_z), [VMEM], parts, name="sum_z", scratch=fold)
+    table = exchange(table.reshape(pieces), WIDE).reshape(-1, cells_z)
     levels = groups.bit_length() - 1
     weights, rotate = call(
         start_kernel,
@@ -358,6 +413,7 @@
         rotate,
         field_parts,
         name="tree",
+        scratch=[pltpu.VMEM((total, cells_z), jnp.float32)],
     )
     return modes.reshape(rank, 3, rows_y, cells_z)
 

time: 85.3 us -> 83 us (0.973)
  waiting for transfers between devices: 20.4 us -> 19.2 us
  blocking collectives: 26.8 us -> 25.9 us
    all_to_all x2, waiting for transfers between devices: 17.7 us -> 16.4 us  [exchange(): return lax.all_to_all(value, axis, 0, 0, tiled=True)]
    all_to_all x2, blocking collectives: 26.8 us -> 25.9 us  [exchange(): return lax.all_to_all(value, axis, 0, 0, tiled=True)]
  transfers between devices with their start and end apart: 6 -> 6, of which waited for: 4 -> 4; matrix products, arithmetic and copies ran while one was open for 2% -> 3% of each run, Pallas kernels for 1% -> 1%
where the time goes in v5:
time: 83 us; the launch traced here: 82.6 us
  starting transfers between devices  26.8 us (32%)
  blocking collectives  25.9 us (31%)
  waiting for transfers between devices  19.2 us (23%)
  Pallas kernels  8.08 us (10%)
  local copies, waits for them, and re-layouts  1.27 us (2%)
  other arithmetic  1.18 us (1%)
    all_to_all x2, blocking collectives, exchange(): return lax.all_to_all(value, axis, 0, 0, tiled=True)  25.9 us
    all_to_all x2, starting transfers between devices, exchange(): return lax.all_to_all(value, axis, 0, 0, tiled=True)  17.4 us
    all_to_all x2, waiting for transfers between devices, exchange(): return lax.all_to_all(value, axis, 0, 0, tiled=True)  16.4 us
    pallas_call x5, Pallas kernels, call(): pl.pallas_call(kernel, out_shape=shapes, in_specs=specs, out_specs=outs,...  6.25 us
    ppermute x1, starting transfers between devices, local(): beyond = lax.ppermute(jnp.where(is_even, first, last), 'space', swaps)  5.55 us
    ppermute x1, starting transfers between devices, local(): lax.ppermute(inner, SNAP, [((i + 1) % groups, i) for i in range(groups)])  3.7 us
    ppermute x1, waiting for transfers between devices, local(): beyond = lax.ppermute(jnp.where(is_even, first, last), 'space', swaps)  2.45 us
    pallas_call x1, Pallas kernels, local(): pl.pallas_call(pack_kernel, out_shape=jax.ShapeDtypeStruct((cells_x, per_...  1.83 us
  transfers between devices with their start and end apart: 6, of which 4 were waited for; matrix products, arithmetic and copies ran while one was open for 3% of the time, Pallas kernels for 1%

profile of v5, /device:TPU:1, one launch (start us, length us, event | category | flops | bytes accessed | tf_op | source)
XLA Modules:
  0.0 82.6 jit_solution(16224793578353985973)
XLA Ops:
  0.0 0.0 copy-start.4
  0.0 0.0 copy-start.2
  0.0 0.0 copy-start
  0.0 1.8 %pack.1 = bf16[32,48,128]{2,1,0:T(8,128)(2,1)} custom-call(bf16[8,3,2,32,128]{4,3,2,1,0:T(8,128)(2,1)} %vel_hbm.1), custom_call_target="tpu_custom_call" | custom-call | tf_op jit(solution)/shard_map/pack/pallas_call | solution.py:322
  1.8 12.0 %all-to-all-start = ((bf16[32,48,128]{2,1,0:T(8,128)(2,1)}), bf16[32,48,128]{2,1,0:T(8,128)(2,1)S(1)}, u32[]{:S(2)}, u32[]{:S(2)}) async-start(bf16[32,48,128]{2,1,0:T(8,128)(2,1)} %pack.1), calls=%async_computation | async-start | bytes 786432 | tf_op jit(solution)/shard_map/all_to_all | solution.py:300
  13.9 0.0 copy-done.4
  13.9 0.7 broadcast_compare_fusion.7
  14.7 0.0 copy-done.2
  14.7 0.1 copy.12
  14.8 0.1 broadcast_in_dim.221
  14.8 0.0 copy-done
  14.9 0.1 fusion.4
  15.0 0.0 copy-start.3
  15.0 0.0 copy-start.1
  15.0 0.2 maximum_select_fusion
  15.2 0.2 copy.11
  15.4 0.2 reshape.58
  15.7 0.1 pad.6.clone
  15.7 0.0 copy-done.3
  15.8 0.0 copy-done.1
  15.9 0.3 slice_reduce_fusion.7
  16.1 0.1 add_multiply_fusion.half_ref
  16.2 0.1 broadcast_select_fusion.2
  16.3 0.1 pad_maximum_fusion.side_ref
  16.4 9.2 %all-to-all-done.own_ref = bf16[32,48,128]{2,1,0:T(8,128)(2,1)S(1)} async-done(((bf16[32,48,128]{2,1,0:T(8,128)(2,1)}), bf16[32,48,128]{2,1,0:T(8,128)(2,1)S(1)}, u32[]{:S(2)}, u32[]{:S(2)}) %all-to-all-start) | async-done | bytes 393248 | tf_op jit(solution)/shard_map/all_to_all | solution.py:300
  25.6 3.7 %collective-permute-start.1 = (bf16[32,32,128]{2,1,0:T(8,128)(2,1)S(1)}, bf16[32,32,128]{2,1,0:T(8,128)(2,1)S(1)}, u32[]{:S(2)}, u32[]{:S(2)}) collective-permute-start(bf16[32,32,128]{2,1,0:T(8,128)(2,1)S(1)} %slice.51), channel_id=1, source_target_pairs={{1,0},{2,1},{3,2},{4,3},{5,4},{6,5},{7,6},{8,7},{9,8},{10,9},{11,1... | collective-permute-start | bytes 786440 | tf_op jit(solution)/shard_map/ppermute | solution.py:370
  29.3 0.0 collective-permute-start
  29.4 5.5 %collective-permute-start.3 = (bf16[32,16,128]{2,1,0:T(8,128)(2,1)S(1)}, bf16[32,16,128]{2,1,0:T(8,128)(2,1)S(1)}, u32[]{:S(2)}, u32[]{:S(2)}) collective-permute-start(bf16[32,16,128]{2,1,0:T(8,128)(2,1)S(1)} %get-tuple-element.39), channel_id=1, source_target_pairs={{32,64},{64,32},{96,128},{128,96},{160,192},{192,160},{33,65},{65,... | collective-permute-start | bytes 393224 | tf_op jit(solution)/shard_map/ppermute | solution.py:367
  34.9 0.1 collective-permute-start.2
  35.0 0.1 copy.13.ref_pos_ref
  35.1 2.4 %collective-permute-done.3.next_ref = bf16[32,16,128]{2,1,0:T(8,128)(2,1)S(1)} collective-permute-done((bf16[32,16,128]{2,1,0:T(8,128)(2,1)S(1)}, bf16[32,16,128]{2,1,0:T(8,128)(2,1)S(1)}, u32[]{:S(2)}, u32[]{:S(2)}) %collective-permute-start.3) | collective-permute-done | bytes 131104 | tf_op jit(solution)/shard_map/ppermute | solution.py:367
  37.6 0.0 collective-permute-done.2.chip_ref
  37.6 0.0 collective-permute-done.1.right_ref
  37.6 0.3 collective-permute-done.left_ref
  37.9 1.2 %gram.1 = (bf16[768,768]{1,0:T(8,128)(2,1)S(1)}, f32[320,128]{1,0:T(8,128)S(1)}) custom-call(f32[2,3,128]{2,1,0:T(4,128)S(1)} %add_multiply_fusion.half_ref, s32[16,1]{1,0:T(8,128)S(1)} %copy.13.ref_pos_ref, bf16[32,48,128]{2,1,0:T(8,128)(2,1)S(1)} %all-to-all-done.own_ref, bf16[32,32,128]{2,1,0:T(8,128)(2,1)S(1)} %collective-permute-done.left_ref, ...), custom_call_target="tpu_custom_call" | custom-call | tf_op jit(solution)/shard_map/gram/pallas_call | solution.py:284
  39.1 15.8 %all_to_all.20 = f32[32,5,2,128]{3,2,1,0:T(2,128)S(1)} all-to-all(f32[32,5,2,128]{3,2,1,0:T(2,128)S(1)} %bitcast.28), channel_id=1, replica_groups=mesh['space'=8,'y'=4,'z'=8] {'space','y'}, dimensions={0} | all-to-all | bytes 327680 | tf_op jit(solution)/shard_map/all_to_all | solution.py:300
  55.0 10.1 %all_to_all.21.parts_ref = f32[8,16,128]{2,1,0:T(8,128)S(1)} all-to-all(f32[8,16,128]{2,1,0:T(8,128)S(1)} %sum_wide.1), channel_id=1, replica_groups=mesh['space'=8,'y'=4,'z'=8] {'z'}, dimensions={0} | all-to-all | bytes 131072 | tf_op jit(solution)/shard_map/all_to_all | solution.py:300
  65.1 0.7 sum_z.1
  65.7 5.4 %all-to-all-start.3 = ((f32[32,5,2,128]{3,2,1,0:T(2,128)}), f32[32,5,2,128]{3,2,1,0:T(2,128)S(1)}, u32[]{:S(2)}, u32[]{:S(2)}) async-start(f32[32,5,2,128]{3,2,1,0:T(2,128)} %bitcast.5), calls=%async_computation.3 | async-start | bytes 327680 | tf_op jit(solution)/shard_map/all_to_all | solution.py:300
  71.1 0.8 start.1
  71.9 7.2 %all-to-all-done.3 = f32[32,5,2,128]{3,2,1,0:T(2,128)S(1)} async-done(((f32[32,5,2,128]{3,2,1,0:T(2,128)}), f32[32,5,2,128]{3,2,1,0:T(2,128)S(1)}, u32[]{:S(2)}, u32[]{:S(2)}) %all-to-all-start.3) | async-done | bytes 163872 | tf_op jit(solution)/shard_map/all_to_all | solution.py:300
  79.1 3.5 %tree.1 = f32[96,128]{1,0:T(8,128)} custom-call(f32[320,128]{1,0:T(8,128)S(1)} %bitcast.26, f32[16,256]{1,0:T(8,128)S(1)} %get-tuple-element.26.weights_ref, f32[256,1024]{1,0:T(8,128)S(1)} %get-tuple-element.27.rotate_ref, bf16[768,768]{1,0:T(8,128)(2,1)S(1)} %get-tuple-element.28.parts_ref), custom_call_target="tpu_custom_call" | custom-call | tf_op jit(solution)/shard_map/tree/pallas_call | solution.py:284
  (14 shorter events, 0.2 us)
Async XLA Ops:
  0.0 13.9 %copy-start.4 = (s32[31]{0:T(128)S(1)}, s32[31]{0:T(128)}, u32[]{:S(2)}) copy-start(s32[31]{0:T(128)} %param.12) | copy-start | bytes 376
  0.0 14.7 %copy-start.2 = (f32[1,8,16]{2,1,0:T(8,128)S(1)}, f32[1,8,16]{2,1,0:T(8,128)}, u32[]{:S(2)}) copy-start(f32[1,8,16]{2,1,0:T(8,128)} %param.10) | copy-start | bytes 1540
  0.0 14.8 %copy-start = (f32[31,32,16]{1,2,0:T(8,128)S(1)}, f32[31,32,16]{1,2,0:T(8,128)}, u32[]{:S(2)}) copy-start(f32[31,32,16]{1,2,0:T(8,128)} %param.11) | copy-start | bytes 190468
  1.8 23.8 %all-to-all-start = ((bf16[32,48,128]{2,1,0:T(8,128)(2,1)}), bf16[32,48,128]{2,1,0:T(8,128)(2,1)S(1)}, u32[]{:S(2)}, u32[]{:S(2)}) async-start(bf16[32,48,128]{2,1,0:T(8,128)(2,1)} %pack.1), calls=%async_computation | async-start | bytes 786432 | tf_op jit(solution)/shard_map/all_to_all | solution.py:300
  15.0 0.8 copy-start.3
  15.0 0.8 %copy-start.1 = (f32[8,3]{0,1:T(4,128)S(1)}, f32[8,3]{0,1:T(4,128)}, u32[]{:S(2)}) copy-start(f32[8,3]{0,1:T(4,128)} %param.9) | copy-start | bytes 292
  25.6 11.9 %collective-permute-start.1 = (bf16[32,32,128]{2,1,0:T(8,128)(2,1)S(1)}, bf16[32,32,128]{2,1,0:T(8,128)(2,1)S(1)}, u32[]{:S(2)}, u32[]{:S(2)}) collective-permute-start(bf16[32,32,128]{2,1,0:T(8,128)(2,1)S(1)} %slice.51), channel_id=1, source_target_pairs={{1,0},{2,1},{3,2},{4,3},{5,4},{6,5},{7,6},{8,7},{9,8},{10,9},{11,1... | collective-permute-start | bytes 786440 | tf_op jit(solution)/shard_map/ppermute | solution.py:370
  29.3 8.5 %collective-permute-start = (bf16[32,32,128]{2,1,0:T(8,128)(2,1)S(1)}, bf16[32,32,128]{2,1,0:T(8,128)(2,1)S(1)}, u32[]{:S(2)}, u32[]{:S(2)}) collective-permute-start(bf16[32,32,128]{2,1,0:T(8,128)(2,1)S(1)} %slice.51), channel_id=1, source_target_pairs={{0,1},{1,2},{2,3},{3,4},{4,5},{5,6},{6,7},{7,8},{8,9},{9,10},{10,1... | collective-permute-start | bytes 786440 | tf_op jit(solution)/shard_map/ppermute | solution.py:369
  29.4 8.2 %collective-permute-start.3 = (bf16[32,16,128]{2,1,0:T(8,128)(2,1)S(1)}, bf16[32,16,128]{2,1,0:T(8,128)(2,1)S(1)}, u32[]{:S(2)}, u32[]{:S(2)}) collective-permute-start(bf16[32,16,128]{2,1,0:T(8,128)(2,1)S(1)} %get-tuple-element.39), channel_id=1, source_target_pairs={{32,64},{64,32},{96,128},{128,96},{160,192},{192,160},{33,65},{65,... | collective-permute-start | bytes 393224 | tf_op jit(solution)/shard_map/ppermute | solution.py:367
  34.9 2.6 %collective-permute-start.2 = (bf16[32,16,128]{2,1,0:T(8,128)(2,1)S(1)}, bf16[32,16,128]{2,1,0:T(8,128)(2,1)S(1)}, u32[]{:S(2)}, u32[]{:S(2)}) collective-permute-start(bf16[32,16,128]{2,1,0:T(8,128)(2,1)S(1)} %get-tuple-element.40), channel_id=1, source_target_pairs={{0,32},{32,0},{64,96},{96,64},{128,160},{160,128},{192,224},{224,1... | collective-permute-start | bytes 393224 | tf_op jit(solution)/shard_map/ppermute | solution.py:365
  65.7 13.4 %all-to-all-start.3 = ((f32[32,5,2,128]{3,2,1,0:T(2,128)}), f32[32,5,2,128]{3,2,1,0:T(2,128)S(1)}, u32[]{:S(2)}, u32[]{:S(2)}) async-start(f32[32,5,2,128]{3,2,1,0:T(2,128)} %bitcast.5), calls=%async_computation.3 | async-start | bytes 327680 | tf_op jit(solution)/shard_map/all_to_all | solution.py:300

commit v6 on v5

--- a/solution.py
+++ b/solution.py
@@ -163,12 +163,30 @@
         out_ref[i * block : (i + 1) * block] = whole
 
 
-def start_kernel(parts_ref, children_ref, weights_ref, rotate_ref):
-    rank, total = weights_ref.shape
-    lanes = parts_ref.shape[2]
+def tables_kernel(children_ref, rest_hbm, rest_ref, sems):
+    count, size, total = rest_hbm.shape
+    tables = jnp.concatenate(split3(children_ref[...].T), axis=0)
+    width = tables.shape[1]
+    child = lax.broadcasted_iota(jnp.int32, (width, total), 0)
+    snap = lax.broadcasted_iota(jnp.int32, (width, total), 1)
+    span = total >> count
+    first = 2 * (total // span)
+    copies = []
+    for level in range(count):
+        chosen = (child == first + snap // span).astype(jnp.float32).astype(BF16)
+        first, span = first + total // span, span * 2
+        spread = dot(tables, chosen)
+        rest_ref[level] = spread[:size] + spread[size : 2 * size] + spread[2 * size :]
+        copies.append(pltpu.make_async_copy(rest_ref.at[level], rest_hbm.at[level], sems.at[level]))
+        copies[-1].start()
+    for copy in copies:
+        copy.wait()
+
+
+def leaf_weights(pieces_ref, rank, total):
+    lanes = pieces_ref.shape[2]
     snaps = lanes // rank
-    levels = rotate_ref.shape[1] // total + 1
-    leaves = jnp.concatenate([parts_ref[:, snaps + 2 + i] for i in range(4)], axis=0)
+    leaves = jnp.concatenate([pieces_ref[:, snaps + 2 + i] for i in range(4)], axis=0)
     groups = leaves.shape[0]
     own_group = lax.broadcasted_iota(jnp.int32, (groups, total), 0)
     own_group = own_group == lax.broadcasted_iota(jnp.int32, (groups, total), 1) // snaps
@@ -176,22 +194,7 @@
     wide = wide[:lanes] + wide[lanes : 2 * lanes] + wide[2 * lanes :]
     row = lax.broadcasted_iota(jnp.int32, wide.shape, 0)
     col = lax.broadcasted_iota(jnp.int32, wide.shape, 1)
-    leaves = jnp.sum(jnp.where(row % snaps == col % snaps, wide, 0.0).reshape(rank, snaps, total), axis=1)
-    tables = jnp.concatenate(split3(children_ref[...].T), axis=0)
-    width = tables.shape[1]
-    child = lax.broadcasted_iota(jnp.int32, (width, total), 0)
-    snap = lax.broadcasted_iota(jnp.int32, (width, total), 1)
-    first, span = 0, snaps
-    for level in range(levels):
-        chosen = (child == first + snap // span).astype(jnp.float32).astype(BF16)
-        first, span = first + total // span, span * 2
-        spread = dot(tables, chosen)
-        size = spread.shape[0] // 3
-        spread = spread[:size] + spread[size : 2 * size] + spread[2 * size :]
-        if level:
-            rotate_ref[:, (level - 1) * total : level * total] = spread
-        else:
-            weights_ref[...] = rotated(leaves, spread)
+    return jnp.sum(jnp.where(row % snaps == col % snaps, wide, 0.0).reshape(rank, snaps, total), axis=1)
 
 
 def rotated(weights, rotate_ref):
@@ -202,9 +205,12 @@
     return total
 
 
-def tree_kernel(cells_all, table_ref, weights_ref, rotate_ref, parts_ref, out_ref, packed_ref):
-    rank, total = weights_ref.shape
+def tree_kernel(
+    cells_all, table_ref, pieces_ref, rest_ref, parts_ref, out_ref, packed_ref
+):
+    total = rest_ref.shape[2]
     lanes = table_ref.shape[1]
+    rank = out_ref.shape[0] * lanes // parts_ref.shape[1]
     h = total // 2
     snaps = lanes // rank
     groups = total // snaps
@@ -233,12 +239,12 @@
 
     row_all = lax.broadcasted_iota(jnp.int32, (total, total), 0)
     col_all = lax.broadcasted_iota(jnp.int32, (total, total), 1)
-    weights = weights_ref[...]
+    weights = leaf_weights(pieces_ref, rank, total)
     levels = groups.bit_length() - 1
     for level in range(levels - 1):
         span = 2 * snaps << level
         if level:
-            weights = rotated(weights, rotate_ref.at[:, (level - 1) * total : level * total])
+            weights = rotated(weights, rest_ref.at[level - 1])
         left = split3(weights)
         same = (row_all // span == col_all // span).astype(jnp.float32).astype(BF16)
         inside = same[:h, :h]
@@ -259,7 +265,7 @@
             turned = turned + sums[j * rank : (j + 1) * rank] * weights[j : j + 1]
         weights = 1.5 * weights - 0.5 * turned / scale
 
-    weights = rotated(weights, rotate_ref.at[:, (levels - 2) * total :])
+    weights = rotated(weights, rest_ref.at[levels - 2])
     left = split3(weights)
     small = mm3(left, split3(moved_by(left)), True)
     small_parts = split3(small)
@@ -335,7 +341,19 @@
     )(velocity)
     own = exchange(packed, SNAP)
 
+    levels = groups.bit_length() - 1
+    rest_shape = (levels - 1, rank * rank, total)
     children = child_maps(merge_rot, merge_order)
+    rest = pl.pallas_call(
+        tables_kernel,
+        out_shape=f32(*rest_shape),
+        in_specs=[VMEM],
+        out_specs=pl.BlockSpec(memory_space=pltpu.HBM),
+        scratch_shapes=[pltpu.VMEM(rest_shape, jnp.float32), pltpu.SemaphoreType.DMA((levels - 1,))],
+        name="tables",
+    )(children)
+    own_map = lax.dynamic_index_in_dim(children, snap_index, 0, keepdims=False).reshape(rank, rank)
+    leaf = jnp.sum(own_map[:, :, None] * leaf_rot[0].T[:, None, :], axis=0).reshape(1, cells_z)
     rows_total = rows_y * slabs
     comp_of = ref_cell // (rows_total * plane)
     row_of = ref_cell // plane % rows_total - space_index * rows_y
@@ -351,20 +369,17 @@
     origin = (space_index == 0) & (lax.axis_index("y") == 0)
     leaf_here = ((space_index == 0) & (at != 0)) | ((space_index == 1) & (at == 0))
     diagonal_here = ((space_index != 1) & (at == 0)) | ((space_index == 1) & (at == 1))
-    leaf = leaf_rot[0].T.reshape(1, cells_z)
     marks = jnp.broadcast_to(diagonal_here.astype(jnp.float32), (groups, cells_z))
     side = jnp.concatenate([jnp.where(leaf_here, leaf, 0.0), marks], axis=0)
     origin = jnp.full((8, cells_z), origin, jnp.float32)
-    own, children, position, half, side, origin = lax.optimization_barrier(
-        (own, children, position, half, side, origin)
-    )
+    own, rest, position, half, side, origin = lax.optimization_barrier((own, rest, position, half, side, origin))
     inner = own[:, snaps : 5 * snaps]
     is_even = space_index % 2 == 0
-    first, last = own[:, : 2 * snaps], own[:, 4 * snaps :]
+    low, high = own[:, : 2 * snaps], own[:, 4 * snaps :]
     swaps = [(i, i ^ 1) for i in range(slabs)]
-    chip = lax.ppermute(jnp.where(is_even, last, first), "space", swaps)
+    chip = lax.ppermute(jnp.where(is_even, high, low), "space", swaps)
     swaps = [(i, i - 1 if i % 2 == 0 else i + 1) for i in range(1, slabs - 1)]
-    beyond = lax.ppermute(jnp.where(is_even, first, last), "space", swaps)
+    beyond = lax.ppermute(jnp.where(is_even, low, high), "space", swaps)
     even = jnp.full((8, cells_z), is_even, jnp.float32)
     left = lax.ppermute(inner, SNAP, [(i, (i + 1) % groups) for i in range(groups)])
     right = lax.ppermute(inner, SNAP, [((i + 1) % groups, i) for i in range(groups)])
@@ -392,25 +407,16 @@
     table = call(
         sum_wide_kernel, f32(depth, 2 * snaps, cells_z), [VMEM] * 2, table, origin, name="sum_wide", scratch=fold
     )
-    parts, children = lax.optimization_barrier((exchange(table, "z"), children))
+    parts = exchange(table, "z")
     table = call(sum_z_kernel, f32(groups * chunk, cells_z), [VMEM], parts, name="sum_z", scratch=fold)
     table = exchange(table.reshape(pieces), WIDE).reshape(-1, cells_z)
-    levels = groups.bit_length() - 1
-    weights, rotate = call(
-        start_kernel,
-        (f32(rank, total), f32(rank * rank, (levels - 1) * total)),
-        [VMEM, VMEM],
-        parts,
-        children,
-        name="start",
-    )
     modes = call(
         functools.partial(tree_kernel, fields * plane * slabs),
         f32(rank * fields, cells_z),
         [VMEM] * 4,
         table,
-        weights,
-        rotate,
+        parts,
+        rest,
         field_parts,
         name="tree",
         scratch=[pltpu.VMEM((total, cells_z), jnp.float32)],

time: 83 us -> 82.3 us (level)
  blocking collectives: 25.9 us -> 39 us
  waiting for transfers between devices: 19.2 us -> 8.69 us
  starting transfers between devices: 26.8 us -> 21.4 us
  Pallas kernels: 8.08 us -> 9.28 us
  local copies, waits for them, and re-layouts: 1.27 us -> 2.1 us
    all_to_all x2 -> x3, blocking collectives: 25.9 us -> 39 us  [exchange(): return lax.all_to_all(value, axis, 0, 0, tiled=True)]
    all_to_all x2 -> x1, waiting for transfers between devices: 16.4 us -> 5.93 us  [exchange(): return lax.all_to_all(value, axis, 0, 0, tiled=True)]
    all_to_all x2 -> x1, starting transfers between devices: 17.4 us -> 12 us  [exchange(): return lax.all_to_all(value, axis, 0, 0, tiled=True)]
    pallas_call x0 -> x1, Pallas kernels: none -> 2.37 us  [local(): pl.pallas_call(tables_kernel, out_shape=f32(*rest_shape), in_specs=[VMEM]...]
    pallas_call x5 -> x4, Pallas kernels: 6.25 us -> 5.08 us  [call(): pl.pallas_call(kernel, out_shape=shapes, in_specs=specs, out_specs=outs,...]
  transfers between devices with their start and end apart: 6 -> 5, of which waited for: 4 -> 3; matrix products, arithmetic and copies ran while one was open for 3% -> 4% of each run, Pallas kernels for 1% -> 3%
where the time goes in v6:
time: 82.3 us; the launch traced here: 82 us
  blocking collectives  39 us (47%)
  starting transfers between devices  21.4 us (26%)
  Pallas kernels  9.28 us (11%)
  waiting for transfers between devices  8.69 us (11%)
  local copies, waits for them, and re-layouts  2.1 us (3%)
  other arithmetic  1.28 us (2%)
    all_to_all x3, blocking collectives, exchange(): return lax.all_to_all(value, axis, 0, 0, tiled=True)  39 us
    all_to_all x1, starting transfers between devices, exchange(): return lax.all_to_all(value, axis, 0, 0, tiled=True)  12 us
    all_to_all x1, waiting for transfers between devices, exchange(): return lax.all_to_all(value, axis, 0, 0, tiled=True)  5.93 us
    ppermute x1, starting transfers between devices, local(): beyond = lax.ppermute(jnp.where(is_even, low, high), 'space', swaps)  5.55 us
    pallas_call x4, Pallas kernels, call(): pl.pallas_call(kernel, out_shape=shapes, in_specs=specs, out_specs=outs,...  5.08 us
    ppermute x1, starting transfers between devices, local(): lax.ppermute(inner, SNAP, [((i + 1) % groups, i) for i in range(groups)])  3.7 us
    ppermute x1, waiting for transfers between devices, local(): beyond = lax.ppermute(jnp.where(is_even, low, high), 'space', swaps)  2.45 us
    pallas_call x1, Pallas kernels, local(): pl.pallas_call(tables_kernel, out_shape=f32(*rest_shape), in_specs=[VMEM]...  2.37 us
  transfers between devices with their start and end apart: 5, of which 3 were waited for; matrix products, arithmetic and copies ran while one was open for 4% of the time, Pallas kernels for 3%

profile of v6, /device:TPU:1, one launch (start us, length us, event | category | flops | bytes accessed | tf_op | source)
XLA Modules:
  0.0 82.0 jit_solution(973744537972297480)
XLA Ops:
  0.0 0.0 copy-start.5
  0.0 0.0 copy-start.3
  0.0 0.0 copy-start.1
  0.0 1.8 %pack.1 = bf16[32,48,128]{2,1,0:T(8,128)(2,1)} custom-call(bf16[8,3,2,32,128]{4,3,2,1,0:T(8,128)(2,1)} %vel_hbm.1), custom_call_target="tpu_custom_call" | custom-call | tf_op jit(solution)/shard_map/pack/pallas_call | solution.py:328
  1.8 12.0 %all-to-all-start = ((bf16[32,48,128]{2,1,0:T(8,128)(2,1)}), bf16[32,48,128]{2,1,0:T(8,128)(2,1)S(1)}, u32[]{:S(2)}, u32[]{:S(2)}) async-start(bf16[32,48,128]{2,1,0:T(8,128)(2,1)} %pack.1), calls=%async_computation | async-start | bytes 786432 | tf_op jit(solution)/shard_map/all_to_all | solution.py:306
  13.9 0.0 copy-done.5
  13.9 0.7 broadcast_compare_fusion.7
  14.7 0.0 copy-done.3
  14.7 0.1 copy.15
  14.8 0.0 copy-done.1
  14.8 0.1 fusion.5
  14.9 0.2 maximum_select_fusion
  15.1 0.2 copy.14
  15.3 0.0 copy-start.4
  15.3 0.0 copy-start.2
  15.3 0.2 reshape.61
  15.6 0.1 mul.39
  15.7 0.1 multiply_reduce_fusion
  15.8 0.1 copy.16
  15.8 0.1 broadcast_in_dim.222
  15.9 0.7 pad.4.children_ref
  16.6 2.4 %tables.1.rest_ref = f32[4,256,256]{2,1,0:T(8,128)} custom-call(f32[128,256]{1,0:T(8,128)} %pad.4.children_ref), custom_call_target="tpu_custom_call" | custom-call | tf_op jit(solution)/shard_map/tables/pallas_call | solution.py:347
  19.0 0.1 pad.6.clone
  19.1 0.0 copy-done.4
  19.1 0.0 copy-done.2
  19.2 0.3 slice_reduce_fusion.7
  19.4 0.1 add_multiply_fusion.half_ref
  19.5 0.1 broadcast_select_fusion.2
  19.6 0.1 pad_maximum_fusion.side_ref
  19.7 5.9 %all-to-all-done.own_ref = bf16[32,48,128]{2,1,0:T(8,128)(2,1)S(1)} async-done(((bf16[32,48,128]{2,1,0:T(8,128)(2,1)}), bf16[32,48,128]{2,1,0:T(8,128)(2,1)S(1)}, u32[]{:S(2)}, u32[]{:S(2)}) %all-to-all-start) | async-done | bytes 393248 | tf_op jit(solution)/shard_map/all_to_all | solution.py:306
  25.6 3.7 %collective-permute-start.1 = (bf16[32,32,128]{2,1,0:T(8,128)(2,1)S(1)}, bf16[32,32,128]{2,1,0:T(8,128)(2,1)S(1)}, u32[]{:S(2)}, u32[]{:S(2)}) collective-permute-start(bf16[32,32,128]{2,1,0:T(8,128)(2,1)S(1)} %slice.51), channel_id=1, source_target_pairs={{1,0},{2,1},{3,2},{4,3},{5,4},{6,5},{7,6},{8,7},{9,8},{10,9},{11,1... | collective-permute-start | bytes 786440 | tf_op jit(solution)/shard_map/ppermute | solution.py:385
  29.3 0.0 collective-permute-start
  29.4 5.5 %collective-permute-start.3 = (bf16[32,16,128]{2,1,0:T(8,128)(2,1)S(1)}, bf16[32,16,128]{2,1,0:T(8,128)(2,1)S(1)}, u32[]{:S(2)}, u32[]{:S(2)}) collective-permute-start(bf16[32,16,128]{2,1,0:T(8,128)(2,1)S(1)} %get-tuple-element.31), channel_id=1, source_target_pairs={{32,64},{64,32},{96,128},{128,96},{160,192},{192,160},{33,65},{65,... | collective-permute-start | bytes 393224 | tf_op jit(solution)/shard_map/ppermute | solution.py:382
  34.9 0.1 collective-permute-start.2
  35.0 0.1 copy.17.ref_pos_ref
  35.1 2.4 %collective-permute-done.3.next_ref = bf16[32,16,128]{2,1,0:T(8,128)(2,1)S(1)} collective-permute-done((bf16[32,16,128]{2,1,0:T(8,128)(2,1)S(1)}, bf16[32,16,128]{2,1,0:T(8,128)(2,1)S(1)}, u32[]{:S(2)}, u32[]{:S(2)}) %collective-permute-start.3) | collective-permute-done | bytes 131104 | tf_op jit(solution)/shard_map/ppermute | solution.py:382
  37.6 0.0 collective-permute-done.2.chip_ref
  37.6 0.0 collective-permute-done.1.right_ref
  37.6 0.3 collective-permute-done.left_ref
  37.9 0.0 copy-start
  37.9 1.2 %gram.1 = (bf16[768,768]{1,0:T(8,128)(2,1)S(1)}, f32[320,128]{1,0:T(8,128)S(1)}) custom-call(f32[2,3,128]{2,1,0:T(4,128)S(1)} %add_multiply_fusion.half_ref, s32[16,1]{1,0:T(8,128)S(1)} %copy.17.ref_pos_ref, bf16[32,48,128]{2,1,0:T(8,128)(2,1)S(1)} %all-to-all-done.own_ref, bf16[32,32,128]{2,1,0:T(8,128)(2,1)S(1)} %collective-permute-done.left_ref, ...), custom_call_target="tpu_custom_call" | custom-call | tf_op jit(solution)/shard_map/gram/pallas_call | solution.py:290
  39.1 15.8 %all_to_all.20 = f32[32,5,2,128]{3,2,1,0:T(2,128)S(1)} all-to-all(f32[32,5,2,128]{3,2,1,0:T(2,128)S(1)} %bitcast.29), channel_id=1, replica_groups=mesh['space'=8,'y'=4,'z'=8] {'space','y'}, dimensions={0} | all-to-all | bytes 327680 | tf_op jit(solution)/shard_map/all_to_all | solution.py:306
  55.0 10.1 %all_to_all.21.parts_ref.pieces_ref = f32[8,16,128]{2,1,0:T(8,128)S(1)} all-to-all(f32[8,16,128]{2,1,0:T(8,128)S(1)} %sum_wide.1), channel_id=1, replica_groups=mesh['space'=8,'y'=4,'z'=8] {'z'}, dimensions={0} | all-to-all | bytes 131072 | tf_op jit(solution)/shard_map/all_to_all | solution.py:306
  65.1 13.1 %all_to_all.22 = f32[32,5,2,128]{3,2,1,0:T(2,128)S(1)} all-to-all(f32[32,5,2,128]{3,2,1,0:T(2,128)S(1)} %bitcast.28), channel_id=1, replica_groups=mesh['space'=8,'y'=4,'z'=8] {'space','y'}, dimensions={0} | all-to-all | bytes 327680 | tf_op jit(solution)/shard_map/all_to_all | solution.py:306
  78.2 0.0 copy-done
  78.2 3.8 %tree.1 = f32[96,128]{1,0:T(8,128)} custom-call(f32[320,128]{1,0:T(8,128)S(1)} %bitcast.26, f32[8,16,128]{2,1,0:T(8,128)S(1)} %all_to_all.21.parts_ref.pieces_ref, f32[4,256,256]{2,1,0:T(8,128)S(1)} %copy-done, bf16[768,768]{1,0:T(8,128)(2,1)S(1)} %get-tuple-element.20.parts_ref), custom_call_target="tpu_custom_call" | custom-call | tf_op jit(solution)/shard_map/tree/pallas_call | solution.py:290
  (15 shorter events, 0.2 us)
Async XLA Ops:
  0.0 13.9 %copy-start.5 = (s32[31]{0:T(128)S(1)}, s32[31]{0:T(128)}, u32[]{:S(2)}) copy-start(s32[31]{0:T(128)} %param.12) | copy-start | bytes 376
  0.0 14.7 %copy-start.3 = (f32[1,8,16]{2,1,0:T(8,128)S(1)}, f32[1,8,16]{2,1,0:T(8,128)}, u32[]{:S(2)}) copy-start(f32[1,8,16]{2,1,0:T(8,128)} %param.10) | copy-start | bytes 1540
  0.0 14.8 %copy-start.1 = (f32[31,32,16]{1,2,0:T(8,128)S(1)}, f32[31,32,16]{1,2,0:T(8,128)}, u32[]{:S(2)}) copy-start(f32[31,32,16]{1,2,0:T(8,128)} %param.11) | copy-start | bytes 190468
  1.8 23.8 %all-to-all-start = ((bf16[32,48,128]{2,1,0:T(8,128)(2,1)}), bf16[32,48,128]{2,1,0:T(8,128)(2,1)S(1)}, u32[]{:S(2)}, u32[]{:S(2)}) async-start(bf16[32,48,128]{2,1,0:T(8,128)(2,1)} %pack.1), calls=%async_computation | async-start | bytes 786432 | tf_op jit(solution)/shard_map/all_to_all | solution.py:306
  15.3 3.8 %copy-start.4 = (s32[16]{0:T(128)S(1)}, s32[16]{0:T(128)}, u32[]{:S(2)}) copy-start(s32[16]{0:T(128)} %param.13) | copy-start | bytes 196
  15.3 3.8 %copy-start.2 = (f32[8,3]{0,1:T(4,128)S(1)}, f32[8,3]{0,1:T(4,128)}, u32[]{:S(2)}) copy-start(f32[8,3]{0,1:T(4,128)} %param.9) | copy-start | bytes 292
  25.6 11.9 %collective-permute-start.1 = (bf16[32,32,128]{2,1,0:T(8,128)(2,1)S(1)}, bf16[32,32,128]{2,1,0:T(8,128)(2,1)S(1)}, u32[]{:S(2)}, u32[]{:S(2)}) collective-permute-start(bf16[32,32,128]{2,1,0:T(8,128)(2,1)S(1)} %slice.51), channel_id=1, source_target_pairs={{1,0},{2,1},{3,2},{4,3},{5,4},{6,5},{7,6},{8,7},{9,8},{10,9},{11,1... | collective-permute-start | bytes 786440 | tf_op jit(solution)/shard_map/ppermute | solution.py:385
  29.3 8.5 %collective-permute-start = (bf16[32,32,128]{2,1,0:T(8,128)(2,1)S(1)}, bf16[32,32,128]{2,1,0:T(8,128)(2,1)S(1)}, u32[]{:S(2)}, u32[]{:S(2)}) collective-permute-start(bf16[32,32,128]{2,1,0:T(8,128)(2,1)S(1)} %slice.51), channel_id=1, source_target_pairs={{0,1},{1,2},{2,3},{3,4},{4,5},{5,6},{6,7},{7,8},{8,9},{9,10},{10,1... | collective-permute-start | bytes 786440 | tf_op jit(solution)/shard_map/ppermute | solution.py:384
  29.4 8.2 %collective-permute-start.3 = (bf16[32,16,128]{2,1,0:T(8,128)(2,1)S(1)}, bf16[32,16,128]{2,1,0:T(8,128)(2,1)S(1)}, u32[]{:S(2)}, u32[]{:S(2)}) collective-permute-start(bf16[32,16,128]{2,1,0:T(8,128)(2,1)S(1)} %get-tuple-element.31), channel_id=1, source_target_pairs={{32,64},{64,32},{96,128},{128,96},{160,192},{192,160},{33,65},{65,... | collective-permute-start | bytes 393224 | tf_op jit(solution)/shard_map/ppermute | solution.py:382
  34.9 2.6 %collective-permute-start.2 = (bf16[32,16,128]{2,1,0:T(8,128)(2,1)S(1)}, bf16[32,16,128]{2,1,0:T(8,128)(2,1)S(1)}, u32[]{:S(2)}, u32[]{:S(2)}) collective-permute-start(bf16[32,16,128]{2,1,0:T(8,128)(2,1)S(1)} %get-tuple-element.32), channel_id=1, source_target_pairs={{0,32},{32,0},{64,96},{96,64},{128,160},{160,128},{192,224},{224,1... | collective-permute-start | bytes 393224 | tf_op jit(solution)/shard_map/ppermute | solution.py:380
  37.9 40.3 %copy-start = (f32[4,256,256]{2,1,0:T(8,128)S(1)}, f32[4,256,256]{2,1,0:T(8,128)}, u32[]{:S(2)}) copy-start(f32[4,256,256]{2,1,0:T(8,128)} %tables.1.rest_ref) | copy-start | bytes 3145732

commit v7 on v6

--- a/solution.py
+++ b/solution.py
@@ -44,13 +44,14 @@
 def pack_kernel(vel_hbm, out_hbm, vel_ref, rows_ref, out_ref, in_sems, out_sems):
     snaps, comps, rows_y, cells_x, lanes = vel_hbm.shape
     arrivals, leaving = {}, []
-    for (c, y), slot in SLOTS.items():
-        arrivals[slot] = pltpu.make_async_copy(vel_hbm.at[:, c, y], vel_ref.at[slot], in_sems.at[slot])
-        arrivals[slot].start()
-    for slot, copy in arrivals.items():
-        copy.wait()
+    for c in range(comps):
+        arrivals[c] = pltpu.make_async_copy(vel_hbm.at[:, c], vel_ref.at[c], in_sems.at[c])
+        arrivals[c].start()
+    for (c, y), slot in sorted(SLOTS.items()):
+        if y == 0:
+            arrivals[c].wait()
         for s in range(snaps):
-            rows_ref[slot, pl.ds(s, cells_x, stride=snaps), :] = vel_ref[slot, s].astype(jnp.float32)
+            rows_ref[slot, pl.ds(s, cells_x, stride=snaps), :] = vel_ref[c, s, y].astype(jnp.float32)
         out_ref[slot] = rows_ref[slot].reshape(cells_x, snaps, lanes).astype(out_ref.dtype)
         target = out_hbm.at[:, pl.ds(slot * snaps, snaps)]
         leaving.append(pltpu.make_async_copy(out_ref.at[slot], target, out_sems.at[slot]))
@@ -259,11 +260,11 @@
         count = products.shape[0]
         sums = dot(jnp.concatenate([upper, lower], axis=0), same)
         sums = sums[count:] + sums[:count]
-        scale = (sums[rank * rank :] + 1e-06) / rank
+        share = 0.5 * rank / (sums[rank * rank :] + 1e-06)
         turned = sums[:rank] * weights[:1]
         for j in range(1, rank):
             turned = turned + sums[j * rank : (j + 1) * rank] * weights[j : j + 1]
-        weights = 1.5 * weights - 0.5 * turned / scale
+        weights = 1.5 * weights - turned * share
 
     weights = rotated(weights, rest_ref.at[levels - 2])
     left = split3(weights)
@@ -331,10 +332,10 @@
         in_specs=[pl.BlockSpec(memory_space=pl.ANY)],
         out_specs=pl.BlockSpec(memory_space=pl.ANY),
         scratch_shapes=[
-            pltpu.VMEM((fields, snaps, cells_x, cells_z), velocity.dtype),
+            pltpu.VMEM((3, snaps, rows_y, cells_x, cells_z), velocity.dtype),
             pltpu.VMEM((fields, cells_x * snaps, cells_z), jnp.float32),
             pltpu.VMEM((fields, cells_x, snaps, cells_z), velocity.dtype),
-            pltpu.SemaphoreType.DMA((fields,)),
+            pltpu.SemaphoreType.DMA((3,)),
             pltpu.SemaphoreType.DMA((fields,)),
         ],
         name="pack",

time: 82.3 us -> 82.4 us (level)
  no operation moved by 1% of the time
where the time goes in v7:
time: 82.4 us; the launch traced here: 82 us
  blocking collectives  39 us (47%)
  starting transfers between devices  21.4 us (26%)
  Pallas kernels  9.32 us (11%)
  waiting for transfers between devices  8.69 us (11%)
  local copies, waits for them, and re-layouts  2.1 us (3%)
  other arithmetic  1.28 us (2%)
    all_to_all x3, blocking collectives, exchange(): return lax.all_to_all(value, axis, 0, 0, tiled=True)  39 us
    all_to_all x1, starting transfers between devices, exchange(): return lax.all_to_all(value, axis, 0, 0, tiled=True)  12 us
    all_to_all x1, waiting for transfers between devices, exchange(): return lax.all_to_all(value, axis, 0, 0, tiled=True)  5.93 us
    ppermute x1, starting transfers between devices, local(): beyond = lax.ppermute(jnp.where(is_even, low, high), 'space', swaps)  5.55 us
    pallas_call x4, Pallas kernels, call(): pl.pallas_call(kernel, out_shape=shapes, in_specs=specs, out_specs=outs,...  5.08 us
    ppermute x1, starting transfers between devices, local(): lax.ppermute(inner, SNAP, [((i + 1) % groups, i) for i in range(groups)])  3.7 us
    ppermute x1, waiting for transfers between devices, local(): beyond = lax.ppermute(jnp.where(is_even, low, high), 'space', swaps)  2.45 us
    pallas_call x1, Pallas kernels, local(): pl.pallas_call(tables_kernel, out_shape=f32(*rest_shape), in_specs=[VMEM]...  2.38 us
  transfers between devices with their start and end apart: 5, of which 3 were waited for; matrix products, arithmetic and copies ran while one was open for 4% of the time, Pallas kernels for 3%

profile of v7, /device:TPU:1, one launch (start us, length us, event | category | flops | bytes accessed | tf_op | source)
XLA Modules:
  0.0 82.0 jit_solution(17567172056769514662)
XLA Ops:
  0.0 0.0 copy-start.5
  0.0 0.0 copy-start.3
  0.0 0.0 copy-start.1
  0.0 1.9 %pack.1 = bf16[32,48,128]{2,1,0:T(8,128)(2,1)} custom-call(bf16[8,3,2,32,128]{4,3,2,1,0:T(8,128)(2,1)} %vel_hbm.1), custom_call_target="tpu_custom_call" | custom-call | tf_op jit(solution)/shard_map/pack/pallas_call | solution.py:329
  1.9 12.0 %all-to-all-start = ((bf16[32,48,128]{2,1,0:T(8,128)(2,1)}), bf16[32,48,128]{2,1,0:T(8,128)(2,1)S(1)}, u32[]{:S(2)}, u32[]{:S(2)}) async-start(bf16[32,48,128]{2,1,0:T(8,128)(2,1)} %pack.1), calls=%async_computation | async-start | bytes 786432 | tf_op jit(solution)/shard_map/all_to_all | solution.py:307
  14.0 0.0 copy-done.5
  14.0 0.7 broadcast_compare_fusion.7
  14.7 0.0 copy-done.3
  14.7 0.1 copy.15
  14.8 0.0 copy-done.1
  14.8 0.1 fusion.5
  14.9 0.2 maximum_select_fusion
  15.1 0.2 copy.14
  15.3 0.0 copy-start.4
  15.3 0.0 copy-start.2
  15.4 0.2 reshape.61
  15.6 0.1 mul.39
  15.7 0.1 multiply_reduce_fusion
  15.8 0.1 copy.16
  15.9 0.1 broadcast_in_dim.222
  16.0 0.7 pad.4.children_ref
  16.6 2.4 %tables.1.rest_ref = f32[4,256,256]{2,1,0:T(8,128)} custom-call(f32[128,256]{1,0:T(8,128)} %pad.4.children_ref), custom_call_target="tpu_custom_call" | custom-call | tf_op jit(solution)/shard_map/tables/pallas_call | solution.py:348
  19.0 0.1 pad.6.clone
  19.1 0.0 copy-done.4
  19.2 0.0 copy-done.2
  19.2 0.3 slice_reduce_fusion.7
  19.5 0.1 add_multiply_fusion.half_ref
  19.6 0.1 broadcast_select_fusion.2
  19.6 0.1 pad_maximum_fusion.side_ref
  19.7 5.9 %all-to-all-done.own_ref = bf16[32,48,128]{2,1,0:T(8,128)(2,1)S(1)} async-done(((bf16[32,48,128]{2,1,0:T(8,128)(2,1)}), bf16[32,48,128]{2,1,0:T(8,128)(2,1)S(1)}, u32[]{:S(2)}, u32[]{:S(2)}) %all-to-all-start) | async-done | bytes 393248 | tf_op jit(solution)/shard_map/all_to_all | solution.py:307
  25.7 3.7 %collective-permute-start.1 = (bf16[32,32,128]{2,1,0:T(8,128)(2,1)S(1)}, bf16[32,32,128]{2,1,0:T(8,128)(2,1)S(1)}, u32[]{:S(2)}, u32[]{:S(2)}) collective-permute-start(bf16[32,32,128]{2,1,0:T(8,128)(2,1)S(1)} %slice.51), channel_id=1, source_target_pairs={{1,0},{2,1},{3,2},{4,3},{5,4},{6,5},{7,6},{8,7},{9,8},{10,9},{11,1... | collective-permute-start | bytes 786440 | tf_op jit(solution)/shard_map/ppermute | solution.py:386
  29.4 0.0 collective-permute-start
  29.4 5.5 %collective-permute-start.3 = (bf16[32,16,128]{2,1,0:T(8,128)(2,1)S(1)}, bf16[32,16,128]{2,1,0:T(8,128)(2,1)S(1)}, u32[]{:S(2)}, u32[]{:S(2)}) collective-permute-start(bf16[32,16,128]{2,1,0:T(8,128)(2,1)S(1)} %get-tuple-element.31), channel_id=1, source_target_pairs={{32,64},{64,32},{96,128},{128,96},{160,192},{192,160},{33,65},{65,... | collective-permute-start | bytes 393224 | tf_op jit(solution)/shard_map/ppermute | solution.py:383
  35.0 0.1 collective-permute-start.2
  35.1 0.1 copy.17.ref_pos_ref
  35.2 2.4 %collective-permute-done.3.next_ref = bf16[32,16,128]{2,1,0:T(8,128)(2,1)S(1)} collective-permute-done((bf16[32,16,128]{2,1,0:T(8,128)(2,1)S(1)}, bf16[32,16,128]{2,1,0:T(8,128)(2,1)S(1)}, u32[]{:S(2)}, u32[]{:S(2)}) %collective-permute-start.3) | collective-permute-done | bytes 131104 | tf_op jit(solution)/shard_map/ppermute | solution.py:383
  37.6 0.0 collective-permute-done.2.chip_ref
  37.6 0.0 collective-permute-done.1.right_ref
  37.6 0.3 collective-permute-done.left_ref
  37.9 0.0 copy-start
  37.9 1.2 %gram.1 = (bf16[768,768]{1,0:T(8,128)(2,1)S(1)}, f32[320,128]{1,0:T(8,128)S(1)}) custom-call(f32[2,3,128]{2,1,0:T(4,128)S(1)} %add_multiply_fusion.half_ref, s32[16,1]{1,0:T(8,128)S(1)} %copy.17.ref_pos_ref, bf16[32,48,128]{2,1,0:T(8,128)(2,1)S(1)} %all-to-all-done.own_ref, bf16[32,32,128]{2,1,0:T(8,128)(2,1)S(1)} %collective-permute-done.left_ref, ...), custom_call_target="tpu_custom_call" | custom-call | tf_op jit(solution)/shard_map/gram/pallas_call | solution.py:291
  39.2 15.8 %all_to_all.20 = f32[32,5,2,128]{3,2,1,0:T(2,128)S(1)} all-to-all(f32[32,5,2,128]{3,2,1,0:T(2,128)S(1)} %bitcast.29), channel_id=1, replica_groups=mesh['space'=8,'y'=4,'z'=8] {'space','y'}, dimensions={0} | all-to-all | bytes 327680 | tf_op jit(solution)/shard_map/all_to_all | solution.py:307
  55.0 10.1 %all_to_all.21.parts_ref.pieces_ref = f32[8,16,128]{2,1,0:T(8,128)S(1)} all-to-all(f32[8,16,128]{2,1,0:T(8,128)S(1)} %sum_wide.1), channel_id=1, replica_groups=mesh['space'=8,'y'=4,'z'=8] {'z'}, dimensions={0} | all-to-all | bytes 131072 | tf_op jit(solution)/shard_map/all_to_all | solution.py:307
  65.1 13.1 %all_to_all.22 = f32[32,5,2,128]{3,2,1,0:T(2,128)S(1)} all-to-all(f32[32,5,2,128]{3,2,1,0:T(2,128)S(1)} %bitcast.28), channel_id=1, replica_groups=mesh['space'=8,'y'=4,'z'=8] {'space','y'}, dimensions={0} | all-to-all | bytes 327680 | tf_op jit(solution)/shard_map/all_to_all | solution.py:307
  78.2 0.0 copy-done
  78.2 3.8 %tree.1 = f32[96,128]{1,0:T(8,128)} custom-call(f32[320,128]{1,0:T(8,128)S(1)} %bitcast.26, f32[8,16,128]{2,1,0:T(8,128)S(1)} %all_to_all.21.parts_ref.pieces_ref, f32[4,256,256]{2,1,0:T(8,128)S(1)} %copy-done, bf16[768,768]{1,0:T(8,128)(2,1)S(1)} %get-tuple-element.20.parts_ref), custom_call_target="tpu_custom_call" | custom-call | tf_op jit(solution)/shard_map/tree/pallas_call | solution.py:291
  (15 shorter events, 0.2 us)
Async XLA Ops:
  0.0 14.0 %copy-start.5 = (s32[31]{0:T(128)S(1)}, s32[31]{0:T(128)}, u32[]{:S(2)}) copy-start(s32[31]{0:T(128)} %param.12) | copy-start | bytes 376
  0.0 14.7 %copy-start.3 = (f32[1,8,16]{2,1,0:T(8,128)S(1)}, f32[1,8,16]{2,1,0:T(8,128)}, u32[]{:S(2)}) copy-start(f32[1,8,16]{2,1,0:T(8,128)} %param.10) | copy-start | bytes 1540
  0.0 14.8 %copy-start.1 = (f32[31,32,16]{1,2,0:T(8,128)S(1)}, f32[31,32,16]{1,2,0:T(8,128)}, u32[]{:S(2)}) copy-start(f32[31,32,16]{1,2,0:T(8,128)} %param.11) | copy-start | bytes 190468
  1.9 23.8 %all-to-all-start = ((bf16[32,48,128]{2,1,0:T(8,128)(2,1)}), bf16[32,48,128]{2,1,0:T(8,128)(2,1)S(1)}, u32[]{:S(2)}, u32[]{:S(2)}) async-start(bf16[32,48,128]{2,1,0:T(8,128)(2,1)} %pack.1), calls=%async_computation | async-start | bytes 786432 | tf_op jit(solution)/shard_map/all_to_all | solution.py:307
  15.3 3.8 %copy-start.4 = (s32[16]{0:T(128)S(1)}, s32[16]{0:T(128)}, u32[]{:S(2)}) copy-start(s32[16]{0:T(128)} %param.13) | copy-start | bytes 196
  15.3 3.8 %copy-start.2 = (f32[8,3]{0,1:T(4,128)S(1)}, f32[8,3]{0,1:T(4,128)}, u32[]{:S(2)}) copy-start(f32[8,3]{0,1:T(4,128)} %param.9) | copy-start | bytes 292
  25.7 11.9 %collective-permute-start.1 = (bf16[32,32,128]{2,1,0:T(8,128)(2,1)S(1)}, bf16[32,32,128]{2,1,0:T(8,128)(2,1)S(1)}, u32[]{:S(2)}, u32[]{:S(2)}) collective-permute-start(bf16[32,32,128]{2,1,0:T(8,128)(2,1)S(1)} %slice.51), channel_id=1, source_target_pairs={{1,0},{2,1},{3,2},{4,3},{5,4},{6,5},{7,6},{8,7},{9,8},{10,9},{11,1... | collective-permute-start | bytes 786440 | tf_op jit(solution)/shard_map/ppermute | solution.py:386
  29.4 8.5 %collective-permute-start = (bf16[32,32,128]{2,1,0:T(8,128)(2,1)S(1)}, bf16[32,32,128]{2,1,0:T(8,128)(2,1)S(1)}, u32[]{:S(2)}, u32[]{:S(2)}) collective-permute-start(bf16[32,32,128]{2,1,0:T(8,128)(2,1)S(1)} %slice.51), channel_id=1, source_target_pairs={{0,1},{1,2},{2,3},{3,4},{4,5},{5,6},{6,7},{7,8},{8,9},{9,10},{10,1... | collective-permute-start | bytes 786440 | tf_op jit(solution)/shard_map/ppermute | solution.py:385
  29.4 8.2 %collective-permute-start.3 = (bf16[32,16,128]{2,1,0:T(8,128)(2,1)S(1)}, bf16[32,16,128]{2,1,0:T(8,128)(2,1)S(1)}, u32[]{:S(2)}, u32[]{:S(2)}) collective-permute-start(bf16[32,16,128]{2,1,0:T(8,128)(2,1)S(1)} %get-tuple-element.31), channel_id=1, source_target_pairs={{32,64},{64,32},{96,128},{128,96},{160,192},{192,160},{33,65},{65,... | collective-permute-start | bytes 393224 | tf_op jit(solution)/shard_map/ppermute | solution.py:383
  35.0 2.6 %collective-permute-start.2 = (bf16[32,16,128]{2,1,0:T(8,128)(2,1)S(1)}, bf16[32,16,128]{2,1,0:T(8,128)(2,1)S(1)}, u32[]{:S(2)}, u32[]{:S(2)}) collective-permute-start(bf16[32,16,128]{2,1,0:T(8,128)(2,1)S(1)} %get-tuple-element.32), channel_id=1, source_target_pairs={{0,32},{32,0},{64,96},{96,64},{128,160},{160,128},{192,224},{224,1... | collective-permute-start | bytes 393224 | tf_op jit(solution)/shard_map/ppermute | solution.py:381
  37.9 40.3 %copy-start = (f32[4,256,256]{2,1,0:T(8,128)S(1)}, f32[4,256,256]{2,1,0:T(8,128)}, u32[]{:S(2)}) copy-start(f32[4,256,256]{2,1,0:T(8,128)} %tables.1.rest_ref) | copy-start | bytes 3145732

commit v8 on v7

--- a/solution.py
+++ b/solution.py
@@ -232,11 +232,11 @@
     last = split3(last)
     cross = split3(cross)
 
-    def moved_by(left):
-        lower = tuple(part[:, :h] for part in left)
-        upper = tuple(part[:, h:] for part in left)
-        begin = mm3(lower, first) + mm3(upper, cross, True)
-        return jnp.concatenate([begin, mm3(lower, cross) + mm3(upper, last)], axis=1)
+    cross_t = split3(packed_ref[h:].T)
+    whole = tuple(
+        jnp.concatenate([jnp.concatenate([f, c], axis=1), jnp.concatenate([t, l], axis=1)], axis=0)
+        for f, c, t, l in zip(first, cross, cross_t, last)
+    )
 
     row_all = lax.broadcasted_iota(jnp.int32, (total, total), 0)
     col_all = lax.broadcasted_iota(jnp.int32, (total, total), 1)
@@ -268,7 +268,7 @@
 
     weights = rotated(weights, rest_ref.at[levels - 2])
     left = split3(weights)
-    small = mm3(left, split3(moved_by(left)), True)
+    small = mm3(left, split3(mm3(left, whole)), True)
     small_parts = split3(small)
     turned = mm3(small_parts, left)
     identity = lax.broadcasted_iota(jnp.int32, small.shape, 0) == lax.broadcasted_iota(jnp.int32, small.shape, 1)

time: 82.4 us -> 82.3 us (level)
  no operation moved by 1% of the time
where the time goes in v8:
time: 82.3 us; the launch traced here: 81.9 us
  blocking collectives  39 us (47%)
  starting transfers between devices  21.4 us (26%)
  Pallas kernels  9.21 us (11%)
  waiting for transfers between devices  8.69 us (11%)
  local copies, waits for them, and re-layouts  2.1 us (3%)
  other arithmetic  1.28 us (2%)
    all_to_all x3, blocking collectives, exchange(): return lax.all_to_all(value, axis, 0, 0, tiled=True)  39 us
    all_to_all x1, starting transfers between devices, exchange(): return lax.all_to_all(value, axis, 0, 0, tiled=True)  12 us
    all_to_all x1, waiting for transfers between devices, exchange(): return lax.all_to_all(value, axis, 0, 0, tiled=True)  5.93 us
    ppermute x1, starting transfers between devices, local(): beyond = lax.ppermute(jnp.where(is_even, low, high), 'space', swaps)  5.55 us
    pallas_call x4, Pallas kernels, call(): pl.pallas_call(kernel, out_shape=shapes, in_specs=specs, out_specs=outs,...  4.97 us
    ppermute x1, starting transfers between devices, local(): lax.ppermute(inner, SNAP, [((i + 1) % groups, i) for i in range(groups)])  3.7 us
    ppermute x1, waiting for transfers between devices, local(): beyond = lax.ppermute(jnp.where(is_even, low, high), 'space', swaps)  2.45 us
    pallas_call x1, Pallas kernels, local(): pl.pallas_call(tables_kernel, out_shape=f32(*rest_shape), in_specs=[VMEM]...  2.38 us
  transfers between devices with their start and end apart: 5, of which 3 were waited for; matrix products, arithmetic and copies ran while one was open for 4% of the time, Pallas kernels for 3%

profile of v8, /device:TPU:1, one launch (start us, length us, event | category | flops | bytes accessed | tf_op | source)
XLA Modules:
  0.0 81.9 jit_solution(10514154275324889018)
XLA Ops:
  0.0 0.0 copy-start.5
  0.0 0.0 copy-start.3
  0.0 0.0 copy-start.1
  0.0 1.9 %pack.1 = bf16[32,48,128]{2,1,0:T(8,128)(2,1)} custom-call(bf16[8,3,2,32,128]{4,3,2,1,0:T(8,128)(2,1)} %vel_hbm.1), custom_call_target="tpu_custom_call" | custom-call | tf_op jit(solution)/shard_map/pack/pallas_call | solution.py:329
  1.9 12.0 %all-to-all-start = ((bf16[32,48,128]{2,1,0:T(8,128)(2,1)}), bf16[32,48,128]{2,1,0:T(8,128)(2,1)S(1)}, u32[]{:S(2)}, u32[]{:S(2)}) async-start(bf16[32,48,128]{2,1,0:T(8,128)(2,1)} %pack.1), calls=%async_computation | async-start | bytes 786432 | tf_op jit(solution)/shard_map/all_to_all | solution.py:307
  14.0 0.0 copy-done.5
  14.0 0.7 broadcast_compare_fusion.7
  14.7 0.0 copy-done.3
  14.7 0.1 copy.15
  14.8 0.0 copy-done.1
  14.8 0.1 fusion.5
  14.9 0.2 maximum_select_fusion
  15.1 0.2 copy.14
  15.3 0.0 copy-start.4
  15.3 0.0 copy-start.2
  15.4 0.2 reshape.61
  15.6 0.1 mul.39
  15.7 0.1 multiply_reduce_fusion
  15.8 0.1 copy.16
  15.9 0.1 broadcast_in_dim.222
  16.0 0.7 pad.4.children_ref
  16.6 2.4 %tables.1.rest_ref = f32[4,256,256]{2,1,0:T(8,128)} custom-call(f32[128,256]{1,0:T(8,128)} %pad.4.children_ref), custom_call_target="tpu_custom_call" | custom-call | tf_op jit(solution)/shard_map/tables/pallas_call | solution.py:348
  19.0 0.1 pad.6.clone
  19.1 0.0 copy-done.4
  19.2 0.0 copy-done.2
  19.2 0.3 slice_reduce_fusion.7
  19.5 0.1 add_multiply_fusion.half_ref
  19.6 0.1 broadcast_select_fusion.2
  19.6 0.1 pad_maximum_fusion.side_ref
  19.7 5.9 %all-to-all-done.own_ref = bf16[32,48,128]{2,1,0:T(8,128)(2,1)S(1)} async-done(((bf16[32,48,128]{2,1,0:T(8,128)(2,1)}), bf16[32,48,128]{2,1,0:T(8,128)(2,1)S(1)}, u32[]{:S(2)}, u32[]{:S(2)}) %all-to-all-start) | async-done | bytes 393248 | tf_op jit(solution)/shard_map/all_to_all | solution.py:307
  25.7 3.7 %collective-permute-start.1 = (bf16[32,32,128]{2,1,0:T(8,128)(2,1)S(1)}, bf16[32,32,128]{2,1,0:T(8,128)(2,1)S(1)}, u32[]{:S(2)}, u32[]{:S(2)}) collective-permute-start(bf16[32,32,128]{2,1,0:T(8,128)(2,1)S(1)} %slice.51), channel_id=1, source_target_pairs={{1,0},{2,1},{3,2},{4,3},{5,4},{6,5},{7,6},{8,7},{9,8},{10,9},{11,1... | collective-permute-start | bytes 786440 | tf_op jit(solution)/shard_map/ppermute | solution.py:386
  29.4 0.0 collective-permute-start
  29.4 5.5 %collective-permute-start.3 = (bf16[32,16,128]{2,1,0:T(8,128)(2,1)S(1)}, bf16[32,16,128]{2,1,0:T(8,128)(2,1)S(1)}, u32[]{:S(2)}, u32[]{:S(2)}) collective-permute-start(bf16[32,16,128]{2,1,0:T(8,128)(2,1)S(1)} %get-tuple-element.31), channel_id=1, source_target_pairs={{32,64},{64,32},{96,128},{128,96},{160,192},{192,160},{33,65},{65,... | collective-permute-start | bytes 393224 | tf_op jit(solution)/shard_map/ppermute | solution.py:383
  35.0 0.1 collective-permute-start.2
  35.1 0.1 copy.17.ref_pos_ref
  35.2 2.4 %collective-permute-done.3.next_ref = bf16[32,16,128]{2,1,0:T(8,128)(2,1)S(1)} collective-permute-done((bf16[32,16,128]{2,1,0:T(8,128)(2,1)S(1)}, bf16[32,16,128]{2,1,0:T(8,128)(2,1)S(1)}, u32[]{:S(2)}, u32[]{:S(2)}) %collective-permute-start.3) | collective-permute-done | bytes 131104 | tf_op jit(solution)/shard_map/ppermute | solution.py:383
  37.6 0.0 collective-permute-done.2.chip_ref
  37.6 0.0 collective-permute-done.1.right_ref
  37.6 0.3 collective-permute-done.left_ref
  37.9 0.0 copy-start
  37.9 1.2 %gram.1 = (bf16[768,768]{1,0:T(8,128)(2,1)S(1)}, f32[320,128]{1,0:T(8,128)S(1)}) custom-call(f32[2,3,128]{2,1,0:T(4,128)S(1)} %add_multiply_fusion.half_ref, s32[16,1]{1,0:T(8,128)S(1)} %copy.17.ref_pos_ref, bf16[32,48,128]{2,1,0:T(8,128)(2,1)S(1)} %all-to-all-done.own_ref, bf16[32,32,128]{2,1,0:T(8,128)(2,1)S(1)} %collective-permute-done.left_ref, ...), custom_call_target="tpu_custom_call" | custom-call | tf_op jit(solution)/shard_map/gram/pallas_call | solution.py:291
  39.2 15.8 %all_to_all.20 = f32[32,5,2,128]{3,2,1,0:T(2,128)S(1)} all-to-all(f32[32,5,2,128]{3,2,1,0:T(2,128)S(1)} %bitcast.29), channel_id=1, replica_groups=mesh['space'=8,'y'=4,'z'=8] {'space','y'}, dimensions={0} | all-to-all | bytes 327680 | tf_op jit(solution)/shard_map/all_to_all | solution.py:307
  55.0 10.1 %all_to_all.21.parts_ref.pieces_ref = f32[8,16,128]{2,1,0:T(8,128)S(1)} all-to-all(f32[8,16,128]{2,1,0:T(8,128)S(1)} %sum_wide.1), channel_id=1, replica_groups=mesh['space'=8,'y'=4,'z'=8] {'z'}, dimensions={0} | all-to-all | bytes 131072 | tf_op jit(solution)/shard_map/all_to_all | solution.py:307
  65.1 13.1 %all_to_all.22 = f32[32,5,2,128]{3,2,1,0:T(2,128)S(1)} all-to-all(f32[32,5,2,128]{3,2,1,0:T(2,128)S(1)} %bitcast.28), channel_id=1, replica_groups=mesh['space'=8,'y'=4,'z'=8] {'space','y'}, dimensions={0} | all-to-all | bytes 327680 | tf_op jit(solution)/shard_map/all_to_all | solution.py:307
  78.2 0.0 copy-done
  78.2 3.7 %tree.1 = f32[96,128]{1,0:T(8,128)} custom-call(f32[320,128]{1,0:T(8,128)S(1)} %bitcast.26, f32[8,16,128]{2,1,0:T(8,128)S(1)} %all_to_all.21.parts_ref.pieces_ref, f32[4,256,256]{2,1,0:T(8,128)S(1)} %copy-done, bf16[768,768]{1,0:T(8,128)(2,1)S(1)} %get-tuple-element.20.parts_ref), custom_call_target="tpu_custom_call" | custom-call | tf_op jit(solution)/shard_map/tree/pallas_call | solution.py:291
  (15 shorter events, 0.2 us)
Async XLA Ops:
  0.0 14.0 %copy-start.5 = (s32[31]{0:T(128)S(1)}, s32[31]{0:T(128)}, u32[]{:S(2)}) copy-start(s32[31]{0:T(128)} %param.12) | copy-start | bytes 376
  0.0 14.7 %copy-start.3 = (f32[1,8,16]{2,1,0:T(8,128)S(1)}, f32[1,8,16]{2,1,0:T(8,128)}, u32[]{:S(2)}) copy-start(f32[1,8,16]{2,1,0:T(8,128)} %param.10) | copy-start | bytes 1540
  0.0 14.8 %copy-start.1 = (f32[31,32,16]{1,2,0:T(8,128)S(1)}, f32[31,32,16]{1,2,0:T(8,128)}, u32[]{:S(2)}) copy-start(f32[31,32,16]{1,2,0:T(8,128)} %param.11) | copy-start | bytes 190468
  1.9 23.8 %all-to-all-start = ((bf16[32,48,128]{2,1,0:T(8,128)(2,1)}), bf16[32,48,128]{2,1,0:T(8,128)(2,1)S(1)}, u32[]{:S(2)}, u32[]{:S(2)}) async-start(bf16[32,48,128]{2,1,0:T(8,128)(2,1)} %pack.1), calls=%async_computation | async-start | bytes 786432 | tf_op jit(solution)/shard_map/all_to_all | solution.py:307
  15.3 3.8 %copy-start.4 = (s32[16]{0:T(128)S(1)}, s32[16]{0:T(128)}, u32[]{:S(2)}) copy-start(s32[16]{0:T(128)} %param.13) | copy-start | bytes 196
  15.3 3.8 %copy-start.2 = (f32[8,3]{0,1:T(4,128)S(1)}, f32[8,3]{0,1:T(4,128)}, u32[]{:S(2)}) copy-start(f32[8,3]{0,1:T(4,128)} %param.9) | copy-start | bytes 292
  25.7 11.9 %collective-permute-start.1 = (bf16[32,32,128]{2,1,0:T(8,128)(2,1)S(1)}, bf16[32,32,128]{2,1,0:T(8,128)(2,1)S(1)}, u32[]{:S(2)}, u32[]{:S(2)}) collective-permute-start(bf16[32,32,128]{2,1,0:T(8,128)(2,1)S(1)} %slice.51), channel_id=1, source_target_pairs={{1,0},{2,1},{3,2},{4,3},{5,4},{6,5},{7,6},{8,7},{9,8},{10,9},{11,1... | collective-permute-start | bytes 786440 | tf_op jit(solution)/shard_map/ppermute | solution.py:386
  29.4 8.5 %collective-permute-start = (bf16[32,32,128]{2,1,0:T(8,128)(2,1)S(1)}, bf16[32,32,128]{2,1,0:T(8,128)(2,1)S(1)}, u32[]{:S(2)}, u32[]{:S(2)}) collective-permute-start(bf16[32,32,128]{2,1,0:T(8,128)(2,1)S(1)} %slice.51), channel_id=1, source_target_pairs={{0,1},{1,2},{2,3},{3,4},{4,5},{5,6},{6,7},{7,8},{8,9},{9,10},{10,1... | collective-permute-start | bytes 786440 | tf_op jit(solution)/shard_map/ppermute | solution.py:385
  29.4 8.2 %collective-permute-start.3 = (bf16[32,16,128]{2,1,0:T(8,128)(2,1)S(1)}, bf16[32,16,128]{2,1,0:T(8,128)(2,1)S(1)}, u32[]{:S(2)}, u32[]{:S(2)}) collective-permute-start(bf16[32,16,128]{2,1,0:T(8,128)(2,1)S(1)} %get-tuple-element.31), channel_id=1, source_target_pairs={{32,64},{64,32},{96,128},{128,96},{160,192},{192,160},{33,65},{65,... | collective-permute-start | bytes 393224 | tf_op jit(solution)/shard_map/ppermute | solution.py:383
  35.0 2.6 %collective-permute-start.2 = (bf16[32,16,128]{2,1,0:T(8,128)(2,1)S(1)}, bf16[32,16,128]{2,1,0:T(8,128)(2,1)S(1)}, u32[]{:S(2)}, u32[]{:S(2)}) collective-permute-start(bf16[32,16,128]{2,1,0:T(8,128)(2,1)S(1)} %get-tuple-element.32), channel_id=1, source_target_pairs={{0,32},{32,0},{64,96},{96,64},{128,160},{160,128},{192,224},{224,1... | collective-permute-start | bytes 393224 | tf_op jit(solution)/shard_map/ppermute | solution.py:381
  37.9 40.3 %copy-start = (f32[4,256,256]{2,1,0:T(8,128)S(1)}, f32[4,256,256]{2,1,0:T(8,128)}, u32[]{:S(2)}) copy-start(f32[4,256,256]{2,1,0:T(8,128)} %tables.1.rest_ref) | copy-start | bytes 3145732
